TPU v7x, 256 devices: a whole 4x4x8 slice. The times are simulated.
256 devices in a mesh: dp: 16 (over z, core), fsdp: 16 (over x, y).
Axes of the slice: x: 4, y: 4, z: 8, core: 2. Of those that a mesh axis runs over, the one named last changes fastest.
Arguments:
- normed: bfloat16 [98304, 4096], P(('dp', 'fsdp')), may hold values from -24 to 24
- queries: bfloat16 [98304, 2048], P(('dp', 'fsdp')), may hold values from -48 to 48
- key_rows: bfloat16 [98304, 512], P(('dp', 'fsdp')), may hold values from -6 to 6
- out_grad: bfloat16 [98304, 2048], P(('dp', 'fsdp')), may hold values from -6 to 6
- value_weight: bfloat16 [4096, 512], P('fsdp'), may hold values from -0.09375 to 0.09375
- doc_ids: int32 [256, 384], P(('dp', 'fsdp')), may hold values from 0 to 3, never falling along the last dimension, each value on 1 to 256 neighbouring positions
- send_to: int32 [256, 8], P(('dp', 'fsdp')), may hold values from 0 to 15, as said below
- take_from: int32 [256, 8], P(('dp', 'fsdp')), may hold values from 0 to 15, as said below
Outputs:
- query_grad: bfloat16 [98304, 2048], P(('dp', 'fsdp'))
- key_grad: bfloat16 [98304, 512], P(('dp', 'fsdp'))
- input_grad: bfloat16 [98304, 4096], P(('dp', 'fsdp'))
- weight_grad: float32 [4096, 512], P(('dp', 'fsdp'))
Inputs may be any that keep to these rules, and one draw needn't show every extreme that they name: `send_to`: entry b of a device's row names the dp index of the device, with the same fsdp index, that packs this device's rows b * 48 to (b + 1) * 48 - 1; the 8 entries of a row are distinct, and every device packs exactly 8 blocks. `take_from`: entry p of a device's row names the dp index of the device whose block, sent to this device by send_to, becomes this device's packed rows p * 48 to (p + 1) * 48 - 1; the entries of a row are distinct, so one device sends at most one block to another. `doc_ids`: along a device's 384 rows document numbers never fall; a document holds at most 256 rows, and one document in every draw holds exactly that many.
All inputs are finite; a program needn't handle non-finite values.
Results may differ from a plain program's by a relative error of at most 0.006.
Values may be sent and summed in bfloat16 or wider, within the bound.
No kernel may reach another device: no remote copies, remote signals or barrier semaphores. Data moves between devices by JAX's collectives and lax.ppermute only.
A program may use at most 128 MiB of HBM per device.

v0:
```python
import jax
import jax.numpy as jnp
from jax import lax
from jax.sharding import PartitionSpec as P

HEADS = 16
KV_HEADS = 4
HEAD_DIM = 128
BLOCK_ROWS = 48


def to_slots(array, outgoing, blocks):
    shaped = array.reshape(blocks, BLOCK_ROWS, array.shape[1])
    return jnp.einsum("pb,bcw->pcw", outgoing, shaped, preferred_element_type=jnp.float32).astype(
        jnp.bfloat16
    )


def from_slots(array, incoming):
    picked = jnp.einsum("bs,scw->bcw", incoming, array, preferred_element_type=jnp.float32).astype(
        jnp.bfloat16
    )
    return picked.reshape(-1, array.shape[2])


def attend(packed_q, packed_k, packed_v, out_grad, doc_row):
    row_count = packed_q.shape[0]
    group_size = HEADS // KV_HEADS
    score_scale = HEAD_DIM ** (-0.5)
    query_heads = packed_q.reshape(row_count, KV_HEADS, group_size, HEAD_DIM)
    grad_heads = out_grad.reshape(row_count, KV_HEADS, group_size, HEAD_DIM)
    key_heads = packed_k.reshape(row_count, KV_HEADS, HEAD_DIM)
    value_heads = packed_v.reshape(row_count, KV_HEADS, HEAD_DIM)
    scores = (
        jnp.einsum("igxd,jgd->gxij", query_heads, key_heads, preferred_element_type=jnp.float32)
        * score_scale
    )
    positions = jnp.arange(row_count, dtype=jnp.int32)
    allowed = (doc_row[:, None] == doc_row[None, :]) & (positions[None, :] <= positions[:, None])
    masked = jnp.where(allowed, scores, -jnp.inf)
    row_peak = jnp.max(masked, axis=-1, keepdims=True)
    exponent = jnp.exp(masked - row_peak)
    attn_probs = exponent / jnp.sum(exponent, axis=-1, keepdims=True)
    probs_half = attn_probs.astype(jnp.bfloat16)
    attn_out = jnp.einsum(
        "gxij,jgd->igxd", probs_half, value_heads, preferred_element_type=jnp.float32
    )
    delta_rows = jnp.sum(grad_heads.astype(jnp.float32) * attn_out, axis=-1)
    prob_grad = jnp.einsum(
        "igxd,jgd->gxij", grad_heads, value_heads, preferred_element_type=jnp.float32
    )
    score_grad = (
        attn_probs * (prob_grad - jnp.transpose(delta_rows, (1, 2, 0))[..., None]) * score_scale
    ).astype(jnp.bfloat16)
    query_grad = jnp.einsum(
        "gxij,jgd->igxd", score_grad, key_heads, preferred_element_type=jnp.float32
    )
    key_grad = jnp.einsum(
        "gxij,igxd->jgd", score_grad, query_heads, preferred_element_type=jnp.float32
    )
    value_grad = jnp.einsum(
        "gxij,igxd->jgd", probs_half, grad_heads, preferred_element_type=jnp.float32
    )
    return (
        query_grad.astype(jnp.bfloat16).reshape(row_count, -1),
        key_grad.astype(jnp.bfloat16).reshape(row_count, -1),
        value_grad.astype(jnp.bfloat16).reshape(row_count, -1),
    )


def local(normed, queries, key_rows, out_grad, value_weight, doc_ids, send_to, take_from):
    dp_count = lax.axis_size("dp")
    fsdp_count = lax.axis_size("fsdp")
    row_count = normed.shape[0]
    blocks = row_count // BLOCK_ROWS
    grad_scale = (row_count * dp_count * fsdp_count) ** (-0.5)
    dp_lanes = jnp.arange(dp_count, dtype=jnp.int32)
    outgoing = (send_to[0][None, :] == dp_lanes[:, None]).astype(jnp.bfloat16)
    incoming = (take_from[0][:, None] == dp_lanes[None, :]).astype(jnp.bfloat16)
    columns = normed
    values = jnp.dot(
        columns,
        lax.all_gather(value_weight, "fsdp", axis=0, tiled=True),
        preferred_element_type=jnp.float32,
    ).astype(jnp.bfloat16)
    arrived = (
        lax.all_to_all(
            to_slots(queries, outgoing, blocks), "dp", split_axis=0, concat_axis=0, tiled=True
        ),
        lax.all_to_all(
            to_slots(key_rows, outgoing, blocks), "dp", split_axis=0, concat_axis=0, tiled=True
        ),
        lax.all_to_all(
            to_slots(values, outgoing, blocks), "dp", split_axis=0, concat_axis=0, tiled=True
        ),
    )
    packed_q = from_slots(arrived[0], incoming)
    packed_k = from_slots(arrived[1], incoming)
    packed_v = from_slots(arrived[2], incoming)
    query_grad, key_grad, value_grad = attend(packed_q, packed_k, packed_v, out_grad, doc_ids[0])
    input_grad = lax.dot_general(
        value_grad,
        lax.all_gather(value_weight, "fsdp", axis=0, tiled=True),
        (((1,), (1,)), ((), ())),
        preferred_element_type=jnp.float32,
    )
    input_grad = input_grad.astype(jnp.bfloat16)
    shaped = value_grad.reshape(blocks, BLOCK_ROWS, value_grad.shape[1])
    returning = jnp.einsum(
        "bs,bcw->scw", incoming, shaped, preferred_element_type=jnp.float32
    ).astype(jnp.bfloat16)
    landed = lax.all_to_all(returning, "dp", split_axis=0, concat_axis=0, tiled=True)
    pair_grad = (
        jnp.einsum("pb,pcw->bcw", outgoing, landed, preferred_element_type=jnp.float32)
        .astype(jnp.bfloat16)
        .reshape(row_count, -1)
    )
    columns = normed
    weight_grad = lax.psum_scatter(
        lax.dot_general(
            columns, pair_grad, (((0,), (0,)), ((), ())), preferred_element_type=jnp.float32
        )
        * grad_scale,
        ("dp", "fsdp"),
        scatter_dimension=0,
        tiled=True,
    )
    return (query_grad, key_grad, input_grad, weight_grad)


def solution(mesh):
    placed = (
        P(("dp", "fsdp"), None),
        P(("dp", "fsdp"), None),
        P(("dp", "fsdp"), None),
        P(("dp", "fsdp"), None),
        P("fsdp", None),
        P(("dp", "fsdp"), None),
        P(("dp", "fsdp"), None),
        P(("dp", "fsdp"), None),
    )
    return jax.shard_map(
        local,
        mesh=mesh,
        in_specs=placed,
        out_specs=(
            P(("dp", "fsdp"), None),
            P(("dp", "fsdp"), None),
            P(("dp", "fsdp"), None),
            P(("dp", "fsdp"), None),
        ),
        check_vma=False,
    )
```

profile of v0, /device:TPU:0, one launch (start us, length us, event | category | flops | bytes accessed | tf_op | source)
XLA Modules:
  0.0 1498.8 jit_solution(17403453055817149073)
XLA Ops:
  8.0 1.7 convolution_convert_fusion.5
  9.7 1.3 copy.45
  11.0 6.9 all-to-all-start
  17.9 2.7 convolution_convert_fusion.1
  20.7 3.4 copy.49
  24.0 14.5 all-to-all-done
  38.6 5.3 all-to-all-start.1
  43.9 0.7 all-gather.2.cloned.1.call-update
  44.6 2.6 copy.58
  47.2 0.8 fusion.23
  48.0 1.7 convolution_convert_fusion.8
  49.7 0.1 copy.47
  49.8 0.8 reshape_reshape.12
  50.7 1.3 copy.81
  51.9 63.7 %all-to-all-done.1 = bf16[16,48,2048]{2,1,0:T(8,128)(2,1)} async-done(((bf16[16,48,2048]{2,1,0:T(8,128)(2,1)}), bf16[16,48,2048]{2,1,0:T(8,128)(2,1)}, u32[]{:S(2)}, u32[]{:S(2)}) %all-to-all-start.1) | async-done | bytes 3145760 | tf_op jit(solution)/shard_map/all_to_all | solution.py:87
  115.6 5.4 fusion.12
  121.0 2.0 copy.51
  123.0 3.8 reshape_reshape.13
  126.8 3.9 copy.65
  130.7 8.7 fusion.47
  139.4 4.8 fusion.8
  144.3 2.3 fusion.17
  146.6 1.9 copy.68
  148.5 1.9 reshape_reshape.15
  150.4 1.5 convolution_convert_fusion.3
  151.9 0.4 copy.70
  152.3 26.8 %all_to_all.20 = bf16[16,48,512]{2,1,0:T(8,128)(2,1)S(1)} all-to-all(bf16[16,48,512]{2,1,0:T(8,128)(2,1)S(1)} %copy.70), channel_id=1, replica_groups=mesh['dp'=16,'fsdp'=16] {'dp'}, dimensions={0} | all-to-all | bytes 1572864 | tf_op jit(solution)/shard_map/all_to_all | solution.py:112
  179.2 0.5 convolution_convert_fusion.6
  179.7 0.1 copy.72
  179.8 5.7 multiply_bitcast_fusion
  185.5 9.0 copy.95
  194.6 4.0 convolution_convert_fusion.9
  198.6 0.5 convolution_convert_fusion.4
  199.1 1.4 copy.55
  200.4 3.8 all-to-all-start.2
  204.3 5.7 convolution_convert_fusion
  210.0 15.1 %all-to-all-done.2 = bf16[16,48,512]{2,1,0:T(8,128)(2,1)S(1)} async-done(((bf16[16,48,512]{2,1,0:T(8,128)(2,1)}), bf16[16,48,512]{2,1,0:T(8,128)(2,1)S(1)}, u32[]{:S(2)}, u32[]{:S(2)}) %all-to-all-start.2) | async-done | bytes 786464 | tf_op jit(solution)/shard_map/all_to_all | solution.py:93
  225.1 0.5 convolution_convert_fusion.7
  225.7 0.1 copy.57
  225.8 0.1 reshape_reshape.14
  225.9 0.3 copy.79
  226.2 3.3 fusion.9
  229.6 4.8 fusion.3
  234.4 2.7 convolution_convert_fusion.2
  237.1 2.7 copy.73
  239.8 4.3 fusion.16
  244.1 0.9 copy.74
  245.1 1246.3 %reduce-scatter.4.cloned.1.call-done = f32[16,512]{1,0:T(8,128)} async-done(((f32[4096,512]{1,0:T(8,128)}), f32[16,512]{1,0:T(8,128)}) %reduce-scatter.4.cloned.1.call-update) | async-done | bytes 32784
  (27 shorter events, 0.2 us)
Async XLA Ops:
  8.0 171.8 %copy-start = (bf16[384,4096]{1,0:T(8,128)(2,1)S(1)}, bf16[384,4096]{1,0:T(8,128)(2,1)}, u32[]{:S(2)}) copy-start(bf16[384,4096]{1,0:T(8,128)(2,1)} %param.8) | copy-start | bytes 9437188
  8.0 9.9 copy-start.8
  11.0 27.6 %all-to-all-start = ((bf16[16,48,512]{2,1,0:T(8,128)(2,1)}), bf16[16,48,512]{2,1,0:T(8,128)(2,1)}, u32[]{:S(2)}, u32[]{:S(2)}) async-start(bf16[16,48,512]{2,1,0:T(8,128)(2,1)} %copy.45), calls=%async_computation | async-start | bytes 1572864 | tf_op jit(solution)/shard_map/all_to_all | solution.py:90
  38.6 77.0 %all-to-all-start.1 = ((bf16[16,48,2048]{2,1,0:T(8,128)(2,1)}), bf16[16,48,2048]{2,1,0:T(8,128)(2,1)}, u32[]{:S(2)}, u32[]{:S(2)}) async-start(bf16[16,48,2048]{2,1,0:T(8,128)(2,1)} %copy.49), calls=%async_computation.1 | async-start | bytes 6291456 | tf_op jit(solution)/shard_map/all_to_all | solution.py:87
  43.8 3.4 copy-start.10
  43.8 4.2 copy-start.9
  43.9 150.7 %all-gather.2.cloned.1.call-start = ((), (), s32[]{:S(2)}) async-start(), calls=%async_computation.5 | async-start | bytes 4456448 | tf_op jit(solution)/shard_map/all_gather | solution.py:83
  44.6 1446.8 %reduce-scatter.4.cloned.1.call-start = ((), (), s32[]{:S(2)}) async-start(), calls=%async_computation.6 | async-start | bytes 8421376
  139.4 4.8 copy-start.4
  144.2 2.3 copy-start.2
  198.6 5.7 copy-start.6
  200.4 24.7 %all-to-all-start.2 = ((bf16[16,48,512]{2,1,0:T(8,128)(2,1)}), bf16[16,48,512]{2,1,0:T(8,128)(2,1)S(1)}, u32[]{:S(2)}, u32[]{:S(2)}) async-start(bf16[16,48,512]{2,1,0:T(8,128)(2,1)} %copy.55), calls=%async_computation.2 | async-start | bytes 1572864 | tf_op jit(solution)/shard_map/all_to_all | solution.py:93
  210.0 16.2 %copy-start.5 = (bf16[384,2048]{0,1:T(8,128)(2,1)S(1)}, bf16[384,2048]{0,1:T(8,128)(2,1)}, u32[]{:S(2)}) copy-start(bf16[384,2048]{0,1:T(8,128)(2,1)} %copy.58) | copy-start | bytes 4718596
  226.2 3.4 copy-start.7
  234.4 2.7 copy-start.3
  237.1 1254.3 %copy-start.1 = (bf16[384,4096]{1,0:T(8,128)(2,1)S(1)}, bf16[384,4096]{1,0:T(8,128)(2,1)}, u32[]{:S(2)}) copy-start(bf16[384,4096]{1,0:T(8,128)(2,1)} %param.8) | copy-start | bytes 9437188
Sparse Core Ops, SparseCore 0:
  47.1 57.8 all-gather.1
Sparse Core Ops, SparseCore 1:
  194.6 1296.7 reduce-scatter.3
where the time goes:
time: 1500 us
  waiting for transfers between devices  1340 us (89%)
  matrix products  55.9 us (4%)
  local copies, waits for them, and re-layouts  38.2 us (3%)
  blocking collectives  26.8 us (2%)
  starting transfers between devices  16.1 us (1%)
  between operations  15.7 us (1%)
    unnamed x3, waiting for transfers between devices  1250 us
    all_to_all x1, waiting for transfers between devices, local(): lax.all_to_all(to_slots(queries, outgoing, blocks), 'dp', split_axis=0, c...  63.7 us
  transfers between devices with their start and end apart: 5, of which 4 were waited for; matrix products, arithmetic and copies ran while one was open for 6% of the time, Pallas kernels for 0%

commit v1 on v0

v1 whole, which is shorter than its diff:
```python
import jax
import jax.numpy as jnp
from jax import lax
from jax.experimental import pallas as pl
from jax.experimental.pallas import tpu as pltpu
from jax.sharding import PartitionSpec as P

HEADS = 16
KV_HEADS = 4
HEAD_DIM = 128
GROUP = HEADS // KV_HEADS
BLOCK_ROWS = 48
QUERY_TILE = 128


def outgoing_kernel(send, q_ref, k_ref, out_ref):
    width = q_ref.shape[1]
    out_ref[0, :, :width] = q_ref[...]
    out_ref[0, :, width:] = k_ref[...]


def outgoing_slots(send, queries, key_rows, peers):
    rows, width = queries.shape
    key_width = key_rows.shape[1]
    blocks = rows // BLOCK_ROWS
    return pl.pallas_call(
        outgoing_kernel,
        grid_spec=pltpu.PrefetchScalarGridSpec(
            num_scalar_prefetch=1,
            grid=(blocks,),
            in_specs=[
                pl.BlockSpec((BLOCK_ROWS, width), lambda b, send: (b, 0)),
                pl.BlockSpec((BLOCK_ROWS, key_width), lambda b, send: (b, 0)),
            ],
            out_specs=pl.BlockSpec(
                (1, BLOCK_ROWS, width + key_width), lambda b, send: (send[b], 0, 0)
            ),
        ),
        out_shape=jax.ShapeDtypeStruct((peers, BLOCK_ROWS, width + key_width), queries.dtype),
        name="outgoing_slots",
    )(send, queries, key_rows)


def values_kernel(send, normed_ref, weight_ref, out_ref, total):
    step = pl.program_id(0)
    part = jnp.dot(normed_ref[...], weight_ref[...], preferred_element_type=jnp.float32)

    @pl.when(step == 0)
    def _():
        total[...] = part

    @pl.when(step > 0)
    def _():
        total[...] += part

    @pl.when(step == pl.num_programs(0) - 1)
    def _():
        for b in range(total.shape[0] // BLOCK_ROWS):
            rows = total[b * BLOCK_ROWS : (b + 1) * BLOCK_ROWS, :]
            out_ref[send[b]] = rows.astype(out_ref.dtype)


def value_slots(send, normed, weight, peers):
    rows, depth = normed.shape
    width = weight.shape[1]
    tile = 512
    return pl.pallas_call(
        values_kernel,
        grid_spec=pltpu.PrefetchScalarGridSpec(
            num_scalar_prefetch=1,
            grid=(depth // tile,),
            in_specs=[
                pl.BlockSpec((rows, tile), lambda k, send: (0, k)),
                pl.BlockSpec((tile, width), lambda k, send: (k, 0)),
            ],
            out_specs=pl.BlockSpec((peers, BLOCK_ROWS, width), lambda k, send: (0, 0, 0)),
            scratch_shapes=[pltpu.VMEM((rows, width), jnp.float32)],
        ),
        out_shape=jax.ShapeDtypeStruct((peers, BLOCK_ROWS, width), normed.dtype),
        name="value_slots",
    )(send, normed, weight)


def attention_kernel(
    take, q_ref, k_ref, v_ref, grad_ref, doc_row, doc_col,
    query_grad, key_grad, value_grad, returning,
    q_rows, k_rows, v_rows, bias, key_total, value_total,
):
    rows = grad_ref.shape[0]
    blocks = rows // BLOCK_ROWS
    scale = HEAD_DIM ** (-0.5)

    @pl.when(pl.program_id(0) == 0)
    def _():
        i = lax.broadcasted_iota(jnp.int32, (rows, rows), 0)
        j = lax.broadcasted_iota(jnp.int32, (rows, rows), 1)
        allowed = (doc_col[...] == doc_row[...]) & (j <= i)
        bias[...] = jnp.where(allowed, 0.0, -jnp.inf)

    for p in range(blocks):
        place = slice(p * BLOCK_ROWS, (p + 1) * BLOCK_ROWS)
        q_rows[place, :] = q_ref[take[p]]
        k_rows[place, :] = k_ref[take[p]]
        v_rows[place, :] = v_ref[take[p]]

    key_total[...] = jnp.zeros_like(key_total)
    value_total[...] = jnp.zeros_like(value_total)
    for start in range(0, rows, QUERY_TILE):
        place = slice(start, start + QUERY_TILE)
        reach = start + QUERY_TILE
        q = jnp.concatenate(
            [q_rows[place, x * HEAD_DIM : (x + 1) * HEAD_DIM] for x in range(GROUP)], axis=0
        )
        g = jnp.concatenate(
            [grad_ref[place, x * HEAD_DIM : (x + 1) * HEAD_DIM] for x in range(GROUP)], axis=0
        )
        k = k_rows[:reach, :]
        v = v_rows[:reach, :]
        nt = (((1,), (1,)), ((), ()))
        tn = (((0,), (0,)), ((), ()))
        scores = lax.dot_general(q, k, nt, preferred_element_type=jnp.float32) * scale
        hide = bias[place, :reach]
        scores = scores + jnp.concatenate([hide] * GROUP, axis=0)
        peak = jnp.max(scores, axis=-1, keepdims=True)
        exponent = jnp.exp(scores - peak)
        probs = exponent / jnp.sum(exponent, axis=-1, keepdims=True)
        half = probs.astype(jnp.bfloat16)
        attn = jnp.dot(half, v, preferred_element_type=jnp.float32)
        delta = jnp.sum(g.astype(jnp.float32) * attn, axis=-1, keepdims=True)
        prob_grad = lax.dot_general(g, v, nt, preferred_element_type=jnp.float32)
        score_grad = (probs * (prob_grad - delta) * scale).astype(jnp.bfloat16)
        back = jnp.dot(score_grad, k, preferred_element_type=jnp.float32)
        for x in range(GROUP):
            query_grad[place, x * HEAD_DIM : (x + 1) * HEAD_DIM] = back[
                x * QUERY_TILE : (x + 1) * QUERY_TILE
            ].astype(query_grad.dtype)
        key_total[:reach, :] += lax.dot_general(
            score_grad, q, tn, preferred_element_type=jnp.float32
        )
        value_total[:reach, :] += lax.dot_general(half, g, tn, preferred_element_type=jnp.float32)
    key_grad[...] = key_total[...].astype(key_grad.dtype)
    value_grad[...] = value_total[...].astype(value_grad.dtype)
    returning[...] = jnp.zeros_like(returning)
    for p in range(blocks):
        place = slice(p * BLOCK_ROWS, (p + 1) * BLOCK_ROWS)
        returning[take[p]] = value_total[place, :].astype(returning.dtype)


def attention(take, arrived, arrived_v, out_grad, doc_ids):
    peers = arrived.shape[0]
    rows = out_grad.shape[0]
    wide = GROUP * HEAD_DIM
    first_key = HEADS
    bf16 = jnp.bfloat16
    return pl.pallas_call(
        attention_kernel,
        grid_spec=pltpu.PrefetchScalarGridSpec(
            num_scalar_prefetch=1,
            grid=(KV_HEADS,),
            in_specs=[
                pl.BlockSpec((peers, BLOCK_ROWS, wide), lambda g, take: (0, 0, g)),
                pl.BlockSpec((peers, BLOCK_ROWS, HEAD_DIM), lambda g, take: (0, 0, first_key + g)),
                pl.BlockSpec((peers, BLOCK_ROWS, HEAD_DIM), lambda g, take: (0, 0, g)),
                pl.BlockSpec((rows, wide), lambda g, take: (0, g)),
                pl.BlockSpec((1, rows), lambda g, take: (0, 0)),
                pl.BlockSpec((rows, 1), lambda g, take: (0, 0)),
            ],
            out_specs=[
                pl.BlockSpec((rows, wide), lambda g, take: (0, g)),
                pl.BlockSpec((rows, HEAD_DIM), lambda g, take: (0, g)),
                pl.BlockSpec((rows, HEAD_DIM), lambda g, take: (0, g)),
                pl.BlockSpec((peers, BLOCK_ROWS, HEAD_DIM), lambda g, take: (0, 0, g)),
            ],
            scratch_shapes=[
                pltpu.VMEM((rows, wide), bf16),
                pltpu.VMEM((rows, HEAD_DIM), bf16),
                pltpu.VMEM((rows, HEAD_DIM), bf16),
                pltpu.VMEM((rows, rows), jnp.float32),
                pltpu.VMEM((rows, HEAD_DIM), jnp.float32),
                pltpu.VMEM((rows, HEAD_DIM), jnp.float32),
            ],
        ),
        out_shape=[
            jax.ShapeDtypeStruct((rows, KV_HEADS * wide), bf16),
            jax.ShapeDtypeStruct((rows, KV_HEADS * HEAD_DIM), bf16),
            jax.ShapeDtypeStruct((rows, KV_HEADS * HEAD_DIM), bf16),
            jax.ShapeDtypeStruct((peers, BLOCK_ROWS, KV_HEADS * HEAD_DIM), bf16),
        ],
        name="attention_backward",
    )(take, arrived, arrived, arrived_v, out_grad, doc_ids, doc_ids.reshape(rows, 1))


def weight_kernel(send, place, normed_ref, landed_ref, out_ref, home):
    @pl.when(pl.program_id(0) == 0)
    def _():
        for b in range(home.shape[0] // BLOCK_ROWS):
            home[b * BLOCK_ROWS : (b + 1) * BLOCK_ROWS, :] = landed_ref[send[b]]

    part = lax.dot_general(
        normed_ref[...], home[...], (((0,), (0,)), ((), ())), preferred_element_type=jnp.float32
    )
    out_ref[...] = part.reshape(out_ref.shape).astype(out_ref.dtype)


def weight_part(send, place, normed, landed, columns):
    rows, depth = normed.shape
    peers, _, width = landed.shape
    steps = place.shape[0]
    tile = depth // peers
    share = tile // columns
    return pl.pallas_call(
        weight_kernel,
        grid_spec=pltpu.PrefetchScalarGridSpec(
            num_scalar_prefetch=2,
            grid=(steps,),
            in_specs=[
                pl.BlockSpec((rows, tile), lambda z, send, place: (0, place[z])),
                pl.BlockSpec((peers, BLOCK_ROWS, width), lambda z, send, place: (0, 0, 0)),
            ],
            out_specs=pl.BlockSpec(
                (columns, 1, share, width), lambda z, send, place: (0, z, 0, 0)
            ),
            scratch_shapes=[pltpu.VMEM((rows, width), jnp.bfloat16)],
        ),
        out_shape=jax.ShapeDtypeStruct((columns, steps, share, width), jnp.bfloat16),
        name="weight_part",
    )(send, place, normed, landed)


def local(normed, queries, key_rows, out_grad, value_weight, doc_ids, send_to, take_from):
    dp_count = lax.axis_size("dp")
    fsdp_count = lax.axis_size("fsdp")
    rows = normed.shape[0]
    grad_scale = (rows * dp_count * fsdp_count) ** (-0.5)
    send, take = send_to[0], take_from[0]
    core = lax.axis_index("dp") % 2

    arrived = lax.all_to_all(
        outgoing_slots(send, queries, key_rows, dp_count), "dp", 0, 0, tiled=True
    )
    weight = lax.all_gather(value_weight, "fsdp", axis=0, tiled=True)
    arrived_v = lax.all_to_all(
        value_slots(send, normed, weight, dp_count), "dp", 0, 0, tiled=True
    )
    query_grad, key_grad, value_grad, returning = attention(
        take, arrived, arrived_v, out_grad, doc_ids
    )
    landed = lax.all_to_all(returning, "dp", 0, 0, tiled=True)
    input_grad = lax.dot_general(
        value_grad, weight, (((1,), (1,)), ((), ())), preferred_element_type=jnp.float32
    ).astype(jnp.bfloat16)

    steps = dp_count // 2
    pairs = 2 * jnp.arange(steps, dtype=jnp.int32)
    theirs = weight_part(send, pairs + (1 - core), normed, landed, fsdp_count)
    swapped = lax.ppermute(theirs, "dp", [(i, i ^ 1) for i in range(dp_count)])
    mine = weight_part(send, pairs + core, normed, landed, fsdp_count)
    chip = (mine.astype(jnp.float32) + swapped.astype(jnp.float32)).astype(jnp.bfloat16)
    chips = lax.all_to_all(chip, "fsdp", 0, 0, tiled=True)
    plane = jnp.sum(chips.astype(jnp.float32), axis=0).astype(jnp.bfloat16)
    groups = [list(range(c, dp_count, 2)) for c in range(2)]
    planes = lax.all_to_all(plane, "dp", 0, 0, axis_index_groups=groups, tiled=True)
    weight_grad = jnp.sum(planes.astype(jnp.float32), axis=0) * grad_scale
    return (query_grad, key_grad, input_grad, weight_grad)


def solution(mesh):
    rows = P(("dp", "fsdp"), None)
    return jax.shard_map(
        local,
        mesh=mesh,
        in_specs=(rows, rows, rows, rows, P("fsdp", None), rows, rows, rows),
        out_specs=(rows, rows, rows, rows),
        check_vma=False,
    )
```

time: 1500 us -> 256 us (0.17)
  waiting for transfers between devices: 1340 us -> 124 us
  matrix products: 55.9 us -> 5.68 us
  Pallas kernels: 0 us -> 44.7 us
  local copies, waits for them, and re-layouts: 38.2 us -> 2.62 us
    unnamed x3 -> x1, waiting for transfers between devices: 1250 us -> 0.68 us
    all_gather x1, waiting for transfers between devices: 0.02 us -> 47 us  [local(): weight = lax.all_gather(value_weight, 'fsdp', axis=0, tiled=True)]
    pallas_call x0 -> x5, Pallas kernels: none -> 44.7 us  [the longest x2 15.5 us: weight_part(): pl.pallas_call(weight_kernel, grid_spec=pltpu.PrefetchScalarGridSpec(num_...]
    dot_general x16 -> x1, matrix products: 47.2 us -> 5.68 us  [local(): lax.dot_general(value_grad, weight, (((1,), (1,)), ((), ())), preferred_e...]
    all_to_all x3 -> x4, waiting for transfers between devices: 93.3 us -> 76.4 us  [the longest x1 33.1 us: local(): lax.all_to_all(outgoing_slots(send, queries, key_rows, dp_count), 'dp', 0...]
  transfers between devices with their start and end apart: 5 -> 6, of which waited for: 4 -> 5; matrix products, arithmetic and copies ran while one was open for 6% -> 3% of each run, Pallas kernels for 0% -> 9%
where the time goes in v1:
time: 256 us; the launch traced here: 254 us
  waiting for transfers between devices  124 us (48%)
  Pallas kernels  44.7 us (17%)
  blocking collectives  35.4 us (14%)
  starting transfers between devices  22.5 us (9%)
  between operations  14.1 us (6%)
  matrix products  5.68 us (2%)
  other arithmetic  5.26 us (2%)
  local copies, waits for them, and re-layouts  2.62 us (1%)
    all_gather x1, waiting for transfers between devices, local(): weight = lax.all_gather(value_weight, 'fsdp', axis=0, tiled=True)  47 us
    all_to_all x1, blocking collectives, local(): chips = lax.all_to_all(chip, 'fsdp', 0, 0, tiled=True)  35.4 us
    all_to_all x1, waiting for transfers between devices, local(): lax.all_to_all(outgoing_slots(send, queries, key_rows, dp_count), 'dp', 0...  33.1 us
    all_to_all x1, waiting for transfers between devices, local(): landed = lax.all_to_all(returning, 'dp', 0, 0, tiled=True)  20.2 us
    all_to_all x1, waiting for transfers between devices, local(): lax.all_to_all(value_slots(send, normed, weight, dp_count), 'dp', 0, 0, t...  19.8 us
    pallas_call x2, Pallas kernels, weight_part(): pl.pallas_call(weight_kernel, grid_spec=pltpu.PrefetchScalarGridSpec(num_...  15.5 us
    pallas_call x1, Pallas kernels, attention(): pl.pallas_call(attention_kernel, grid_spec=pltpu.PrefetchScalarGridSpec(n...  14.3 us
    pallas_call x1, Pallas kernels, value_slots(): pl.pallas_call(values_kernel, grid_spec=pltpu.PrefetchScalarGridSpec(num_...  8.67 us
  transfers between devices with their start and end apart: 6, of which 5 were waited for; matrix products, arithmetic and copies ran while one was open for 3% of the time, Pallas kernels for 9%

profile of v1, /device:TPU:0, one launch (start us, length us, event | category | flops | bytes accessed | tf_op | source)
XLA Modules:
  0.0 254.3 jit_solution(5509759092837944902)
XLA Ops:
  7.2 0.0 all-gather.2.cloned.1.call-start
  7.2 0.7 all-gather.2.cloned.1.call-update
  7.9 6.3 %outgoing_slots.1 = bf16[16,48,2560]{2,1,0:T(8,128)(2,1)} custom-call(s32[8]{0:T(128)} %bitcast.5, bf16[384,2048]{1,0:T(8,128)(2,1)} %q_ref.1, bf16[384,512]{1,0:T(8,128)(2,1)} %k_ref.1), custom_call_target="tpu_custom_call" | custom-call | tf_op jit(solution)/shard_map/outgoing_slots/pallas_call | solution.py:26
  14.2 6.9 %all-to-all-start = ((bf16[16,48,2560]{2,1,0:T(8,128)(2,1)}), bf16[16,48,2560]{2,1,0:T(8,128)(2,1)}, u32[]{:S(2)}, u32[]{:S(2)}) async-start(bf16[16,48,2560]{2,1,0:T(8,128)(2,1)} %outgoing_slots.1), calls=%async_computation | async-start | bytes 7864320 | tf_op jit(solution)/shard_map/all_to_all | solution.py:238
  21.1 0.0 copy-start.2
  21.1 47.0 %all-gather.2.cloned.1.call-done.weight_ref = bf16[4096,512]{1,0:T(8,128)(2,1)} async-done(((bf16[256,512]{1,0:T(8,128)(2,1)}), bf16[4096,512]{1,0:T(8,128)(2,1)}) %all-gather.2.cloned.1.call-update) | async-done | bytes 4194320 | tf_op jit(solution)/shard_map/all_gather | solution.py:241
  68.0 8.7 %value_slots.1 = bf16[16,48,512]{2,1,0:T(8,128)(2,1)} custom-call(s32[8]{0:T(128)} %bitcast.6, bf16[384,4096]{1,0:T(8,128)(2,1)} %normed_ref.5, bf16[4096,512]{1,0:T(8,128)(2,1)} %all-gather.2.cloned.1.call-done.weight_ref), custom_call_target="tpu_custom_call" | custom-call | tf_op jit(solution)/shard_map/value_slots/pallas_call | solution.py:67
  76.7 33.1 %all-to-all-done.q_ref.k_ref = bf16[16,48,2560]{2,1,0:T(8,128)(2,1)} async-done(((bf16[16,48,2560]{2,1,0:T(8,128)(2,1)}), bf16[16,48,2560]{2,1,0:T(8,128)(2,1)}, u32[]{:S(2)}, u32[]{:S(2)}) %all-to-all-start) | async-done | bytes 3932192 | tf_op jit(solution)/shard_map/all_to_all | solution.py:238
  109.8 4.6 %all-to-all-start.1 = ((bf16[16,48,512]{2,1,0:T(8,128)(2,1)}), bf16[16,48,512]{2,1,0:T(8,128)(2,1)S(1)}, u32[]{:S(2)}, u32[]{:S(2)}) async-start(bf16[16,48,512]{2,1,0:T(8,128)(2,1)} %value_slots.1), calls=%async_computation.1 | async-start | bytes 1572864 | tf_op jit(solution)/shard_map/all_to_all | solution.py:242
  114.4 0.0 copy-done.2
  114.4 0.8 copy.13.doc_col
  115.3 19.8 %all-to-all-done.1.v_ref = bf16[16,48,512]{2,1,0:T(8,128)(2,1)S(1)} async-done(((bf16[16,48,512]{2,1,0:T(8,128)(2,1)}), bf16[16,48,512]{2,1,0:T(8,128)(2,1)S(1)}, u32[]{:S(2)}, u32[]{:S(2)}) %all-to-all-start.1) | async-done | bytes 786464 | tf_op jit(solution)/shard_map/all_to_all | solution.py:242
  135.0 0.0 copy-start.1
  135.0 0.9 copy-done.1
  135.9 14.3 %attention_backward.1 = (bf16[384,2048]{1,0:T(8,128)(2,1)}, bf16[384,512]{1,0:T(8,128)(2,1)}, bf16[384,512]{1,0:T(8,128)(2,1)}, bf16[16,48,512]{2,1,0:T(8,128)(2,1)}) custom-call(s32[8]{0:T(128)} %bitcast.10, bf16[16,48,2560]{2,1,0:T(8,128)(2,1)} %all-to-all-done.q_ref.k_ref, bf16[16,48,2560]{2,1,0:T(8,128)(2,1)} %all-to-all-done.q_ref.k_ref, ...), custom_call_target="tpu_custom_call" | custom-call | tf_op jit(solution)/shard_map/attention_backward/pallas_call | solution.py:155
  150.2 5.2 %all-to-all-start.2 = ((bf16[16,48,512]{2,1,0:T(8,128)(2,1)}), bf16[16,48,512]{2,1,0:T(8,128)(2,1)S(1)}, u32[]{:S(2)}, u32[]{:S(2)}) async-start(bf16[16,48,512]{2,1,0:T(8,128)(2,1)} %get-tuple-element.11), calls=%async_computation.2 | async-start | bytes 1572864 | tf_op jit(solution)/shard_map/all_to_all | solution.py:248
  155.4 0.5 fusion.place
  155.9 20.2 %all-to-all-done.2.landed_ref = bf16[16,48,512]{2,1,0:T(8,128)(2,1)S(1)} async-done(((bf16[16,48,512]{2,1,0:T(8,128)(2,1)}), bf16[16,48,512]{2,1,0:T(8,128)(2,1)S(1)}, u32[]{:S(2)}, u32[]{:S(2)}) %all-to-all-start.2) | async-done | bytes 786464 | tf_op jit(solution)/shard_map/all_to_all | solution.py:248
  176.2 0.0 copy-start
  176.2 0.9 copy-done
  177.1 7.7 %weight_part.3 = bf16[16,8,16,512]{3,2,1,0:T(8,128)(2,1)} custom-call(s32[8]{0:T(128)} %bitcast.7, s32[8]{0:T(128)} %fusion.place, bf16[384,4096]{1,0:T(8,128)(2,1)} %normed_ref.5, bf16[16,48,512]{2,1,0:T(8,128)(2,1)} %copy-done), custom_call_target="tpu_custom_call" | custom-call | tf_op jit(solution)/shard_map/weight_part/pallas_call | solution.py:211
  184.8 2.3 collective-permute-start
  187.1 0.5 fusion.1.place
  187.6 7.8 %weight_part.2 = bf16[16,8,16,512]{3,2,1,0:T(8,128)(2,1)} custom-call(s32[8]{0:T(128)} %bitcast.8, s32[8]{0:T(128)} %fusion.1.place, bf16[384,4096]{1,0:T(8,128)(2,1)} %normed_ref.5, bf16[16,48,512]{2,1,0:T(8,128)(2,1)} %copy-done), custom_call_target="tpu_custom_call" | custom-call | tf_op jit(solution)/shard_map/weight_part/pallas_call | solution.py:211
  195.4 0.0 collective-permute-done
  195.4 2.5 add_convert_fusion
  197.9 0.0 copy-start.3
  197.9 35.4 %all_to_all.25 = bf16[16,8,16,512]{3,2,1,0:T(8,128)(2,1)S(1)} all-to-all(bf16[16,8,16,512]{3,2,1,0:T(8,128)(2,1)S(1)} %add_convert_fusion), channel_id=1, replica_groups=mesh['dp'=16,'fsdp'=16] {'fsdp'}, dimensions={0} | all-to-all | bytes 4194304 | tf_op jit(solution)/shard_map/all_to_all | solution.py:259
  233.3 1.1 reduce_sum.21
  234.4 3.4 %all-to-all-start.4 = ((bf16[8,16,512]{2,1,0:T(8,128)(2,1)}), bf16[8,16,512]{2,1,0:T(8,128)(2,1)S(1)}, u32[]{:S(2)}, u32[]{:S(2)}) async-start(bf16[8,16,512]{2,1,0:T(8,128)(2,1)} %reduce_sum.21), calls=%async_computation.4 | async-start | bytes 262144 | tf_op jit(solution)/shard_map/all_to_all | solution.py:262
  237.8 0.0 copy-done.3
  237.8 5.7 %convolution_convert_fusion = bf16[384,4096]{1,0:T(8,128)(2,1)} fusion(bf16[384,512]{1,0:T(8,128)(2,1)S(1)} %copy-done.3, bf16[4096,512]{1,0:T(8,128)(2,1)} %all-gather.2.cloned.1.call-done.weight_ref), kind=kOutput, calls=%fused_computation | convolution fusion | flops 1612185600 | bytes 7733248 | tf_op jit(solution)/shard_map/dot_general | solution.py:249
  243.5 3.3 %all-to-all-done.4 = bf16[8,16,512]{2,1,0:T(8,128)(2,1)S(1)} async-done(((bf16[8,16,512]{2,1,0:T(8,128)(2,1)}), bf16[8,16,512]{2,1,0:T(8,128)(2,1)S(1)}, u32[]{:S(2)}, u32[]{:S(2)}) %all-to-all-start.4) | async-done | bytes 131104 | tf_op jit(solution)/shard_map/all_to_all | solution.py:262
  246.8 0.6 broadcast_multiply_fusion
  (1 shorter events, 0.0 us)
Async XLA Ops:
  7.2 60.9 %all-gather.2.cloned.1.call-start = ((), (), s32[]{:S(2)}) async-start(), calls=%async_computation.5 | async-start | bytes 4456448 | tf_op jit(solution)/shard_map/all_gather | solution.py:241
  14.2 95.6 %all-to-all-start = ((bf16[16,48,2560]{2,1,0:T(8,128)(2,1)}), bf16[16,48,2560]{2,1,0:T(8,128)(2,1)}, u32[]{:S(2)}, u32[]{:S(2)}) async-start(bf16[16,48,2560]{2,1,0:T(8,128)(2,1)} %outgoing_slots.1), calls=%async_computation | async-start | bytes 7864320 | tf_op jit(solution)/shard_map/all_to_all | solution.py:238
  21.1 93.4 %copy-start.2 = (s32[1,384]{1,0:T(1,128)S(1)}, s32[1,384]{1,0:T(1,128)}, u32[]{:S(2)}) copy-start(s32[1,384]{1,0:T(1,128)} %doc_row.1) | copy-start | bytes 4612
  109.8 25.2 %all-to-all-start.1 = ((bf16[16,48,512]{2,1,0:T(8,128)(2,1)}), bf16[16,48,512]{2,1,0:T(8,128)(2,1)S(1)}, u32[]{:S(2)}, u32[]{:S(2)}) async-start(bf16[16,48,512]{2,1,0:T(8,128)(2,1)} %value_slots.1), calls=%async_computation.1 | async-start | bytes 1572864 | tf_op jit(solution)/shard_map/all_to_all | solution.py:242
  135.0 0.9 copy-start.1
  150.2 26.0 %all-to-all-start.2 = ((bf16[16,48,512]{2,1,0:T(8,128)(2,1)}), bf16[16,48,512]{2,1,0:T(8,128)(2,1)S(1)}, u32[]{:S(2)}, u32[]{:S(2)}) async-start(bf16[16,48,512]{2,1,0:T(8,128)(2,1)} %get-tuple-element.11), calls=%async_computation.2 | async-start | bytes 1572864 | tf_op jit(solution)/shard_map/all_to_all | solution.py:248
  176.2 0.9 copy-start
  184.8 10.6 %collective-permute-start = (bf16[16,8,16,512]{3,2,1,0:T(8,128)(2,1)}, bf16[16,8,16,512]{3,2,1,0:T(8,128)(2,1)S(1)}, u32[]{:S(2)}, u32[]{:S(2)}) collective-permute-start(bf16[16,8,16,512]{3,2,1,0:T(8,128)(2,1)} %weight_part.3), channel_id=1, source_target_pairs={{0,16},{16,0},{32,48},{48,32},{64,80},{80,64},{96,112},{112,96},{1... | collective-permute-start | bytes 6291464 | tf_op jit(solution)/shard_map/ppermute | solution.py:256
  197.9 39.9 %copy-start.3 = (bf16[384,512]{1,0:T(8,128)(2,1)S(1)}, bf16[384,512]{1,0:T(8,128)(2,1)}, u32[]{:S(2)}) copy-start(bf16[384,512]{1,0:T(8,128)(2,1)} %get-tuple-element.10) | copy-start | bytes 1179652
  234.4 12.4 %all-to-all-start.4 = ((bf16[8,16,512]{2,1,0:T(8,128)(2,1)}), bf16[8,16,512]{2,1,0:T(8,128)(2,1)S(1)}, u32[]{:S(2)}, u32[]{:S(2)}) async-start(bf16[8,16,512]{2,1,0:T(8,128)(2,1)} %reduce_sum.21), calls=%async_computation.4 | async-start | bytes 262144 | tf_op jit(solution)/shard_map/all_to_all | solution.py:262
Sparse Core Ops, SparseCore 0:
  10.4 57.5 all-gather.1

commit v2 on v1

--- a/solution.py
+++ b/solution.py
@@ -5,6 +5,7 @@
 from jax.experimental.pallas import tpu as pltpu
 from jax.sharding import PartitionSpec as P
 
+
 HEADS = 16
 KV_HEADS = 4
 HEAD_DIM = 128
@@ -41,50 +42,167 @@
     )(send, queries, key_rows)
 
 
-def values_kernel(send, normed_ref, weight_ref, out_ref, total):
+def halves(core, ref, width):
+    own = ref.at[:, pl.ds(pl.multiple_of(core * width, width), width)]
+    other = ref.at[:, pl.ds(pl.multiple_of((1 - core) * width, width), width)]
+    return own, other
+
+
+def values_kernel(core, piece, block, normed_ref, own_ref, other_ref, *rest):
+    outs, total = rest[:-1], rest[-1]
     step = pl.program_id(0)
-    part = jnp.dot(normed_ref[...], weight_ref[...], preferred_element_type=jnp.float32)
+    width = own_ref.shape[2]
+    own, other = halves(core[0], total, width)
 
     @pl.when(step == 0)
     def _():
-        total[...] = part
-
-    @pl.when(step > 0)
-    def _():
-        total[...] += part
+        total[...] = jnp.zeros_like(total)
+
+    rows = normed_ref[...]
+    own[...] += jnp.dot(rows, own_ref[0], preferred_element_type=jnp.float32)
+    other[...] += jnp.dot(rows, other_ref[0], preferred_element_type=jnp.float32)
 
     @pl.when(step == pl.num_programs(0) - 1)
     def _():
-        for b in range(total.shape[0] // BLOCK_ROWS):
-            rows = total[b * BLOCK_ROWS : (b + 1) * BLOCK_ROWS, :]
-            out_ref[send[b]] = rows.astype(out_ref.dtype)
-
-
-def value_slots(send, normed, weight, peers):
-    rows, depth = normed.shape
-    width = weight.shape[1]
-    tile = 512
+        for o, out in enumerate(outs):
+            first = pl.multiple_of(block[o] * BLOCK_ROWS, 16)
+            out[...] = total[pl.ds(first, BLOCK_ROWS), :].astype(out.dtype)
+
+
+def value_blocks(core, piece, block, normed, own, other):
+    rows, _ = normed.shape
+    pieces, tile, width = own.shape
+    slots = block.shape[0]
     return pl.pallas_call(
         values_kernel,
         grid_spec=pltpu.PrefetchScalarGridSpec(
-            num_scalar_prefetch=1,
-            grid=(depth // tile,),
-            in_specs=[
-                pl.BlockSpec((rows, tile), lambda k, send: (0, k)),
-                pl.BlockSpec((tile, width), lambda k, send: (k, 0)),
-            ],
-            out_specs=pl.BlockSpec((peers, BLOCK_ROWS, width), lambda k, send: (0, 0, 0)),
-            scratch_shapes=[pltpu.VMEM((rows, width), jnp.float32)],
-        ),
-        out_shape=jax.ShapeDtypeStruct((peers, BLOCK_ROWS, width), normed.dtype),
-        name="value_slots",
-    )(send, normed, weight)
+            num_scalar_prefetch=3,
+            grid=(pieces,),
+            in_specs=[
+                pl.BlockSpec((rows, tile), lambda k, core, piece, block: (0, piece[k])),
+                pl.BlockSpec((1, tile, width), lambda k, *_: (k, 0, 0)),
+                pl.BlockSpec((1, tile, width), lambda k, *_: (k, 0, 0)),
+            ],
+            out_specs=[pl.BlockSpec((BLOCK_ROWS, 2 * width), lambda k, *_: (0, 0))] * slots,
+            scratch_shapes=[pltpu.VMEM((rows, 2 * width), jnp.float32)],
+        ),
+        out_shape=[jax.ShapeDtypeStruct((BLOCK_ROWS, 2 * width), normed.dtype)] * slots,
+        cost_estimate=pl.CostEstimate(
+            flops=4 * rows * width * tile * pieces,
+            bytes_accessed=2 * (normed.size + own.size + other.size),
+            transcendentals=0,
+        ),
+        name="value_blocks",
+    )(core, piece, block, normed, own, other)
+
+
+def pack_kernel(place, *refs):
+    out = refs[-1]
+    for o, ref in enumerate(refs[:-1]):
+
+        @pl.when(place[o] >= 0)
+        def _():
+            first = pl.multiple_of(place[o] * BLOCK_ROWS, 16)
+            out[pl.ds(first, BLOCK_ROWS), :] = ref[...]
+
+
+def pack(place, blocks, rows):
+    width = blocks[0].shape[1]
+    return pl.pallas_call(
+        pack_kernel,
+        grid_spec=pltpu.PrefetchScalarGridSpec(
+            num_scalar_prefetch=1,
+            grid=(1,),
+            in_specs=[pl.BlockSpec((BLOCK_ROWS, width), lambda k, place: (0, 0))] * len(blocks),
+            out_specs=pl.BlockSpec((rows, width), lambda k, place: (0, 0)),
+        ),
+        out_shape=jax.ShapeDtypeStruct((rows, width), blocks[0].dtype),
+        name="pack_values",
+    )(place, *blocks)
+
+
+def pick_kernel(column, in_ref, out_ref):
+    out_ref[...] = in_ref[...]
+
+
+def pick_columns(column, array, tile):
+    rows = array.shape[0]
+    steps = column.shape[0]
+    return pl.pallas_call(
+        pick_kernel,
+        grid_spec=pltpu.PrefetchScalarGridSpec(
+            num_scalar_prefetch=1,
+            grid=(steps,),
+            in_specs=[pl.BlockSpec((rows, tile), lambda z, column: (0, column[z]))],
+            out_specs=pl.BlockSpec((rows, tile), lambda z, column: (0, z)),
+        ),
+        out_shape=jax.ShapeDtypeStruct((rows, tile * steps), array.dtype),
+        name="pick_columns",
+    )(column, array)
+
+
+def turn_kernel(column, own_ref, got_ref, out_ref):
+    rows = own_ref.shape[0]
+    out_ref[:, :rows] = own_ref[...].T
+    out_ref[:, rows:] = got_ref[...].T
+
+
+def turn_columns(column, array, got, tile):
+    rows = array.shape[0]
+    steps = column.shape[0]
+    return pl.pallas_call(
+        turn_kernel,
+        grid_spec=pltpu.PrefetchScalarGridSpec(
+            num_scalar_prefetch=1,
+            grid=(steps,),
+            in_specs=[
+                pl.BlockSpec((rows, tile), lambda z, column: (0, column[z])),
+                pl.BlockSpec((rows, tile), lambda z, column: (0, z)),
+            ],
+            out_specs=pl.BlockSpec((tile, 2 * rows), lambda z, column: (z, 0)),
+        ),
+        out_shape=jax.ShapeDtypeStruct((tile * steps, 2 * rows), array.dtype),
+        name="turn_columns",
+    )(column, array, got)
+
+
+def input_grad_kernel(core, piece, grad_ref, own_ref, other_ref, out_ref):
+    own, other = halves(core[0], grad_ref, own_ref.shape[2])
+    nt = (((1,), (1,)), ((), ()))
+    total = lax.dot_general(own[...], own_ref[0], nt, preferred_element_type=jnp.float32)
+    total += lax.dot_general(other[...], other_ref[0], nt, preferred_element_type=jnp.float32)
+    out_ref[...] = total.astype(out_ref.dtype)
+
+
+def input_gradient(core, piece, value_grad, own, other):
+    rows = value_grad.shape[0]
+    pieces, tile, width = own.shape
+    return pl.pallas_call(
+        input_grad_kernel,
+        grid_spec=pltpu.PrefetchScalarGridSpec(
+            num_scalar_prefetch=2,
+            grid=(pieces,),
+            in_specs=[
+                pl.BlockSpec((rows, 2 * width), lambda k, *_: (0, 0)),
+                pl.BlockSpec((1, tile, width), lambda k, *_: (k, 0, 0)),
+                pl.BlockSpec((1, tile, width), lambda k, *_: (k, 0, 0)),
+            ],
+            out_specs=pl.BlockSpec((rows, tile), lambda k, core, piece: (0, piece[k])),
+        ),
+        out_shape=jax.ShapeDtypeStruct((rows, tile * pieces), value_grad.dtype),
+        cost_estimate=pl.CostEstimate(
+            flops=4 * rows * width * tile * pieces,
+            bytes_accessed=2 * (rows * tile * pieces + own.size + other.size),
+            transcendentals=0,
+        ),
+        name="input_gradient",
+    )(core, piece, value_grad, own, other)
 
 
 def attention_kernel(
     take, q_ref, k_ref, v_ref, grad_ref, doc_row, doc_col,
     query_grad, key_grad, value_grad, returning,
-    q_rows, k_rows, v_rows, bias, key_total, value_total,
+    q_rows, k_rows, bias, key_total, value_total,
 ):
     rows = grad_ref.shape[0]
     blocks = rows // BLOCK_ROWS
@@ -101,7 +219,6 @@
         place = slice(p * BLOCK_ROWS, (p + 1) * BLOCK_ROWS)
         q_rows[place, :] = q_ref[take[p]]
         k_rows[place, :] = k_ref[take[p]]
-        v_rows[place, :] = v_ref[take[p]]
 
     key_total[...] = jnp.zeros_like(key_total)
     value_total[...] = jnp.zeros_like(value_total)
@@ -115,7 +232,7 @@
             [grad_ref[place, x * HEAD_DIM : (x + 1) * HEAD_DIM] for x in range(GROUP)], axis=0
         )
         k = k_rows[:reach, :]
-        v = v_rows[:reach, :]
+        v = v_ref[:reach, :]
         nt = (((1,), (1,)), ((), ()))
         tn = (((0,), (0,)), ((), ()))
         scores = lax.dot_general(q, k, nt, preferred_element_type=jnp.float32) * scale
@@ -146,7 +263,7 @@
         returning[take[p]] = value_total[place, :].astype(returning.dtype)
 
 
-def attention(take, arrived, arrived_v, out_grad, doc_ids):
+def attention(take, arrived, packed_v, out_grad, doc_ids):
     peers = arrived.shape[0]
     rows = out_grad.shape[0]
     wide = GROUP * HEAD_DIM
@@ -160,7 +277,7 @@
             in_specs=[
                 pl.BlockSpec((peers, BLOCK_ROWS, wide), lambda g, take: (0, 0, g)),
                 pl.BlockSpec((peers, BLOCK_ROWS, HEAD_DIM), lambda g, take: (0, 0, first_key + g)),
-                pl.BlockSpec((peers, BLOCK_ROWS, HEAD_DIM), lambda g, take: (0, 0, g)),
+                pl.BlockSpec((rows, HEAD_DIM), lambda g, take: (0, g)),
                 pl.BlockSpec((rows, wide), lambda g, take: (0, g)),
                 pl.BlockSpec((1, rows), lambda g, take: (0, 0)),
                 pl.BlockSpec((rows, 1), lambda g, take: (0, 0)),
@@ -173,7 +290,6 @@
             ],
             scratch_shapes=[
                 pltpu.VMEM((rows, wide), bf16),
-                pltpu.VMEM((rows, HEAD_DIM), bf16),
                 pltpu.VMEM((rows, HEAD_DIM), bf16),
                 pltpu.VMEM((rows, rows), jnp.float32),
                 pltpu.VMEM((rows, HEAD_DIM), jnp.float32),
@@ -187,80 +303,133 @@
             jax.ShapeDtypeStruct((peers, BLOCK_ROWS, KV_HEADS * HEAD_DIM), bf16),
         ],
         name="attention_backward",
-    )(take, arrived, arrived, arrived_v, out_grad, doc_ids, doc_ids.reshape(rows, 1))
-
-
-def weight_kernel(send, place, normed_ref, landed_ref, out_ref, home):
+    )(take, arrived, arrived, packed_v, out_grad, doc_ids, doc_ids.reshape(rows, 1))
+
+
+def weight_kernel(send, turned_ref, landed_ref, swapped_ref, out_ref, home):
+    rows = home.shape[0] // 2
+
     @pl.when(pl.program_id(0) == 0)
     def _():
-        for b in range(home.shape[0] // BLOCK_ROWS):
-            home[b * BLOCK_ROWS : (b + 1) * BLOCK_ROWS, :] = landed_ref[send[b]]
-
-    part = lax.dot_general(
-        normed_ref[...], home[...], (((0,), (0,)), ((), ())), preferred_element_type=jnp.float32
-    )
+        for b in range(rows // BLOCK_ROWS):
+            place = slice(b * BLOCK_ROWS, (b + 1) * BLOCK_ROWS)
+            home[place, :] = landed_ref[send[0, b]]
+        for b in range(rows // BLOCK_ROWS):
+            place = slice(rows + b * BLOCK_ROWS, rows + (b + 1) * BLOCK_ROWS)
+            home[place, :] = swapped_ref[send[1, b]]
+
+    part = jnp.dot(turned_ref[...], home[...], preferred_element_type=jnp.float32)
     out_ref[...] = part.reshape(out_ref.shape).astype(out_ref.dtype)
 
 
-def weight_part(send, place, normed, landed, columns):
-    rows, depth = normed.shape
+def weight_part(send, turned, landed, swapped, columns, steps):
+    depth, rows = turned.shape
     peers, _, width = landed.shape
-    steps = place.shape[0]
-    tile = depth // peers
+    tile = depth // steps
     share = tile // columns
     return pl.pallas_call(
         weight_kernel,
         grid_spec=pltpu.PrefetchScalarGridSpec(
-            num_scalar_prefetch=2,
+            num_scalar_prefetch=1,
             grid=(steps,),
             in_specs=[
-                pl.BlockSpec((rows, tile), lambda z, send, place: (0, place[z])),
-                pl.BlockSpec((peers, BLOCK_ROWS, width), lambda z, send, place: (0, 0, 0)),
-            ],
-            out_specs=pl.BlockSpec(
-                (columns, 1, share, width), lambda z, send, place: (0, z, 0, 0)
-            ),
+                pl.BlockSpec((tile, rows), lambda z, send: (z, 0)),
+                pl.BlockSpec((peers, BLOCK_ROWS, width), lambda z, send: (0, 0, 0)),
+                pl.BlockSpec((peers, BLOCK_ROWS, width), lambda z, send: (0, 0, 0)),
+            ],
+            out_specs=pl.BlockSpec((columns, 1, share, width), lambda z, send: (0, z, 0, 0)),
             scratch_shapes=[pltpu.VMEM((rows, width), jnp.bfloat16)],
         ),
         out_shape=jax.ShapeDtypeStruct((columns, steps, share, width), jnp.bfloat16),
         name="weight_part",
-    )(send, place, normed, landed)
+    )(send, turned, landed, swapped)
+
+
+def grid_offsets(outer, inner):
+    far = [(i, j) for i in range(outer) for j in range(inner)]
+    reach = lambda o: -(min(o[0], outer - o[0]) + min(o[1], inner - o[1]))
+    return sorted(far, key=lambda o: (reach(o), o))
+
+
+def shift(index, offset, outer, inner, sign):
+    i = (index // inner + sign * offset[0]) % outer
+    j = (index % inner + sign * offset[1]) % inner
+    return i * inner + j
+
+
+def exchange(arrays, axis, offsets, outer, inner):
+    moved = []
+    for array, offset in zip(arrays, offsets):
+        if offset == (0, 0):
+            moved.append(array)
+            continue
+        pairs = [(i, shift(i, offset, outer, inner, 1)) for i in range(outer * inner)]
+        moved.append(lax.ppermute(array, axis, pairs))
+    return moved
+
+
+def near(index, offsets, outer, inner, sign):
+    steps = jnp.array(offsets, jnp.int32)
+    i = lax.rem(index // inner + sign * steps[:, 0] + outer, outer)
+    j = lax.rem(index % inner + sign * steps[:, 1] + inner, inner)
+    return i * inner + j
 
 
 def local(normed, queries, key_rows, out_grad, value_weight, doc_ids, send_to, take_from):
     dp_count = lax.axis_size("dp")
     fsdp_count = lax.axis_size("fsdp")
-    rows = normed.shape[0]
+    planes = dp_count // 2
+    side = int(fsdp_count**0.5)
+    rows, depth = normed.shape
+    blocks = rows // BLOCK_ROWS
     grad_scale = (rows * dp_count * fsdp_count) ** (-0.5)
     send, take = send_to[0], take_from[0]
-    core = lax.axis_index("dp") % 2
-
-    arrived = lax.all_to_all(
-        outgoing_slots(send, queries, key_rows, dp_count), "dp", 0, 0, tiled=True
-    )
-    weight = lax.all_gather(value_weight, "fsdp", axis=0, tiled=True)
-    arrived_v = lax.all_to_all(
-        value_slots(send, normed, weight, dp_count), "dp", 0, 0, tiled=True
-    )
+    dp, fsdp = lax.axis_index("dp"), lax.axis_index("fsdp")
+    core = dp % 2
+    core_of = core.reshape(1)
+    cores = [(i, i ^ 1) for i in range(dp_count)]
+    dp_offsets = grid_offsets(planes, 2)
+    fsdp_offsets = grid_offsets(side, side)
+    number = jnp.arange(blocks, dtype=jnp.int32)
+
+    slots = outgoing_slots(send, queries, key_rows, dp_count)
+    arrived = lax.all_to_all(slots, "dp", 0, 0, tiled=True)
+
+    width = value_weight.shape[1] // 2
+    half = lax.dynamic_slice_in_dim(value_weight, core * width, width, axis=1)
+    pieces = exchange([half] * fsdp_count, "fsdp", fsdp_offsets, side, side)
+    own = jnp.stack(pieces)
+    piece = near(fsdp, fsdp_offsets, side, side, -1)
+    other = lax.ppermute(own, "dp", cores)
+
+    target = near(dp, dp_offsets, planes, 2, 1)
+    source = near(dp, dp_offsets, planes, 2, -1)
+    block = jnp.sum(jnp.where(send[None, :] == target[:, None], number, 0), axis=1)
+    place = jnp.sum(jnp.where(take[None, :] == source[:, None], number + 1, 0), axis=1) - 1
+    leaving = value_blocks(core_of, piece, block, normed, own, other)
+    landed_v = exchange(leaving, "dp", dp_offsets, planes, 2)
+    packed_v = pack(place, landed_v, rows)
+
+    column = 2 * jnp.arange(planes, dtype=jnp.int32)
+    tile = depth // dp_count
+    got = lax.ppermute(pick_columns(column + 1 - core, normed, tile), "dp", cores)
+    turned = turn_columns(column + core, normed, got, tile)
+    partner = lax.ppermute(send_to, "dp", cores)
+    sends = jnp.concatenate([send_to, partner], axis=0)
+
     query_grad, key_grad, value_grad, returning = attention(
-        take, arrived, arrived_v, out_grad, doc_ids
+        take, arrived, packed_v, out_grad, doc_ids
     )
     landed = lax.all_to_all(returning, "dp", 0, 0, tiled=True)
-    input_grad = lax.dot_general(
-        value_grad, weight, (((1,), (1,)), ((), ())), preferred_element_type=jnp.float32
-    ).astype(jnp.bfloat16)
-
-    steps = dp_count // 2
-    pairs = 2 * jnp.arange(steps, dtype=jnp.int32)
-    theirs = weight_part(send, pairs + (1 - core), normed, landed, fsdp_count)
-    swapped = lax.ppermute(theirs, "dp", [(i, i ^ 1) for i in range(dp_count)])
-    mine = weight_part(send, pairs + core, normed, landed, fsdp_count)
-    chip = (mine.astype(jnp.float32) + swapped.astype(jnp.float32)).astype(jnp.bfloat16)
+    swapped = lax.ppermute(landed, "dp", cores)
+    input_grad = input_gradient(core_of, piece, value_grad, own, other)
+
+    chip = weight_part(sends, turned, landed, swapped, fsdp_count, planes)
     chips = lax.all_to_all(chip, "fsdp", 0, 0, tiled=True)
     plane = jnp.sum(chips.astype(jnp.float32), axis=0).astype(jnp.bfloat16)
     groups = [list(range(c, dp_count, 2)) for c in range(2)]
-    planes = lax.all_to_all(plane, "dp", 0, 0, axis_index_groups=groups, tiled=True)
-    weight_grad = jnp.sum(planes.astype(jnp.float32), axis=0) * grad_scale
+    parts = lax.all_to_all(plane, "dp", 0, 0, axis_index_groups=groups, tiled=True)
+    weight_grad = jnp.sum(parts.astype(jnp.float32), axis=0) * grad_scale
     return (query_grad, key_grad, input_grad, weight_grad)
 
 

time: 256 us -> 251 us (0.980)
  waiting for transfers between devices: 124 us -> 50.2 us
  starting transfers between devices: 22.5 us -> 79.2 us
  Pallas kernels: 44.7 us -> 71.9 us
  between operations: 14.1 us -> 1.23 us
  matrix products: 5.68 us -> 0 us
    ppermute x1 -> x34, starting transfers between devices: 2.31 us -> 64.3 us  [the longest x30 61.1 us: exchange(): moved.append(lax.ppermute(array, axis, pairs))]
    all_to_all x2 -> x1, waiting for transfers between devices: 52.8 us -> 0.01 us  [local(): arrived = lax.all_to_all(slots, 'dp', 0, 0, tiled=True)]
    all_gather x1 -> x0, waiting for transfers between devices: 47 us -> none  [local(): weight = lax.all_gather(value_weight, 'fsdp', axis=0, tiled=True)]
    ppermute x1 -> x34, waiting for transfers between devices: 0.01 us -> 36.7 us  [the longest x30 32.6 us: exchange(): moved.append(lax.ppermute(array, axis, pairs))]
    pallas_call x1 -> x5, Pallas kernels: 8.67 us -> 43 us  [the longest x1 13.5 us: value_blocks(): pl.pallas_call(values_kernel, grid_spec=pltpu.PrefetchScalarGridSpec(num_...]
    pallas_call x2 -> x1, Pallas kernels: 15.5 us -> 8.45 us  [weight_part(): pl.pallas_call(weight_kernel, grid_spec=pltpu.PrefetchScalarGridSpec(num_...]
    all_to_all x1, waiting for transfers between devices: 20.2 us -> 13.6 us  [local(): landed = lax.all_to_all(returning, 'dp', 0, 0, tiled=True)]
    dot_general x1 -> x0, matrix products: 5.68 us -> none  [local(): lax.dot_general(value_grad, weight, (((1,), (1,)), ((), ())), preferred_e...]
  transfers between devices with their start and end apart: 6 -> 37, of which waited for: 5 -> 11; matrix products, arithmetic and copies ran while one was open for 3% -> 2% of each run, Pallas kernels for 9% -> 17%
where the time goes in v2:
time: 251 us; the launch traced here: 248 us
  starting transfers between devices  79.2 us (32%)
  Pallas kernels  71.9 us (29%)
  waiting for transfers between devices  50.2 us (20%)
  blocking collectives  35.9 us (14%)
  other arithmetic  5.38 us (2%)
  local copies, waits for them, and re-layouts  3.69 us (1%)
    ppermute x30, starting transfers between devices, exchange(): moved.append(lax.ppermute(array, axis, pairs))  61.1 us
    all_to_all x1, blocking collectives, local(): chips = lax.all_to_all(chip, 'fsdp', 0, 0, tiled=True)  35.9 us
    ppermute x30, waiting for transfers between devices, exchange(): moved.append(lax.ppermute(array, axis, pairs))  32.6 us
    pallas_call x1, Pallas kernels, attention(): pl.pallas_call(attention_kernel, grid_spec=pltpu.PrefetchScalarGridSpec(n...  14.2 us
    all_to_all x1, waiting for transfers between devices, local(): landed = lax.all_to_all(returning, 'dp', 0, 0, tiled=True)  13.6 us
    pallas_call x1, Pallas kernels, value_blocks(): pl.pallas_call(values_kernel, grid_spec=pltpu.PrefetchScalarGridSpec(num_...  13.5 us
    pallas_call x1, Pallas kernels, input_gradient(): pl.pallas_call(input_grad_kernel, grid_spec=pltpu.PrefetchScalarGridSpec(...  13.1 us
    pallas_call x1, Pallas kernels, weight_part(): pl.pallas_call(weight_kernel, grid_spec=pltpu.PrefetchScalarGridSpec(num_...  8.45 us
  transfers between devices with their start and end apart: 37, of which 11 were waited for; matrix products, arithmetic and copies ran while one was open for 2% of the time, Pallas kernels for 17%

profile of v2, /device:TPU:0, one launch (start us, length us, event | category | flops | bytes accessed | tf_op | source)
XLA Modules:
  0.0 247.6 jit_solution(594791829980344176)
XLA Ops:
  0.6 6.3 %outgoing_slots.1 = bf16[16,48,2560]{2,1,0:T(8,128)(2,1)} custom-call(s32[8]{0:T(128)} %bitcast.47, bf16[384,2048]{1,0:T(8,128)(2,1)} %q_ref.1, bf16[384,512]{1,0:T(8,128)(2,1)} %k_ref.1), custom_call_target="tpu_custom_call" | custom-call | tf_op jit(solution)/shard_map/outgoing_slots/pallas_call | solution.py:27
  6.9 7.0 %all-to-all-start = ((bf16[16,48,2560]{2,1,0:T(8,128)(2,1)}), bf16[16,48,2560]{2,1,0:T(8,128)(2,1)}, u32[]{:S(2)}, u32[]{:S(2)}) async-start(bf16[16,48,2560]{2,1,0:T(8,128)(2,1)} %outgoing_slots.1), calls=%async_computation | async-start | bytes 7864320 | tf_op jit(solution)/shard_map/all_to_all | solution.py:396
  14.0 5.7 %collective-permute-start = (bf16[256,256]{1,0:T(8,128)(2,1)S(1)}, bf16[256,256]{1,0:T(8,128)(2,1)S(1)}, u32[]{:S(2)}, u32[]{:S(2)}) collective-permute-start(bf16[256,256]{1,0:T(8,128)(2,1)S(1)} %constant_dynamic-slice_fusion), channel_id=1, source_target_pairs={{0,10},{1,11},{2,8},{3,9},{4,14},{5,15},{6,12},{7,13},{8,2},{9,3},... | collective-permute-start | bytes 393224 | tf_op jit(solution)/shard_map/ppermute | solution.py:367
  20.2 3.0 %collective-permute-start.2 = (bf16[256,256]{1,0:T(8,128)(2,1)S(1)}, bf16[256,256]{1,0:T(8,128)(2,1)S(1)}, u32[]{:S(2)}, u32[]{:S(2)}) collective-permute-start(bf16[256,256]{1,0:T(8,128)(2,1)S(1)} %constant_dynamic-slice_fusion), channel_id=1, source_target_pairs={{0,9},{1,10},{2,11},{3,8},{4,13},{5,14},{6,15},{7,12},{8,1},{9,2},... | collective-permute-start | bytes 393224 | tf_op jit(solution)/shard_map/ppermute | solution.py:367
  23.2 2.6 %collective-permute-start.3 = (bf16[256,256]{1,0:T(8,128)(2,1)S(1)}, bf16[256,256]{1,0:T(8,128)(2,1)S(1)}, u32[]{:S(2)}, u32[]{:S(2)}) collective-permute-start(bf16[256,256]{1,0:T(8,128)(2,1)S(1)} %constant_dynamic-slice_fusion), channel_id=1, source_target_pairs={{0,11},{1,8},{2,9},{3,10},{4,15},{5,12},{6,13},{7,14},{8,3},{9,0},... | collective-permute-start | bytes 393224 | tf_op jit(solution)/shard_map/ppermute | solution.py:367
  25.8 4.1 %collective-permute-start.4 = (bf16[256,256]{1,0:T(8,128)(2,1)S(1)}, bf16[256,256]{1,0:T(8,128)(2,1)S(1)}, u32[]{:S(2)}, u32[]{:S(2)}) collective-permute-start(bf16[256,256]{1,0:T(8,128)(2,1)S(1)} %constant_dynamic-slice_fusion), channel_id=1, source_target_pairs={{0,14},{1,15},{2,12},{3,13},{4,2},{5,3},{6,0},{7,1},{8,6},{9,7},{1... | collective-permute-start | bytes 393224 | tf_op jit(solution)/shard_map/ppermute | solution.py:367
  29.9 1.6 collective-permute-start.5
  31.4 3.1 %collective-permute-done.1 = bf16[256,256]{1,0:T(8,128)(2,1)S(1)} collective-permute-done((bf16[256,256]{1,0:T(8,128)(2,1)S(1)}, bf16[256,256]{1,0:T(8,128)(2,1)S(1)}, u32[]{:S(2)}, u32[]{:S(2)}) %collective-permute-start.1) | collective-permute-done | bytes 131104 | tf_op jit(solution)/shard_map/ppermute | solution.py:367
  34.7 1.5 collective-permute-done.3
  36.1 5.4 %collective-permute-start.8 = (bf16[256,256]{1,0:T(8,128)(2,1)S(1)}, bf16[256,256]{1,0:T(8,128)(2,1)S(1)}, u32[]{:S(2)}, u32[]{:S(2)}) collective-permute-start(bf16[256,256]{1,0:T(8,128)(2,1)S(1)} %constant_dynamic-slice_fusion), channel_id=1, source_target_pairs={{0,8},{1,9},{2,10},{3,11},{4,12},{5,13},{6,14},{7,15},{8,0},{9,1},... | collective-permute-start | bytes 393224 | tf_op jit(solution)/shard_map/ppermute | solution.py:367
  41.7 2.8 %collective-permute-start.10 = (bf16[256,256]{1,0:T(8,128)(2,1)S(1)}, bf16[256,256]{1,0:T(8,128)(2,1)S(1)}, u32[]{:S(2)}, u32[]{:S(2)}) collective-permute-start(bf16[256,256]{1,0:T(8,128)(2,1)S(1)} %constant_dynamic-slice_fusion), channel_id=1, source_target_pairs={{0,15},{1,12},{2,13},{3,14},{4,3},{5,0},{6,1},{7,2},{8,7},{9,4},{1... | collective-permute-start | bytes 393224 | tf_op jit(solution)/shard_map/ppermute | solution.py:367
  45.1 3.3 %collective-permute-start.12 = (bf16[256,256]{1,0:T(8,128)(2,1)S(1)}, bf16[256,256]{1,0:T(8,128)(2,1)S(1)}, u32[]{:S(2)}, u32[]{:S(2)}) collective-permute-start(bf16[256,256]{1,0:T(8,128)(2,1)S(1)} %constant_dynamic-slice_fusion), channel_id=1, source_target_pairs={{0,3},{1,0},{2,1},{3,2},{4,7},{5,4},{6,5},{7,6},{8,11},{9,8},{10,9... | collective-permute-start | bytes 393224 | tf_op jit(solution)/shard_map/ppermute | solution.py:367
  48.5 1.2 collective-permute-start.13
  49.7 2.1 collective-permute-start.14
  52.0 2.7 %collective-permute-done.13 = bf16[256,256]{1,0:T(8,128)(2,1)S(1)} collective-permute-done((bf16[256,256]{1,0:T(8,128)(2,1)S(1)}, bf16[256,256]{1,0:T(8,128)(2,1)S(1)}, u32[]{:S(2)}, u32[]{:S(2)}) %collective-permute-start.13) | collective-permute-done | bytes 131104 | tf_op jit(solution)/shard_map/ppermute | solution.py:367
  55.2 0.8 select_reduce_fusion.block
  56.7 2.7 %collective-permute-done.15.other_ref = bf16[16,256,256]{2,1,0:T(8,128)(2,1)} collective-permute-done((bf16[16,256,256]{2,1,0:T(8,128)(2,1)S(1)}, bf16[16,256,256]{2,1,0:T(8,128)(2,1)}, u32[]{:S(2)}, u32[]{:S(2)}) %collective-permute-start.15) | collective-permute-done | bytes 2097184 | tf_op jit(solution)/shard_map/ppermute | solution.py:403
  59.4 13.5 %value_blocks.1 = (bf16[48,512]{1,0:T(8,128)(2,1)}, bf16[48,512]{1,0:T(8,128)(2,1)}, bf16[48,512]{1,0:T(8,128)(2,1)}, bf16[48,512]{1,0:T(8,128)(2,1)}, bf16[48,5...) custom-call(s32[1]{0:T(128)} %bitcast.3.core, ...), custom_call_target="tpu_custom_call" | custom-call | flops 1610612736 | bytes 7340032 | tf_op jit(solution)/shard_map/value_blocks/pallas_call | solution.py:76
  72.9 5.0 %collective-permute-start.16 = (bf16[48,512]{1,0:T(8,128)(2,1)}, bf16[48,512]{1,0:T(8,128)(2,1)S(1)}, u32[]{:S(2)}, u32[]{:S(2)}) collective-permute-start(bf16[48,512]{1,0:T(8,128)(2,1)} %get-tuple-element.24), channel_id=1, source_target_pairs={{0,144},{16,128},{32,176},{48,160},{64,208},{80,192},{96,240},{112... | collective-permute-start | bytes 147464 | tf_op jit(solution)/shard_map/ppermute | solution.py:367
  78.5 3.2 %collective-permute-start.18 = (bf16[48,512]{1,0:T(8,128)(2,1)}, bf16[48,512]{1,0:T(8,128)(2,1)S(1)}, u32[]{:S(2)}, u32[]{:S(2)}) collective-permute-start(bf16[48,512]{1,0:T(8,128)(2,1)} %get-tuple-element.26), channel_id=1, source_target_pairs={{0,128},{16,144},{32,160},{48,176},{64,192},{80,208},{96,224},{112... | collective-permute-start | bytes 147464 | tf_op jit(solution)/shard_map/ppermute | solution.py:367
  81.8 1.3 collective-permute-start.19
  83.1 2.5 %collective-permute-start.20 = (bf16[48,512]{1,0:T(8,128)(2,1)}, bf16[48,512]{1,0:T(8,128)(2,1)S(1)}, u32[]{:S(2)}, u32[]{:S(2)}) collective-permute-start(bf16[48,512]{1,0:T(8,128)(2,1)} %get-tuple-element.28), channel_id=1, source_target_pairs={{0,80},{16,64},{32,112},{48,96},{64,144},{80,128},{96,176},{112,16... | collective-permute-start | bytes 147464 | tf_op jit(solution)/shard_map/ppermute | solution.py:367
  85.6 20.3 %collective-permute-done.16.refs_0_ = bf16[48,512]{1,0:T(8,128)(2,1)S(1)} collective-permute-done((bf16[48,512]{1,0:T(8,128)(2,1)}, bf16[48,512]{1,0:T(8,128)(2,1)S(1)}, u32[]{:S(2)}, u32[]{:S(2)}) %collective-permute-start.16) | collective-permute-done | bytes 49184 | tf_op jit(solution)/shard_map/ppermute | solution.py:367
  105.9 2.8 %collective-permute-start.21 = (bf16[48,512]{1,0:T(8,128)(2,1)}, bf16[48,512]{1,0:T(8,128)(2,1)S(1)}, u32[]{:S(2)}, u32[]{:S(2)}) collective-permute-start(bf16[48,512]{1,0:T(8,128)(2,1)} %get-tuple-element.29), channel_id=1, source_target_pairs={{0,96},{16,112},{32,128},{48,144},{64,160},{80,176},{96,192},{112,... | collective-permute-start | bytes 147464 | tf_op jit(solution)/shard_map/ppermute | solution.py:367
  108.7 2.5 %collective-permute-start.22 = (bf16[48,512]{1,0:T(8,128)(2,1)}, bf16[48,512]{1,0:T(8,128)(2,1)S(1)}, u32[]{:S(2)}, u32[]{:S(2)}) collective-permute-start(bf16[48,512]{1,0:T(8,128)(2,1)} %get-tuple-element.30), channel_id=1, source_target_pairs={{0,160},{16,176},{32,192},{48,208},{64,224},{80,240},{96,0},{112,1... | collective-permute-start | bytes 147464 | tf_op jit(solution)/shard_map/ppermute | solution.py:367
  111.2 2.8 %collective-permute-done.18.refs_2_ = bf16[48,512]{1,0:T(8,128)(2,1)S(1)} collective-permute-done((bf16[48,512]{1,0:T(8,128)(2,1)}, bf16[48,512]{1,0:T(8,128)(2,1)S(1)}, u32[]{:S(2)}, u32[]{:S(2)}) %collective-permute-start.18) | collective-permute-done | bytes 49184 | tf_op jit(solution)/shard_map/ppermute | solution.py:367
  114.1 1.1 collective-permute-start.23
  115.9 3.6 %collective-permute-start.26 = (bf16[48,512]{1,0:T(8,128)(2,1)}, bf16[48,512]{1,0:T(8,128)(2,1)S(1)}, u32[]{:S(2)}, u32[]{:S(2)}) collective-permute-start(bf16[48,512]{1,0:T(8,128)(2,1)} %get-tuple-element.34), channel_id=1, source_target_pairs={{0,192},{16,208},{32,224},{48,240},{64,0},{80,16},{96,32},{112,48}... | collective-permute-start | bytes 147464 | tf_op jit(solution)/shard_map/ppermute | solution.py:367
  119.5 1.1 collective-permute-start.27
  120.6 1.5 collective-permute-start.28
  122.7 2.7 %collective-permute-start.30 = (bf16[48,512]{1,0:T(8,128)(2,1)}, bf16[48,512]{1,0:T(8,128)(2,1)S(1)}, u32[]{:S(2)}, u32[]{:S(2)}) collective-permute-start(bf16[48,512]{1,0:T(8,128)(2,1)} %get-tuple-element.38), channel_id=1, source_target_pairs={{0,224},{16,240},{32,0},{48,16},{64,32},{80,48},{96,64},{112,80},{... | collective-permute-start | bytes 147464 | tf_op jit(solution)/shard_map/ppermute | solution.py:367
  125.9 0.8 copy.16.doc_col
  126.8 0.9 collective-permute-done.29.refs_13_
  128.3 2.9 %pack_values.1.v_ref = bf16[384,512]{1,0:T(8,128)(2,1)} custom-call(s32[16]{0:T(128)} %broadcast_add_fusion.place, bf16[48,512]{1,0:T(8,128)(2,1)} %copy-done.5, bf16[48,512]{1,0:T(8,128)(2,1)} %copy-done.6, bf16[48,512]{1,0:T(8,128)(2,1)} %copy-done.7, bf16[48,512]{1,0:T(8,128)(2,1)} %copy-done.8, bf16[48,512]{1,0:T(8,128)(2,1)} %copy-done.9, ...), custom_call_target="tpu_custom_call" | custom-call | tf_op jit(solution)/shard_map/pack_values/pallas_call | solution.py:111
  131.2 14.2 %attention_backward.1 = (bf16[384,2048]{1,0:T(8,128)(2,1)}, bf16[384,512]{1,0:T(8,128)(2,1)}, bf16[384,512]{1,0:T(8,128)(2,1)}, bf16[16,48,512]{2,1,0:T(8,128)(2,1)}) custom-call(s32[8]{0:T(128)} %bitcast.45, bf16[16,48,2560]{2,1,0:T(8,128)(2,1)} %all-to-all-done.q_ref.k_ref, bf16[16,48,2560]{2,1,0:T(8,128)(2,1)} %all-to-all-done.q_ref.k_ref, ...), custom_call_target="tpu_custom_call" | custom-call | tf_op jit(solution)/shard_map/attention_backward/pallas_call | solution.py:272
  145.4 4.6 %all-to-all-start.1 = ((bf16[16,48,512]{2,1,0:T(8,128)(2,1)}), bf16[16,48,512]{2,1,0:T(8,128)(2,1)S(1)}, u32[]{:S(2)}, u32[]{:S(2)}) async-start(bf16[16,48,512]{2,1,0:T(8,128)(2,1)} %get-tuple-element.43), calls=%async_computation.1 | async-start | bytes 1572864 | tf_op jit(solution)/shard_map/all_to_all | solution.py:423
  150.5 6.1 %pick_columns.1 = bf16[384,2048]{1,0:T(8,128)(2,1)} custom-call(s32[8]{0:T(128)} %add_subtract_fusion.column, bf16[384,4096]{1,0:T(8,128)(2,1)} %own_ref.1), custom_call_target="tpu_custom_call" | custom-call | tf_op jit(solution)/shard_map/pick_columns/pallas_call | solution.py:131
  157.0 13.6 %all-to-all-done.1.landed_ref = bf16[16,48,512]{2,1,0:T(8,128)(2,1)S(1)} async-done(((bf16[16,48,512]{2,1,0:T(8,128)(2,1)}), bf16[16,48,512]{2,1,0:T(8,128)(2,1)S(1)}, u32[]{:S(2)}, u32[]{:S(2)}) %all-to-all-start.1) | async-done | bytes 786464 | tf_op jit(solution)/shard_map/all_to_all | solution.py:423
  170.6 2.5 %collective-permute-start.33 = (bf16[16,48,512]{2,1,0:T(8,128)(2,1)S(1)}, bf16[16,48,512]{2,1,0:T(8,128)(2,1)S(1)}, u32[]{:S(2)}, u32[]{:S(2)}) collective-permute-start(bf16[16,48,512]{2,1,0:T(8,128)(2,1)S(1)} %all-to-all-done.1.landed_ref), channel_id=1, source_target_pairs={{0,16},{16,0},{32,48},{48,32},{64,80},{80,64},{96,112},{112,96},{1... | collective-permute-start | bytes 2359304 | tf_op jit(solution)/shard_map/ppermute | solution.py:424
  173.7 1.4 collective-permute-done.31
  175.6 1.2 copy-done.2
  176.8 7.4 %turn_columns.1.turned_ref = bf16[2048,768]{1,0:T(8,128)(2,1)} custom-call(s32[8]{0:T(128)} %fusion.12.column, bf16[384,4096]{1,0:T(8,128)(2,1)} %own_ref.1, bf16[384,2048]{1,0:T(8,128)(2,1)} %copy-done.2), custom_call_target="tpu_custom_call" | custom-call | tf_op jit(solution)/shard_map/turn_columns/pallas_call | solution.py:153
  184.2 0.9 copy-done.3
  185.1 8.4 %weight_part.1 = bf16[16,8,16,512]{3,2,1,0:T(8,128)(2,1)} custom-call(s32[2,8]{1,0:T(2,128)} %pad_add_fusion.send, bf16[2048,768]{1,0:T(8,128)(2,1)} %turn_columns.1.turned_ref, bf16[16,48,512]{2,1,0:T(8,128)(2,1)} %copy-done.1, bf16[16,48,512]{2,1,0:T(8,128)(2,1)} %copy-done.3), custom_call_target="tpu_custom_call" | custom-call | tf_op jit(solution)/shard_map/weight_part/pallas_call | solution.py:330
  193.5 35.9 %all_to_all.20 = bf16[16,8,16,512]{3,2,1,0:T(8,128)(2,1)S(1)} all-to-all(bf16[16,8,16,512]{3,2,1,0:T(8,128)(2,1)} %weight_part.1), channel_id=1, replica_groups=mesh['dp'=16,'fsdp'=16] {'fsdp'}, dimensions={0} | all-to-all | bytes 4194304 | tf_op jit(solution)/shard_map/all_to_all | solution.py:428
  229.5 1.1 reduce_sum.41
  230.5 3.4 %all-to-all-start.3 = ((bf16[8,16,512]{2,1,0:T(8,128)(2,1)}), bf16[8,16,512]{2,1,0:T(8,128)(2,1)S(1)}, u32[]{:S(2)}, u32[]{:S(2)}) async-start(bf16[8,16,512]{2,1,0:T(8,128)(2,1)} %reduce_sum.41), calls=%async_computation.3 | async-start | bytes 262144 | tf_op jit(solution)/shard_map/all_to_all | solution.py:431
  233.9 13.1 %input_gradient.1 = bf16[384,4096]{1,0:T(8,128)(2,1)} custom-call(s32[1]{0:T(128)} %bitcast.3.core, s32[16]{0:T(128)} %fusion.6.piece, bf16[384,512]{1,0:T(8,128)(2,1)} %get-tuple-element.42.grad_ref, bf16[16,256,256]{2,1,0:T(8,128)(2,1)} %copy-done, bf16[16,256,256]{2,1,0:T(8,128)(2,1)} %collective-permute-done.15.other_ref), custom_call_target="tpu_custom_call" | custom-call | flops 1610612736 | bytes 7340032 | tf_op jit(solution)/shard_map/input_gradient/pallas_call | solution.py:180
  (124 shorter events, 8.1 us)
Async XLA Ops:
  6.9 124.3 %all-to-all-start = ((bf16[16,48,2560]{2,1,0:T(8,128)(2,1)}), bf16[16,48,2560]{2,1,0:T(8,128)(2,1)}, u32[]{:S(2)}, u32[]{:S(2)}) async-start(bf16[16,48,2560]{2,1,0:T(8,128)(2,1)} %outgoing_slots.1), calls=%async_computation | async-start | bytes 7864320 | tf_op jit(solution)/shard_map/all_to_all | solution.py:396
  14.0 41.2 %copy-start.27 = (s32[16,1]{0,1:T(1,128)S(1)}, s32[16,1]{0,1:T(1,128)}, u32[]{:S(2)}) copy-start(s32[16,1]{0,1:T(1,128)} %constant.103) | copy-start | bytes 196
  14.0 41.2 %copy-start.28 = (s32[16,1]{0,1:T(1,128)S(1)}, s32[16,1]{0,1:T(1,128)}, u32[]{:S(2)}) copy-start(s32[16,1]{0,1:T(1,128)} %constant.101) | copy-start | bytes 196
  14.0 41.2 %copy-start.22 = (s32[1,8]{1,0:T(1,128)S(1)}, s32[1,8]{1,0:T(1,128)}, u32[]{:S(2)}) copy-start(s32[1,8]{1,0:T(1,128)} %param.17) | copy-start | bytes 100
  14.0 42.0 %copy-start.25 = (s32[16,1]{0,1:T(1,128)S(1)}, s32[16,1]{0,1:T(1,128)}, u32[]{:S(2)}) copy-start(s32[16,1]{0,1:T(1,128)} %constant.104) | copy-start | bytes 196
  14.0 42.0 %copy-start.26 = (s32[16,1]{0,1:T(1,128)S(1)}, s32[16,1]{0,1:T(1,128)}, u32[]{:S(2)}) copy-start(s32[16,1]{0,1:T(1,128)} %constant.102) | copy-start | bytes 196
  14.0 42.0 %copy-start.23 = (s32[16,1]{0,1:T(1,128)S(1)}, s32[16,1]{0,1:T(1,128)}, u32[]{:S(2)}) copy-start(s32[16,1]{0,1:T(1,128)} %constant.108) | copy-start | bytes 196
  14.0 42.0 %copy-start.24 = (s32[16,1]{0,1:T(1,128)S(1)}, s32[16,1]{0,1:T(1,128)}, u32[]{:S(2)}) copy-start(s32[16,1]{0,1:T(1,128)} %constant.106) | copy-start | bytes 196
  14.0 15.8 %collective-permute-start = (bf16[256,256]{1,0:T(8,128)(2,1)S(1)}, bf16[256,256]{1,0:T(8,128)(2,1)S(1)}, u32[]{:S(2)}, u32[]{:S(2)}) collective-permute-start(bf16[256,256]{1,0:T(8,128)(2,1)S(1)} %constant_dynamic-slice_fusion), channel_id=1, source_target_pairs={{0,10},{1,11},{2,8},{3,9},{4,14},{5,15},{6,12},{7,13},{8,2},{9,3},... | collective-permute-start | bytes 393224 | tf_op jit(solution)/shard_map/ppermute | solution.py:367
  19.8 14.7 %collective-permute-start.1 = (bf16[256,256]{1,0:T(8,128)(2,1)S(1)}, bf16[256,256]{1,0:T(8,128)(2,1)S(1)}, u32[]{:S(2)}, u32[]{:S(2)}) collective-permute-start(bf16[256,256]{1,0:T(8,128)(2,1)S(1)} %constant_dynamic-slice_fusion), channel_id=1, source_target_pairs={{0,6},{1,7},{2,4},{3,5},{4,10},{5,11},{6,8},{7,9},{8,14},{9,15},{1... | collective-permute-start | bytes 393224 | tf_op jit(solution)/shard_map/ppermute | solution.py:367
  20.2 14.4 %collective-permute-start.2 = (bf16[256,256]{1,0:T(8,128)(2,1)S(1)}, bf16[256,256]{1,0:T(8,128)(2,1)S(1)}, u32[]{:S(2)}, u32[]{:S(2)}) collective-permute-start(bf16[256,256]{1,0:T(8,128)(2,1)S(1)} %constant_dynamic-slice_fusion), channel_id=1, source_target_pairs={{0,9},{1,10},{2,11},{3,8},{4,13},{5,14},{6,15},{7,12},{8,1},{9,2},... | collective-permute-start | bytes 393224 | tf_op jit(solution)/shard_map/ppermute | solution.py:367
  23.2 13.0 %collective-permute-start.3 = (bf16[256,256]{1,0:T(8,128)(2,1)S(1)}, bf16[256,256]{1,0:T(8,128)(2,1)S(1)}, u32[]{:S(2)}, u32[]{:S(2)}) collective-permute-start(bf16[256,256]{1,0:T(8,128)(2,1)S(1)} %constant_dynamic-slice_fusion), channel_id=1, source_target_pairs={{0,11},{1,8},{2,9},{3,10},{4,15},{5,12},{6,13},{7,14},{8,3},{9,0},... | collective-permute-start | bytes 393224 | tf_op jit(solution)/shard_map/ppermute | solution.py:367
  25.8 15.7 %collective-permute-start.4 = (bf16[256,256]{1,0:T(8,128)(2,1)S(1)}, bf16[256,256]{1,0:T(8,128)(2,1)S(1)}, u32[]{:S(2)}, u32[]{:S(2)}) collective-permute-start(bf16[256,256]{1,0:T(8,128)(2,1)S(1)} %constant_dynamic-slice_fusion), channel_id=1, source_target_pairs={{0,14},{1,15},{2,12},{3,13},{4,2},{5,3},{6,0},{7,1},{8,6},{9,7},{1... | collective-permute-start | bytes 393224 | tf_op jit(solution)/shard_map/ppermute | solution.py:367
  29.9 11.8 %collective-permute-start.5 = (bf16[256,256]{1,0:T(8,128)(2,1)S(1)}, bf16[256,256]{1,0:T(8,128)(2,1)S(1)}, u32[]{:S(2)}, u32[]{:S(2)}) collective-permute-start(bf16[256,256]{1,0:T(8,128)(2,1)S(1)} %constant_dynamic-slice_fusion), channel_id=1, source_target_pairs={{0,2},{1,3},{2,0},{3,1},{4,6},{5,7},{6,4},{7,5},{8,10},{9,11},{10,... | collective-permute-start | bytes 393224 | tf_op jit(solution)/shard_map/ppermute | solution.py:367
  34.5 10.6 %collective-permute-start.6 = (bf16[256,256]{1,0:T(8,128)(2,1)S(1)}, bf16[256,256]{1,0:T(8,128)(2,1)S(1)}, u32[]{:S(2)}, u32[]{:S(2)}) collective-permute-start(bf16[256,256]{1,0:T(8,128)(2,1)S(1)} %constant_dynamic-slice_fusion), channel_id=1, source_target_pairs={{0,5},{1,6},{2,7},{3,4},{4,9},{5,10},{6,11},{7,8},{8,13},{9,14},{1... | collective-permute-start | bytes 393224 | tf_op jit(solution)/shard_map/ppermute | solution.py:367
  34.5 10.6 %collective-permute-start.7 = (bf16[256,256]{1,0:T(8,128)(2,1)S(1)}, bf16[256,256]{1,0:T(8,128)(2,1)S(1)}, u32[]{:S(2)}, u32[]{:S(2)}) collective-permute-start(bf16[256,256]{1,0:T(8,128)(2,1)S(1)} %constant_dynamic-slice_fusion), channel_id=1, source_target_pairs={{0,7},{1,4},{2,5},{3,6},{4,11},{5,8},{6,9},{7,10},{8,15},{9,12},{1... | collective-permute-start | bytes 393224 | tf_op jit(solution)/shard_map/ppermute | solution.py:367
  36.1 12.3 %collective-permute-start.8 = (bf16[256,256]{1,0:T(8,128)(2,1)S(1)}, bf16[256,256]{1,0:T(8,128)(2,1)S(1)}, u32[]{:S(2)}, u32[]{:S(2)}) collective-permute-start(bf16[256,256]{1,0:T(8,128)(2,1)S(1)} %constant_dynamic-slice_fusion), channel_id=1, source_target_pairs={{0,8},{1,9},{2,10},{3,11},{4,12},{5,13},{6,14},{7,15},{8,0},{9,1},... | collective-permute-start | bytes 393224 | tf_op jit(solution)/shard_map/ppermute | solution.py:367
  41.6 8.2 %collective-permute-start.9 = (bf16[256,256]{1,0:T(8,128)(2,1)S(1)}, bf16[256,256]{1,0:T(8,128)(2,1)S(1)}, u32[]{:S(2)}, u32[]{:S(2)}) collective-permute-start(bf16[256,256]{1,0:T(8,128)(2,1)S(1)} %constant_dynamic-slice_fusion), channel_id=1, source_target_pairs={{0,13},{1,14},{2,15},{3,12},{4,1},{5,2},{6,3},{7,0},{8,5},{9,6},{1... | collective-permute-start | bytes 393224 | tf_op jit(solution)/shard_map/ppermute | solution.py:367
  41.7 10.2 %collective-permute-start.10 = (bf16[256,256]{1,0:T(8,128)(2,1)S(1)}, bf16[256,256]{1,0:T(8,128)(2,1)S(1)}, u32[]{:S(2)}, u32[]{:S(2)}) collective-permute-start(bf16[256,256]{1,0:T(8,128)(2,1)S(1)} %constant_dynamic-slice_fusion), channel_id=1, source_target_pairs={{0,15},{1,12},{2,13},{3,14},{4,3},{5,0},{6,1},{7,2},{8,7},{9,4},{1... | collective-permute-start | bytes 393224 | tf_op jit(solution)/shard_map/ppermute | solution.py:367
  45.1 6.8 %collective-permute-start.11 = (bf16[256,256]{1,0:T(8,128)(2,1)S(1)}, bf16[256,256]{1,0:T(8,128)(2,1)S(1)}, u32[]{:S(2)}, u32[]{:S(2)}) collective-permute-start(bf16[256,256]{1,0:T(8,128)(2,1)S(1)} %constant_dynamic-slice_fusion), channel_id=1, source_target_pairs={{0,1},{1,2},{2,3},{3,0},{4,5},{5,6},{6,7},{7,4},{8,9},{9,10},{10,1... | collective-permute-start | bytes 393224 | tf_op jit(solution)/shard_map/ppermute | solution.py:367
  45.1 6.8 %collective-permute-start.12 = (bf16[256,256]{1,0:T(8,128)(2,1)S(1)}, bf16[256,256]{1,0:T(8,128)(2,1)S(1)}, u32[]{:S(2)}, u32[]{:S(2)}) collective-permute-start(bf16[256,256]{1,0:T(8,128)(2,1)S(1)} %constant_dynamic-slice_fusion), channel_id=1, source_target_pairs={{0,3},{1,0},{2,1},{3,2},{4,7},{5,4},{6,5},{7,6},{8,11},{9,8},{10,9... | collective-permute-start | bytes 393224 | tf_op jit(solution)/shard_map/ppermute | solution.py:367
  48.5 6.3 %collective-permute-start.13 = (bf16[256,256]{1,0:T(8,128)(2,1)S(1)}, bf16[256,256]{1,0:T(8,128)(2,1)S(1)}, u32[]{:S(2)}, u32[]{:S(2)}) collective-permute-start(bf16[256,256]{1,0:T(8,128)(2,1)S(1)} %constant_dynamic-slice_fusion), channel_id=1, source_target_pairs={{0,4},{1,5},{2,6},{3,7},{4,8},{5,9},{6,10},{7,11},{8,12},{9,13},{1... | collective-permute-start | bytes 393224 | tf_op jit(solution)/shard_map/ppermute | solution.py:367
  49.7 5.0 %collective-permute-start.14 = (bf16[256,256]{1,0:T(8,128)(2,1)S(1)}, bf16[256,256]{1,0:T(8,128)(2,1)S(1)}, u32[]{:S(2)}, u32[]{:S(2)}) collective-permute-start(bf16[256,256]{1,0:T(8,128)(2,1)S(1)} %constant_dynamic-slice_fusion), channel_id=1, source_target_pairs={{0,12},{1,13},{2,14},{3,15},{4,0},{5,1},{6,2},{7,3},{8,4},{9,5},{1... | collective-permute-start | bytes 393224 | tf_op jit(solution)/shard_map/ppermute | solution.py:367
  54.8 4.6 %collective-permute-start.15 = (bf16[16,256,256]{2,1,0:T(8,128)(2,1)S(1)}, bf16[16,256,256]{2,1,0:T(8,128)(2,1)}, u32[]{:S(2)}, u32[]{:S(2)}) collective-permute-start(bf16[16,256,256]{2,1,0:T(8,128)(2,1)S(1)} %bitcast_dynamic-update-slice_fusion.own_ref), channel_id=1, source_target_pairs={{0,16},{16,0},{32,48},{48,32},{64,80},{80,64},{96,112},{112,96},{1... | collective-permute-start | bytes 6291464 | tf_op jit(solution)/shard_map/ppermute | solution.py:403
  59.4 56.4 %copy-start.21 = (s32[1,8]{1,0:T(1,128)S(1)}, s32[1,8]{1,0:T(1,128)}, u32[]{:S(2)}) copy-start(s32[1,8]{1,0:T(1,128)} %param.18) | copy-start | bytes 100
  59.4 66.5 %copy-start.20 = (s32[1,384]{1,0:T(1,128)S(1)}, s32[1,384]{1,0:T(1,128)}, u32[]{:S(2)}) copy-start(s32[1,384]{1,0:T(1,128)} %doc_row.1) | copy-start | bytes 4612
  72.9 33.0 %collective-permute-start.16 = (bf16[48,512]{1,0:T(8,128)(2,1)}, bf16[48,512]{1,0:T(8,128)(2,1)S(1)}, u32[]{:S(2)}, u32[]{:S(2)}) collective-permute-start(bf16[48,512]{1,0:T(8,128)(2,1)} %get-tuple-element.24), channel_id=1, source_target_pairs={{0,144},{16,128},{32,176},{48,160},{64,208},{80,192},{96,240},{112... | collective-permute-start | bytes 147464 | tf_op jit(solution)/shard_map/ppermute | solution.py:367
  78.0 30.7 %collective-permute-start.17 = (bf16[48,512]{1,0:T(8,128)(2,1)}, bf16[48,512]{1,0:T(8,128)(2,1)S(1)}, u32[]{:S(2)}, u32[]{:S(2)}) collective-permute-start(bf16[48,512]{1,0:T(8,128)(2,1)} %get-tuple-element.25), channel_id=1, source_target_pairs={{0,112},{16,96},{32,144},{48,128},{64,176},{80,160},{96,208},{112,... | collective-permute-start | bytes 147464 | tf_op jit(solution)/shard_map/ppermute | solution.py:367
  78.5 35.5 %collective-permute-start.18 = (bf16[48,512]{1,0:T(8,128)(2,1)}, bf16[48,512]{1,0:T(8,128)(2,1)S(1)}, u32[]{:S(2)}, u32[]{:S(2)}) collective-permute-start(bf16[48,512]{1,0:T(8,128)(2,1)} %get-tuple-element.26), channel_id=1, source_target_pairs={{0,128},{16,144},{32,160},{48,176},{64,192},{80,208},{96,224},{112... | collective-permute-start | bytes 147464 | tf_op jit(solution)/shard_map/ppermute | solution.py:367
  81.8 33.3 %collective-permute-start.19 = (bf16[48,512]{1,0:T(8,128)(2,1)}, bf16[48,512]{1,0:T(8,128)(2,1)S(1)}, u32[]{:S(2)}, u32[]{:S(2)}) collective-permute-start(bf16[48,512]{1,0:T(8,128)(2,1)} %get-tuple-element.27), channel_id=1, source_target_pairs={{0,176},{16,160},{32,208},{48,192},{64,240},{80,224},{96,16},{112,... | collective-permute-start | bytes 147464 | tf_op jit(solution)/shard_map/ppermute | solution.py:367
  83.1 32.0 %collective-permute-start.20 = (bf16[48,512]{1,0:T(8,128)(2,1)}, bf16[48,512]{1,0:T(8,128)(2,1)S(1)}, u32[]{:S(2)}, u32[]{:S(2)}) collective-permute-start(bf16[48,512]{1,0:T(8,128)(2,1)} %get-tuple-element.28), channel_id=1, source_target_pairs={{0,80},{16,64},{32,112},{48,96},{64,144},{80,128},{96,176},{112,16... | collective-permute-start | bytes 147464 | tf_op jit(solution)/shard_map/ppermute | solution.py:367
  105.9 21.7 %copy-start.5 = (bf16[48,512]{1,0:T(8,128)(2,1)}, bf16[48,512]{1,0:T(8,128)(2,1)S(1)}, u32[]{:S(2)}) copy-start(bf16[48,512]{1,0:T(8,128)(2,1)S(1)} %collective-permute-done.16.refs_0_) | copy-start | bytes 147460
  105.9 10.0 %collective-permute-start.21 = (bf16[48,512]{1,0:T(8,128)(2,1)}, bf16[48,512]{1,0:T(8,128)(2,1)S(1)}, u32[]{:S(2)}, u32[]{:S(2)}) collective-permute-start(bf16[48,512]{1,0:T(8,128)(2,1)} %get-tuple-element.29), channel_id=1, source_target_pairs={{0,96},{16,112},{32,128},{48,144},{64,160},{80,176},{96,192},{112,... | collective-permute-start | bytes 147464 | tf_op jit(solution)/shard_map/ppermute | solution.py:367
  108.7 19.0 %copy-start.6 = (bf16[48,512]{1,0:T(8,128)(2,1)}, bf16[48,512]{1,0:T(8,128)(2,1)S(1)}, u32[]{:S(2)}) copy-start(bf16[48,512]{1,0:T(8,128)(2,1)S(1)} %collective-permute-done.17.refs_1_) | copy-start | bytes 147460
  108.7 10.8 %collective-permute-start.22 = (bf16[48,512]{1,0:T(8,128)(2,1)}, bf16[48,512]{1,0:T(8,128)(2,1)S(1)}, u32[]{:S(2)}, u32[]{:S(2)}) collective-permute-start(bf16[48,512]{1,0:T(8,128)(2,1)} %get-tuple-element.30), channel_id=1, source_target_pairs={{0,160},{16,176},{32,192},{48,208},{64,224},{80,240},{96,0},{112,1... | collective-permute-start | bytes 147464 | tf_op jit(solution)/shard_map/ppermute | solution.py:367
  114.1 6.6 %collective-permute-start.23 = (bf16[48,512]{1,0:T(8,128)(2,1)}, bf16[48,512]{1,0:T(8,128)(2,1)S(1)}, u32[]{:S(2)}, u32[]{:S(2)}) collective-permute-start(bf16[48,512]{1,0:T(8,128)(2,1)} %get-tuple-element.31), channel_id=1, source_target_pairs={{0,208},{16,192},{32,240},{48,224},{64,16},{80,0},{96,48},{112,32}... | collective-permute-start | bytes 147464 | tf_op jit(solution)/shard_map/ppermute | solution.py:367
  115.1 7.0 %collective-permute-start.24 = (bf16[48,512]{1,0:T(8,128)(2,1)}, bf16[48,512]{1,0:T(8,128)(2,1)S(1)}, u32[]{:S(2)}, u32[]{:S(2)}) collective-permute-start(bf16[48,512]{1,0:T(8,128)(2,1)} %get-tuple-element.32), channel_id=1, source_target_pairs={{0,48},{16,32},{32,80},{48,64},{64,112},{80,96},{96,144},{112,128}... | collective-permute-start | bytes 147464 | tf_op jit(solution)/shard_map/ppermute | solution.py:367
  115.2 7.5 %collective-permute-start.25 = (bf16[48,512]{1,0:T(8,128)(2,1)}, bf16[48,512]{1,0:T(8,128)(2,1)S(1)}, u32[]{:S(2)}, u32[]{:S(2)}) collective-permute-start(bf16[48,512]{1,0:T(8,128)(2,1)} %get-tuple-element.33), channel_id=1, source_target_pairs={{0,64},{16,80},{32,96},{48,112},{64,128},{80,144},{96,160},{112,17... | collective-permute-start | bytes 147464 | tf_op jit(solution)/shard_map/ppermute | solution.py:367
  115.9 10.8 %collective-permute-start.26 = (bf16[48,512]{1,0:T(8,128)(2,1)}, bf16[48,512]{1,0:T(8,128)(2,1)S(1)}, u32[]{:S(2)}, u32[]{:S(2)}) collective-permute-start(bf16[48,512]{1,0:T(8,128)(2,1)} %get-tuple-element.34), channel_id=1, source_target_pairs={{0,192},{16,208},{32,224},{48,240},{64,0},{80,16},{96,32},{112,48}... | collective-permute-start | bytes 147464 | tf_op jit(solution)/shard_map/ppermute | solution.py:367
  119.5 7.2 %collective-permute-start.27 = (bf16[48,512]{1,0:T(8,128)(2,1)}, bf16[48,512]{1,0:T(8,128)(2,1)S(1)}, u32[]{:S(2)}, u32[]{:S(2)}) collective-permute-start(bf16[48,512]{1,0:T(8,128)(2,1)} %get-tuple-element.35), channel_id=1, source_target_pairs={{0,240},{16,224},{32,16},{48,0},{64,48},{80,32},{96,80},{112,64},{... | collective-permute-start | bytes 147464 | tf_op jit(solution)/shard_map/ppermute | solution.py:367
  120.6 6.1 %collective-permute-start.28 = (bf16[48,512]{1,0:T(8,128)(2,1)}, bf16[48,512]{1,0:T(8,128)(2,1)S(1)}, u32[]{:S(2)}, u32[]{:S(2)}) collective-permute-start(bf16[48,512]{1,0:T(8,128)(2,1)} %get-tuple-element.36), channel_id=1, source_target_pairs={{0,16},{16,0},{32,48},{48,32},{64,80},{80,64},{96,112},{112,96},{1... | collective-permute-start | bytes 147464 | tf_op jit(solution)/shard_map/ppermute | solution.py:367
  122.1 5.5 %collective-permute-start.29 = (bf16[48,512]{1,0:T(8,128)(2,1)}, bf16[48,512]{1,0:T(8,128)(2,1)S(1)}, u32[]{:S(2)}, u32[]{:S(2)}) collective-permute-start(bf16[48,512]{1,0:T(8,128)(2,1)} %get-tuple-element.37), channel_id=1, source_target_pairs={{0,32},{16,48},{32,64},{48,80},{64,96},{80,112},{96,128},{112,144}... | collective-permute-start | bytes 147464 | tf_op jit(solution)/shard_map/ppermute | solution.py:367
  122.7 5.0 %collective-permute-start.30 = (bf16[48,512]{1,0:T(8,128)(2,1)}, bf16[48,512]{1,0:T(8,128)(2,1)S(1)}, u32[]{:S(2)}, u32[]{:S(2)}) collective-permute-start(bf16[48,512]{1,0:T(8,128)(2,1)} %get-tuple-element.38), channel_id=1, source_target_pairs={{0,224},{16,240},{32,0},{48,16},{64,32},{80,48},{96,64},{112,80},{... | collective-permute-start | bytes 147464 | tf_op jit(solution)/shard_map/ppermute | solution.py:367
  145.4 25.2 %all-to-all-start.1 = ((bf16[16,48,512]{2,1,0:T(8,128)(2,1)}), bf16[16,48,512]{2,1,0:T(8,128)(2,1)S(1)}, u32[]{:S(2)}, u32[]{:S(2)}) async-start(bf16[16,48,512]{2,1,0:T(8,128)(2,1)} %get-tuple-element.43), calls=%async_computation.1 | async-start | bytes 1572864 | tf_op jit(solution)/shard_map/all_to_all | solution.py:423
  156.6 19.0 %collective-permute-start.32 = (bf16[384,2048]{1,0:T(8,128)(2,1)}, bf16[384,2048]{1,0:T(8,128)(2,1)S(1)}, u32[]{:S(2)}, u32[]{:S(2)}) collective-permute-start(bf16[384,2048]{1,0:T(8,128)(2,1)} %pick_columns.1), channel_id=1, source_target_pairs={{0,16},{16,0},{32,48},{48,32},{64,80},{80,64},{96,112},{112,96},{1... | collective-permute-start | bytes 4718600 | tf_op jit(solution)/shard_map/ppermute | solution.py:415
  170.6 13.6 %collective-permute-start.33 = (bf16[16,48,512]{2,1,0:T(8,128)(2,1)S(1)}, bf16[16,48,512]{2,1,0:T(8,128)(2,1)S(1)}, u32[]{:S(2)}, u32[]{:S(2)}) collective-permute-start(bf16[16,48,512]{2,1,0:T(8,128)(2,1)S(1)} %all-to-all-done.1.landed_ref), channel_id=1, source_target_pairs={{0,16},{16,0},{32,48},{48,32},{64,80},{80,64},{96,112},{112,96},{1... | collective-permute-start | bytes 2359304 | tf_op jit(solution)/shard_map/ppermute | solution.py:424
  173.1 1.9 collective-permute-start.31
  230.5 16.4 %all-to-all-start.3 = ((bf16[8,16,512]{2,1,0:T(8,128)(2,1)}), bf16[8,16,512]{2,1,0:T(8,128)(2,1)S(1)}, u32[]{:S(2)}, u32[]{:S(2)}) async-start(bf16[8,16,512]{2,1,0:T(8,128)(2,1)} %reduce_sum.41), calls=%async_computation.3 | async-start | bytes 262144 | tf_op jit(solution)/shard_map/all_to_all | solution.py:431
  (18 other events, 108.1 us)

commit v3 on v1

v3 whole, which is shorter than its diff:
```python
import functools

import jax
import jax.numpy as jnp
from jax import lax
from jax.experimental import pallas as pl
from jax.experimental.pallas import tpu as pltpu
from jax.sharding import PartitionSpec as P


HEADS = 16
KV_HEADS = 4
HEAD_DIM = 128
GROUP = HEADS // KV_HEADS
BLOCK_ROWS = 48
QUERY_TILE = 128


def outgoing_kernel(send, q_ref, k_ref, out_ref):
    width = q_ref.shape[1]
    out_ref[0, :, :width] = q_ref[...]
    out_ref[0, :, width:] = k_ref[...]


def outgoing_slots(send, queries, key_rows, peers):
    rows, width = queries.shape
    key_width = key_rows.shape[1]
    blocks = rows // BLOCK_ROWS
    return pl.pallas_call(
        outgoing_kernel,
        grid_spec=pltpu.PrefetchScalarGridSpec(
            num_scalar_prefetch=1,
            grid=(blocks,),
            in_specs=[
                pl.BlockSpec((BLOCK_ROWS, width), lambda b, send: (b, 0)),
                pl.BlockSpec((BLOCK_ROWS, key_width), lambda b, send: (b, 0)),
            ],
            out_specs=pl.BlockSpec(
                (1, BLOCK_ROWS, width + key_width), lambda b, send: (send[b], 0, 0)
            ),
        ),
        out_shape=jax.ShapeDtypeStruct((peers, BLOCK_ROWS, width + key_width), queries.dtype),
        name="outgoing_slots",
    )(send, queries, key_rows)


def halves(core, ref, width):
    own = ref.at[:, pl.ds(pl.multiple_of(core * width, width), width)]
    other = ref.at[:, pl.ds(pl.multiple_of((1 - core) * width, width), width)]
    return own, other


def values_kernel(core, block, normed_ref, own_ref, other_ref, *rest):
    outs, total = rest[:-1], rest[-1]
    step = pl.program_id(0)
    own, other = halves(core[0], total, own_ref.shape[1])

    @pl.when(step == 0)
    def _():
        total[...] = jnp.zeros_like(total)

    rows = normed_ref[...]
    own[...] += jnp.dot(rows, own_ref[...], preferred_element_type=jnp.float32)
    other[...] += jnp.dot(rows, other_ref[...], preferred_element_type=jnp.float32)

    @pl.when(step == pl.num_programs(0) - 1)
    def _():
        for o, out in enumerate(outs):
            for c in range(out.shape[0]):
                first = pl.multiple_of(block[2 * o + c] * BLOCK_ROWS, 16)
                out[c] = total[pl.ds(first, BLOCK_ROWS), :].astype(out.dtype)


def value_blocks(core, block, normed, own, other):
    rows, depth = normed.shape
    width = own.shape[1]
    slots = block.shape[0] // 2
    tile = depth // 4
    shape = (2, BLOCK_ROWS, 2 * width)
    return pl.pallas_call(
        values_kernel,
        grid_spec=pltpu.PrefetchScalarGridSpec(
            num_scalar_prefetch=2,
            grid=(depth // tile,),
            in_specs=[
                pl.BlockSpec((rows, tile), lambda k, *_: (0, k)),
                pl.BlockSpec((tile, width), lambda k, *_: (k, 0)),
                pl.BlockSpec((tile, width), lambda k, *_: (k, 0)),
            ],
            out_specs=[pl.BlockSpec(shape, lambda k, *_: (0, 0, 0))] * slots,
            scratch_shapes=[pltpu.VMEM((rows, 2 * width), jnp.float32)],
        ),
        out_shape=[jax.ShapeDtypeStruct(shape, normed.dtype)] * slots,
        cost_estimate=pl.CostEstimate(
            flops=4 * rows * width * depth,
            bytes_accessed=2 * (normed.size + own.size + other.size),
            transcendentals=0,
        ),
        name="value_blocks",
    )(core, block, normed, own, other)


def pack_kernel(core, place, *refs):
    *own, swapped, out = refs
    sources = [ref.at[core[0]] for ref in own]
    sources += [swapped.at[o, core[0]] for o in range(swapped.shape[0])]
    for o, ref in enumerate(sources):

        @pl.when(place[o] >= 0)
        def _():
            first = pl.multiple_of(place[o] * BLOCK_ROWS, 16)
            out[pl.ds(first, BLOCK_ROWS), :] = ref[...]


def pack(core, place, own, swapped, rows):
    width = swapped.shape[3]
    shape = (2, BLOCK_ROWS, width)
    return pl.pallas_call(
        pack_kernel,
        grid_spec=pltpu.PrefetchScalarGridSpec(
            num_scalar_prefetch=2,
            grid=(1,),
            in_specs=[pl.BlockSpec(shape, lambda k, *_: (0, 0, 0))] * len(own)
            + [pl.BlockSpec((len(own),) + shape, lambda k, *_: (0, 0, 0, 0))],
            out_specs=pl.BlockSpec((rows, width), lambda k, *_: (0, 0)),
        ),
        out_shape=jax.ShapeDtypeStruct((rows, width), swapped.dtype),
    )(core, place, *own, swapped)


def turn_kernel(column, line, in_ref, *rest):
    outs, turned = rest[:-1], rest[-1]
    turned[...] = in_ref[...].T.reshape(turned.shape)
    for o, out in enumerate(outs):
        out[...] = turned[line[o]]


def turn_columns(column, line, array, tile):
    rows = array.shape[0]
    steps, lines = column.shape[0], line.shape[0]
    share = tile // lines
    return pl.pallas_call(
        turn_kernel,
        grid_spec=pltpu.PrefetchScalarGridSpec(
            num_scalar_prefetch=2,
            grid=(steps,),
            in_specs=[pl.BlockSpec((rows, tile), lambda z, column, line: (0, column[z]))],
            out_specs=[pl.BlockSpec((share, rows), lambda z, column, line: (z, 0))] * lines,
            scratch_shapes=[pltpu.VMEM((lines, share, rows), array.dtype)],
        ),
        out_shape=[jax.ShapeDtypeStruct((share * steps, rows), array.dtype)] * lines,
        name="turn_columns",
    )(column, line, array)


def input_grad_kernel(core, grad_ref, own_ref, other_ref, out_ref):
    own, other = halves(core[0], grad_ref, own_ref.shape[1])
    nt = (((1,), (1,)), ((), ()))
    total = lax.dot_general(own[...], own_ref[...], nt, preferred_element_type=jnp.float32)
    total += lax.dot_general(other[...], other_ref[...], nt, preferred_element_type=jnp.float32)
    out_ref[...] = total.astype(out_ref.dtype)


def input_gradient(core, value_grad, own, other):
    rows = value_grad.shape[0]
    depth, width = own.shape
    tile = depth // 8
    return pl.pallas_call(
        input_grad_kernel,
        grid_spec=pltpu.PrefetchScalarGridSpec(
            num_scalar_prefetch=1,
            grid=(depth // tile,),
            in_specs=[
                pl.BlockSpec((rows, 2 * width), lambda k, *_: (0, 0)),
                pl.BlockSpec((tile, width), lambda k, *_: (k, 0)),
                pl.BlockSpec((tile, width), lambda k, *_: (k, 0)),
            ],
            out_specs=pl.BlockSpec((rows, tile), lambda k, *_: (0, k)),
        ),
        out_shape=jax.ShapeDtypeStruct((rows, depth), value_grad.dtype),
        cost_estimate=pl.CostEstimate(
            flops=4 * rows * width * depth,
            bytes_accessed=2 * (rows * depth + own.size + other.size),
            transcendentals=0,
        ),
        name="input_gradient",
    )(core, value_grad, own, other)


def attention_kernel(
    take, back_block, q_ref, k_ref, v_ref, grad_ref, doc_row, doc_col,
    query_grad, key_grad, value_grad, *rest,
):
    returning = rest[:-5]
    q_rows, k_rows, bias, key_total, value_total = rest[-5:]
    rows = grad_ref.shape[0]
    blocks = rows // BLOCK_ROWS
    scale = HEAD_DIM ** (-0.5)

    @pl.when(pl.program_id(0) == 0)
    def _():
        i = lax.broadcasted_iota(jnp.int32, (rows, rows), 0)
        j = lax.broadcasted_iota(jnp.int32, (rows, rows), 1)
        allowed = (doc_col[...] == doc_row[...]) & (j <= i)
        bias[...] = jnp.where(allowed, 0.0, -jnp.inf)

    for p in range(blocks):
        place = slice(p * BLOCK_ROWS, (p + 1) * BLOCK_ROWS)
        q_rows[place, :] = q_ref[take[p]]
        k_rows[place, :] = k_ref[take[p]]

    key_total[...] = jnp.zeros_like(key_total)
    value_total[...] = jnp.zeros_like(value_total)
    for start in range(0, rows, QUERY_TILE):
        place = slice(start, start + QUERY_TILE)
        reach = start + QUERY_TILE
        q = jnp.concatenate(
            [q_rows[place, x * HEAD_DIM : (x + 1) * HEAD_DIM] for x in range(GROUP)], axis=0
        )
        g = jnp.concatenate(
            [grad_ref[place, x * HEAD_DIM : (x + 1) * HEAD_DIM] for x in range(GROUP)], axis=0
        )
        k = k_rows[:reach, :]
        v = v_ref[:reach, :]
        nt = (((1,), (1,)), ((), ()))
        tn = (((0,), (0,)), ((), ()))
        scores = lax.dot_general(q, k, nt, preferred_element_type=jnp.float32) * scale
        hide = bias[place, :reach]
        scores = scores + jnp.concatenate([hide] * GROUP, axis=0)
        peak = jnp.max(scores, axis=-1, keepdims=True)
        exponent = jnp.exp(scores - peak)
        probs = exponent / jnp.sum(exponent, axis=-1, keepdims=True)
        half = probs.astype(jnp.bfloat16)
        attn = jnp.dot(half, v, preferred_element_type=jnp.float32)
        delta = jnp.sum(g.astype(jnp.float32) * attn, axis=-1, keepdims=True)
        prob_grad = lax.dot_general(g, v, nt, preferred_element_type=jnp.float32)
        score_grad = (probs * (prob_grad - delta) * scale).astype(jnp.bfloat16)
        back = jnp.dot(score_grad, k, preferred_element_type=jnp.float32)
        for x in range(GROUP):
            query_grad[place, x * HEAD_DIM : (x + 1) * HEAD_DIM] = back[
                x * QUERY_TILE : (x + 1) * QUERY_TILE
            ].astype(query_grad.dtype)
        key_total[:reach, :] += lax.dot_general(
            score_grad, q, tn, preferred_element_type=jnp.float32
        )
        value_total[:reach, :] += lax.dot_general(half, g, tn, preferred_element_type=jnp.float32)
    key_grad[...] = key_total[...].astype(key_grad.dtype)
    value_grad[...] = value_total[...].astype(value_grad.dtype)
    for o, out in enumerate(returning):
        for c in range(out.shape[0]):
            first = pl.multiple_of(back_block[2 * o + c] * BLOCK_ROWS, 16)
            out[c] = value_total[pl.ds(first, BLOCK_ROWS), :].astype(out.dtype)


def attention(take, back_block, arrived, packed_v, out_grad, doc_ids):
    peers = arrived.shape[0]
    rows = out_grad.shape[0]
    wide = GROUP * HEAD_DIM
    first_key = HEADS
    bf16 = jnp.bfloat16
    return pl.pallas_call(
        attention_kernel,
        grid_spec=pltpu.PrefetchScalarGridSpec(
            num_scalar_prefetch=2,
            grid=(KV_HEADS,),
            in_specs=[
                pl.BlockSpec((peers, BLOCK_ROWS, wide), lambda g, *_: (0, 0, g)),
                pl.BlockSpec((peers, BLOCK_ROWS, HEAD_DIM), lambda g, *_: (0, 0, first_key + g)),
                pl.BlockSpec((rows, HEAD_DIM), lambda g, *_: (0, g)),
                pl.BlockSpec((rows, wide), lambda g, *_: (0, g)),
                pl.BlockSpec((1, rows), lambda g, *_: (0, 0)),
                pl.BlockSpec((rows, 1), lambda g, *_: (0, 0)),
            ],
            out_specs=[
                pl.BlockSpec((rows, wide), lambda g, *_: (0, g)),
                pl.BlockSpec((rows, HEAD_DIM), lambda g, *_: (0, g)),
                pl.BlockSpec((rows, HEAD_DIM), lambda g, *_: (0, g)),
            ]
            + [pl.BlockSpec((2, BLOCK_ROWS, HEAD_DIM), lambda g, *_: (0, 0, g))] * (peers // 2),
            scratch_shapes=[
                pltpu.VMEM((rows, wide), bf16),
                pltpu.VMEM((rows, HEAD_DIM), bf16),
                pltpu.VMEM((rows, rows), jnp.float32),
                pltpu.VMEM((rows, HEAD_DIM), jnp.float32),
                pltpu.VMEM((rows, HEAD_DIM), jnp.float32),
            ],
        ),
        out_shape=[
            jax.ShapeDtypeStruct((rows, KV_HEADS * wide), bf16),
            jax.ShapeDtypeStruct((rows, KV_HEADS * HEAD_DIM), bf16),
            jax.ShapeDtypeStruct((rows, KV_HEADS * HEAD_DIM), bf16),
        ]
        + [jax.ShapeDtypeStruct((2, BLOCK_ROWS, KV_HEADS * HEAD_DIM), bf16)] * (peers // 2),
        name="attention_backward",
    )(take, back_block, arrived, arrived, packed_v, out_grad, doc_ids, doc_ids.reshape(rows, 1))


def weight_kernel(loads, line, *refs):
    pieces = len(loads)
    own = pieces // 2
    sources = refs[: own + 1 + sum(loads)]
    stay, *leave = refs[len(sources) : -4]
    left, right, total, sems = refs[-4:]
    depth, rows = left.shape[1:]
    at = own + 1
    for i, parts in enumerate(loads):
        part = sources[min(i, own)].at[pl.ds(max(i - own, 0) * depth, depth)]
        pltpu.make_async_copy(part, left.at[i], sems.at[i, 0]).start()
        for j in range(parts):
            place = pl.ds(j * (rows // parts), rows // parts)
            pltpu.make_async_copy(sources[at], right.at[i, place], sems.at[i, 1]).start()
            at += 1
    total[...] = jnp.zeros_like(total)

    def add(i, _):
        pltpu.make_async_copy(left.at[i], left.at[i], sems.at[i, 0]).wait()
        pltpu.make_async_copy(right.at[i], right.at[i], sems.at[i, 1]).wait()
        part = jnp.dot(left[i], right[i], preferred_element_type=jnp.float32)
        total[...] += part.reshape(total.shape)
        return 0

    lax.fori_loop(0, pieces, add, 0)
    stay[...] = total[:, line[0]]
    for o, out in enumerate(leave):
        out[...] = total[:, line[o + 1]].astype(out.dtype)


def weight_part(line, turned, homes, steps):
    rows = turned[0].shape[1]
    depth = turned[0].shape[0] // 2
    width = homes[0][0].shape[1]
    pieces, lines = len(homes), line.shape[0]
    share = depth // steps // lines
    shape = (steps, share, width)
    loads = tuple(len(parts) for parts in homes)
    flat = [part for parts in homes for part in parts]
    bf16 = jnp.bfloat16
    return pl.pallas_call(
        functools.partial(weight_kernel, loads),
        grid_spec=pltpu.PrefetchScalarGridSpec(
            num_scalar_prefetch=1,
            grid=(1,),
            in_specs=[pl.BlockSpec(memory_space=pl.ANY)] * (len(turned) + len(flat)),
            out_specs=[pl.BlockSpec(shape, lambda k, line: (0, 0, 0))] * lines,
            scratch_shapes=[
                pltpu.VMEM((pieces, depth, rows), bf16),
                pltpu.VMEM((pieces, rows, width), bf16),
                pltpu.VMEM((steps, lines, share, width), jnp.float32),
                pltpu.SemaphoreType.DMA((pieces, 2)),
            ],
        ),
        out_shape=[jax.ShapeDtypeStruct(shape, jnp.float32)]
        + [jax.ShapeDtypeStruct(shape, bf16)] * (lines - 1),
        name="weight_part",
    )(line, *turned, *flat)


def ring(count, step, stride=1):
    size = count[1]
    return [
        (i, i + ((i // stride % size + step) % size - i // stride % size) * stride)
        for i in range(count[0])
    ]


def far_first(count):
    return sorted(range(count), key=lambda d: -min(d, count - d))


def gather_ring(array, at, size, shift):
    cut = array.shape[0] // 2
    before, after = shift(array, 1), shift(array, -1)
    top, low = shift(before[:cut], 1), shift(after[cut:], -1)
    out = jnp.zeros((size,) + array.shape, array.dtype)
    none = (0,) * (array.ndim - 1)
    for step, row, piece in ((0, 0, array), (1, 0, before), (2, 0, top), (2, cut, low), (3, 0, after)):
        out = lax.dynamic_update_slice(out, piece[None], ((at + size - step) % size, row) + none)
    return out


def local(normed, queries, key_rows, out_grad, value_weight, doc_ids, send_to, take_from):
    dp_count = lax.axis_size("dp")
    fsdp_count = lax.axis_size("fsdp")
    planes = dp_count // 2
    side = int(fsdp_count**0.5)
    rows, depth = normed.shape
    blocks = rows // BLOCK_ROWS
    grad_scale = (rows * dp_count * fsdp_count) ** (-0.5)
    send, take = send_to[0], take_from[0]
    dp, fsdp = lax.axis_index("dp"), lax.axis_index("fsdp")
    core, plane_at = dp % 2, dp // 2
    core_of = core.reshape(1)
    cores = [(i, i ^ 1) for i in range(dp_count)]
    hops = far_first(planes)
    number = jnp.arange(blocks, dtype=jnp.int32)
    hop_steps = jnp.array(hops, jnp.int32)
    pair = jnp.arange(2, dtype=jnp.int32)

    def along_z(arrays):
        return [
            a if d == 0 else lax.ppermute(a, "dp", ring((dp_count, planes), d, 2))
            for a, d in zip(arrays, hops)
        ]

    def swap(arrays):
        return [lax.ppermute(a, "dp", cores) for a in arrays]

    def along_x(array, step):
        return lax.ppermute(array, "fsdp", ring((fsdp_count, side), step, side))

    def along_y(array, step):
        return lax.ppermute(array, "fsdp", ring((fsdp_count, side), step, 1))

    def which(table, devices):
        return jnp.sum(jnp.where(table[None, :] == devices[:, None], number + 1, 0), axis=1) - 1

    slots = outgoing_slots(send, queries, key_rows, dp_count)
    arrived = lax.all_to_all(slots, "dp", 0, 0, tiled=True)

    width = value_weight.shape[1] // 2
    half = lax.dynamic_slice_in_dim(value_weight, core * width, width, axis=1)
    x, y = fsdp // side, fsdp % side
    line = gather_ring(half, x, side, along_x)
    own = gather_ring(line, y, side, along_y)
    own = jnp.transpose(own, (1, 0, 2, 3)).reshape(depth, width)
    (other,) = swap([own])

    onward = (((plane_at + hop_steps) % planes * 2)[:, None] + pair).reshape(-1)
    origin = (plane_at + planes - hop_steps) % planes * 2
    origin = jnp.concatenate([origin + core, origin + 1 - core])
    block = jnp.maximum(which(send, onward), 0)
    back_block = jnp.maximum(which(take, onward), 0)
    place, home_place = which(take, origin), which(send, origin)
    leaving = value_blocks(core_of, block, normed, own, other)
    landed = along_z(leaving)
    (swapped,) = swap([jnp.stack(landed)])
    packed_v = pack(core_of, place, landed, swapped, rows)

    column = 2 * jnp.arange(planes, dtype=jnp.int32)
    tile = depth // dp_count
    x_line = (x + jnp.arange(side, dtype=jnp.int32)) % side
    columns = jnp.concatenate([column + core, column + 1 - core])
    turned = turn_columns(columns, x_line, normed, tile)
    turned = [along_x(a, d) if d else a for d, a in enumerate(turned)]

    query_grad, key_grad, value_grad, *returning = attention(
        take, back_block, arrived, packed_v, out_grad, doc_ids
    )
    landed = along_z(returning)
    (swapped,) = swap([jnp.stack(landed)])
    home = pack(core_of, home_place, landed, swapped, rows)
    cut = rows // 2
    before, after = along_x(home, 1), along_x(home, -1)
    top, low = along_x(before[:cut], 1), along_x(after[cut:], -1)
    homes = [(home,), (before,), (top, low), (after,)]
    homes += [tuple(swap(parts)) for parts in homes]
    theirs = jnp.concatenate([a[a.shape[0] // 2 :] for a in turned])
    turned += swap([theirs])

    y_line = (y + jnp.arange(side, dtype=jnp.int32)) % side
    stay, *leave = weight_part(y_line, turned, homes, planes)
    leave = [along_y(a, d + 1) for d, a in enumerate(leave)]
    plane = (stay + sum(a.astype(jnp.float32) for a in leave)).astype(jnp.bfloat16)
    groups = [list(range(c, dp_count, 2)) for c in range(2)]
    parts = lax.all_to_all(plane, "dp", 0, 0, axis_index_groups=groups, tiled=True)
    input_grad = input_gradient(core_of, value_grad, own, other)
    weight_grad = jnp.sum(parts.astype(jnp.float32), axis=0) * grad_scale
    return (query_grad, key_grad, input_grad, weight_grad)


def solution(mesh):
    rows = P(("dp", "fsdp"), None)
    return jax.shard_map(
        local,
        mesh=mesh,
        in_specs=(rows, rows, rows, rows, P("fsdp", None), rows, rows, rows),
        out_specs=(rows, rows, rows, rows),
        check_vma=False,
    )
```

time: 256 us -> 252 us (0.984)
  starting transfers between devices: 22.5 us -> 73 us
  blocking collectives: 35.4 us -> 0 us
  waiting for transfers between devices: 124 us -> 95.5 us
  Pallas kernels: 44.7 us -> 58.6 us
  between operations: 14.1 us -> 1.47 us
  local copies, waits for them, and re-layouts: 2.62 us -> 12.4 us
  matrix products: 5.68 us -> 0 us
    ppermute x1 -> x41, waiting for transfers between devices: 0.01 us -> 94 us  [the longest x14 49.8 us: along_z(): lax.ppermute(a, 'dp', ring((dp_count, planes), d, 2))]
    all_to_all x3 -> x1, waiting for transfers between devices: 73.1 us -> 0.01 us  [local(): arrived = lax.all_to_all(slots, 'dp', 0, 0, tiled=True)]
    ppermute x1 -> x41, starting transfers between devices: 2.31 us -> 61.8 us  [the longest x14 32.3 us: along_z(): lax.ppermute(a, 'dp', ring((dp_count, planes), d, 2))]
    all_gather x1 -> x0, waiting for transfers between devices: 47 us -> none  [local(): weight = lax.all_gather(value_weight, 'fsdp', axis=0, tiled=True)]
    all_to_all x1 -> x0, blocking collectives: 35.4 us -> none  [local(): chips = lax.all_to_all(chip, 'fsdp', 0, 0, tiled=True)]
    pallas_call x3 -> x6, Pallas kernels: 24.2 us -> 38 us  [the longest x1 11.2 us: turn_columns(): pl.pallas_call(turn_kernel, grid_spec=pltpu.PrefetchScalarGridSpec(num_sc...]
    all_to_all x3 -> x1, starting transfers between devices: 16.7 us -> 6.92 us  [local(): arrived = lax.all_to_all(slots, 'dp', 0, 0, tiled=True)]
    unnamed x8 -> x112, local copies, waits for them, and re-layouts: 1.8 us -> 8.3 us
  transfers between devices with their start and end apart: 6 -> 43, of which waited for: 5 -> 23; matrix products, arithmetic and copies ran while one was open for 3% -> 5% of each run, Pallas kernels for 9% -> 15%
where the time goes in v3:
time: 252 us; the launch traced here: 248 us
  waiting for transfers between devices  95.5 us (38%)
  starting transfers between devices  73 us (29%)
  Pallas kernels  58.6 us (23%)
  local copies, waits for them, and re-layouts  12.4 us (5%)
  other arithmetic  7.03 us (3%)
    ppermute x14, waiting for transfers between devices, along_z(): lax.ppermute(a, 'dp', ring((dp_count, planes), d, 2))  49.8 us
    ppermute x14, starting transfers between devices, along_z(): lax.ppermute(a, 'dp', ring((dp_count, planes), d, 2))  32.3 us
    ppermute x7, waiting for transfers between devices, along_y(): return lax.ppermute(array, 'fsdp', ring((fsdp_count, side), step, 1))  24.2 us
    ppermute x11, starting transfers between devices, along_x(): return lax.ppermute(array, 'fsdp', ring((fsdp_count, side), step, side))  17.4 us
    ppermute x11, waiting for transfers between devices, along_x(): return lax.ppermute(array, 'fsdp', ring((fsdp_count, side), step, side))  16.1 us
    pallas_call x1, Pallas kernels, attention(): pl.pallas_call(attention_kernel, grid_spec=pltpu.PrefetchScalarGridSpec(n...  14.4 us
    ppermute x7, starting transfers between devices, along_y(): return lax.ppermute(array, 'fsdp', ring((fsdp_count, side), step, 1))  11.3 us
    pallas_call x1, Pallas kernels, turn_columns(): pl.pallas_call(turn_kernel, grid_spec=pltpu.PrefetchScalarGridSpec(num_sc...  11.2 us
  transfers between devices with their start and end apart: 43, of which 23 were waited for; matrix products, arithmetic and copies ran while one was open for 5% of the time, Pallas kernels for 15%

profile of v3, /device:TPU:0, one launch (start us, length us, event | category | flops | bytes accessed | tf_op | source)
XLA Modules:
  0.0 248.0 jit_solution(5009161974255273595)
XLA Ops:
  1.8 3.2 %collective-permute-start.2 = (bf16[256,256]{1,0:T(8,128)(2,1)S(1)}, bf16[256,256]{1,0:T(8,128)(2,1)S(1)}, u32[]{:S(2)}, u32[]{:S(2)}) collective-permute-start(bf16[256,256]{1,0:T(8,128)(2,1)S(1)} %get-tuple-element.63), channel_id=1, source_target_pairs={{0,12},{1,13},{2,14},{3,15},{4,0},{5,1},{6,2},{7,3},{8,4},{9,5},{1... | collective-permute-start | bytes 393224 | tf_op jit(solution)/shard_map/ppermute | solution.py:409
  5.0 6.2 %outgoing_slots.1 = bf16[16,48,2560]{2,1,0:T(8,128)(2,1)} custom-call(s32[8]{0:T(128)} %bitcast.71, bf16[384,2048]{1,0:T(8,128)(2,1)} %q_ref.1, bf16[384,512]{1,0:T(8,128)(2,1)} %k_ref.1), custom_call_target="tpu_custom_call" | custom-call | tf_op jit(solution)/shard_map/outgoing_slots/pallas_call | solution.py:29
  11.2 6.9 %all-to-all-start = ((bf16[16,48,2560]{2,1,0:T(8,128)(2,1)}), bf16[16,48,2560]{2,1,0:T(8,128)(2,1)}, u32[]{:S(2)}, u32[]{:S(2)}) async-start(bf16[16,48,2560]{2,1,0:T(8,128)(2,1)} %outgoing_slots.1), calls=%async_computation | async-start | bytes 7864320 | tf_op jit(solution)/shard_map/all_to_all | solution.py:418
  18.6 3.0 %collective-permute-start.3 = (bf16[128,256]{1,0:T(8,128)(2,1)S(1)}, bf16[128,256]{1,0:T(8,128)(2,1)S(1)}, u32[]{:S(2)}, u32[]{:S(2)}) collective-permute-start(bf16[128,256]{1,0:T(8,128)(2,1)S(1)} %slice.41), channel_id=1, source_target_pairs={{0,12},{1,13},{2,14},{3,15},{4,0},{5,1},{6,2},{7,3},{8,4},{9,5},{1... | collective-permute-start | bytes 196616 | tf_op jit(solution)/shard_map/ppermute | solution.py:409
  21.6 2.2 collective-permute-done.1
  23.9 1.6 collective-permute-start.4
  25.5 1.7 collective-permute-start.6
  27.2 11.3 %collective-permute-done.4 = bf16[4,256,256]{2,1,0:T(8,128)(2,1)S(1)} collective-permute-done((bf16[4,256,256]{2,1,0:T(8,128)(2,1)S(1)}, bf16[4,256,256]{2,1,0:T(8,128)(2,1)S(1)}, u32[]{:S(2)}, u32[]{:S(2)}) %collective-permute-start.4) | collective-permute-done | bytes 524320 | tf_op jit(solution)/shard_map/ppermute | solution.py:412
  39.9 3.0 %collective-permute-start.7 = (bf16[2,256,256]{2,1,0:T(8,128)(2,1)S(1)}, bf16[2,256,256]{2,1,0:T(8,128)(2,1)S(1)}, u32[]{:S(2)}, u32[]{:S(2)}) collective-permute-start(bf16[2,256,256]{2,1,0:T(8,128)(2,1)S(1)} %slice.43), channel_id=1, source_target_pairs={{0,3},{1,0},{2,1},{3,2},{4,7},{5,4},{6,5},{7,6},{8,11},{9,8},{10,9... | collective-permute-start | bytes 786440 | tf_op jit(solution)/shard_map/ppermute | solution.py:412
  43.0 4.4 %collective-permute-done.5 = bf16[2,256,256]{2,1,0:T(8,128)(2,1)S(1)} collective-permute-done((bf16[2,256,256]{2,1,0:T(8,128)(2,1)S(1)}, bf16[2,256,256]{2,1,0:T(8,128)(2,1)S(1)}, u32[]{:S(2)}, u32[]{:S(2)}) %collective-permute-start.5) | collective-permute-done | bytes 262176 | tf_op jit(solution)/shard_map/ppermute | solution.py:412
  49.4 2.5 %collective-permute-done.8.other_ref = bf16[4096,256]{1,0:T(8,128)(2,1)} collective-permute-done((bf16[4096,256]{1,0:T(8,128)(2,1)S(1)}, bf16[4096,256]{1,0:T(8,128)(2,1)}, u32[]{:S(2)}, u32[]{:S(2)}) %collective-permute-start.8) | collective-permute-done | bytes 2097184 | tf_op jit(solution)/shard_map/ppermute | solution.py:406
  51.9 6.6 %value_blocks.1 = (bf16[2,48,512]{2,1,0:T(8,128)(2,1)}, bf16[2,48,512]{2,1,0:T(8,128)(2,1)}, bf16[2,48,512]{2,1,0:T(8,128)(2,1)}, bf16[2,48,512]{2,1,0:T(8,128)(...) custom-call(s32[1]{0:T(128)} %bitcast.2.core, ...), custom_call_target="tpu_custom_call" | custom-call | flops 1610612736 | bytes 7340032 | tf_op jit(solution)/shard_map/value_blocks/pallas_call | solution.py:80
  58.6 5.6 %collective-permute-start.9 = (bf16[2,48,512]{2,1,0:T(8,128)(2,1)}, bf16[2,48,512]{2,1,0:T(8,128)(2,1)S(1)}, u32[]{:S(2)}, u32[]{:S(2)}) collective-permute-start(bf16[2,48,512]{2,1,0:T(8,128)(2,1)} %get-tuple-element.31), channel_id=1, source_target_pairs={{0,128},{16,144},{32,160},{48,176},{64,192},{80,208},{96,224},{112... | collective-permute-start | bytes 294920 | tf_op jit(solution)/shard_map/ppermute | solution.py:401
  64.8 11.2 %turn_columns.1 = (bf16[1024,384]{1,0:T(8,128)(2,1)}, bf16[1024,384]{1,0:T(8,128)(2,1)}, bf16[1024,384]{1,0:T(8,128)(2,1)}, bf16[1024,384]{1,0:T(8,128)(2,1)}) custom-call(s32[16]{0:T(128)} %pad_add_fusion.1.column, s32[4]{0:T(128)} %and_select_fusion.line, bf16[384,4096]{1,0:T(8,128)(2,1)} %in_ref.1), custom_call_target="tpu_custom_call" | custom-call | tf_op jit(solution)/shard_map/turn_columns/pallas_call | solution.py:142
  76.1 4.1 %collective-permute-start.18 = (bf16[1024,384]{1,0:T(8,128)(2,1)}, bf16[1024,384]{1,0:T(8,128)(2,1)S(1)}, u32[]{:S(2)}, u32[]{:S(2)}) collective-permute-start(bf16[1024,384]{1,0:T(8,128)(2,1)} %get-tuple-element.44), channel_id=1, source_target_pairs={{0,8},{1,9},{2,10},{3,11},{4,12},{5,13},{6,14},{7,15},{8,0},{9,1},... | collective-permute-start | bytes 2359304 | tf_op jit(solution)/shard_map/ppermute | solution.py:409
  80.7 35.2 %collective-permute-done.9.refs_0_ = bf16[2,48,512]{2,1,0:T(8,128)(2,1)S(1)} collective-permute-done((bf16[2,48,512]{2,1,0:T(8,128)(2,1)}, bf16[2,48,512]{2,1,0:T(8,128)(2,1)S(1)}, u32[]{:S(2)}, u32[]{:S(2)}) %collective-permute-start.9) | collective-permute-done | bytes 98336 | tf_op jit(solution)/shard_map/ppermute | solution.py:401
  116.6 2.4 collective-permute-done.10.refs_1_
  119.7 2.8 %collective-permute-done.11.refs_2_ = bf16[2,48,512]{2,1,0:T(8,128)(2,1)S(1)} collective-permute-done((bf16[2,48,512]{2,1,0:T(8,128)(2,1)S(1)}, bf16[2,48,512]{2,1,0:T(8,128)(2,1)S(1)}, u32[]{:S(2)}, u32[]{:S(2)}) %collective-permute-start.11) | collective-permute-done | bytes 98336 | tf_op jit(solution)/shard_map/ppermute | solution.py:401
  122.5 4.3 %collective-permute-start.13 = (bf16[2,48,512]{2,1,0:T(8,128)(2,1)S(1)}, bf16[2,48,512]{2,1,0:T(8,128)(2,1)S(1)}, u32[]{:S(2)}, u32[]{:S(2)}) collective-permute-start(bf16[2,48,512]{2,1,0:T(8,128)(2,1)S(1)} %copy-done.41), channel_id=1, source_target_pairs={{0,192},{16,208},{32,224},{48,240},{64,0},{80,16},{96,32},{112,48}... | collective-permute-start | bytes 294920 | tf_op jit(solution)/shard_map/ppermute | solution.py:401
  128.6 1.5 collective-permute-done.13.refs_4_
  130.1 1.6 collective-permute-start.15
  134.0 1.4 collective-permute-done.15.refs_6_
  137.6 1.0 slice.34
  139.9 3.0 %shard_map.120.v_ref = bf16[384,512]{1,0:T(8,128)(2,1)} custom-call(s32[1]{0:T(128)} %bitcast.2.core, s32[16]{0:T(128)} %broadcast_add_fusion.2.place, bf16[2,48,512]{2,1,0:T(8,128)(2,1)} %copy-done.13, bf16[2,48,512]{2,1,0:T(8,128)(2,1)} %copy-done.15, bf16[2,48,512]{2,1,0:T(8,128)(2,1)} %copy-done.16, bf16[2,48,512]{2,1,0:T(8,128)(2,1)} %copy-done.18, ...), custom_call_target="tpu_custom_call" | custom-call | tf_op jit(solution)/shard_map/pallas_call | solution.py:118
  143.0 14.4 %attention_backward.1 = (bf16[384,2048]{1,0:T(8,128)(2,1)}, bf16[384,512]{1,0:T(8,128)(2,1)}, bf16[384,512]{1,0:T(8,128)(2,1)}, bf16[2,48,512]{2,1,0:T(8,128)(2,...) custom-call(s32[8]{0:T(128)} %bitcast.73, ...), custom_call_target="tpu_custom_call" | custom-call | tf_op jit(solution)/shard_map/attention_backward/pallas_call | solution.py:261
  157.5 2.3 collective-permute-start.21
  160.2 3.2 %collective-permute-start.22 = (bf16[2,48,512]{2,1,0:T(8,128)(2,1)S(1)}, bf16[2,48,512]{2,1,0:T(8,128)(2,1)S(1)}, u32[]{:S(2)}, u32[]{:S(2)}) collective-permute-start(bf16[2,48,512]{2,1,0:T(8,128)(2,1)S(1)} %copy-done.48), channel_id=1, source_target_pairs={{0,96},{16,112},{32,128},{48,144},{64,160},{80,176},{96,192},{112,... | collective-permute-start | bytes 294920 | tf_op jit(solution)/shard_map/ppermute | solution.py:401
  163.4 1.8 collective-permute-start.23
  165.2 4.1 %collective-permute-start.24 = (bf16[2,48,512]{2,1,0:T(8,128)(2,1)S(1)}, bf16[2,48,512]{2,1,0:T(8,128)(2,1)S(1)}, u32[]{:S(2)}, u32[]{:S(2)}) collective-permute-start(bf16[2,48,512]{2,1,0:T(8,128)(2,1)S(1)} %copy-done.44), channel_id=1, source_target_pairs={{0,64},{16,80},{32,96},{48,112},{64,128},{80,144},{96,160},{112,17... | collective-permute-start | bytes 294920 | tf_op jit(solution)/shard_map/ppermute | solution.py:401
  169.3 5.0 %collective-permute-start.25 = (bf16[2,48,512]{2,1,0:T(8,128)(2,1)S(1)}, bf16[2,48,512]{2,1,0:T(8,128)(2,1)S(1)}, u32[]{:S(2)}, u32[]{:S(2)}) collective-permute-start(bf16[2,48,512]{2,1,0:T(8,128)(2,1)S(1)} %copy-done.42), channel_id=1, source_target_pairs={{0,192},{16,208},{32,224},{48,240},{64,0},{80,16},{96,32},{112,48}... | collective-permute-start | bytes 294920 | tf_op jit(solution)/shard_map/ppermute | solution.py:401
  174.3 2.6 %collective-permute-done.22.refs_1_ = bf16[2,48,512]{2,1,0:T(8,128)(2,1)S(1)} collective-permute-done((bf16[2,48,512]{2,1,0:T(8,128)(2,1)S(1)}, bf16[2,48,512]{2,1,0:T(8,128)(2,1)S(1)}, u32[]{:S(2)}, u32[]{:S(2)}) %collective-permute-start.22) | collective-permute-done | bytes 98336 | tf_op jit(solution)/shard_map/ppermute | solution.py:401
  176.9 3.3 %collective-permute-start.27 = (bf16[2,48,512]{2,1,0:T(8,128)(2,1)S(1)}, bf16[2,48,512]{2,1,0:T(8,128)(2,1)S(1)}, u32[]{:S(2)}, u32[]{:S(2)}) collective-permute-start(bf16[2,48,512]{2,1,0:T(8,128)(2,1)S(1)} %copy-done.39), channel_id=1, source_target_pairs={{0,224},{16,240},{32,0},{48,16},{64,32},{80,48},{96,64},{112,80},{... | collective-permute-start | bytes 294920 | tf_op jit(solution)/shard_map/ppermute | solution.py:401
  180.4 2.4 collective-permute-done.26.refs_5_
  184.4 1.3 collective-permute-done.28.refs_8_
  185.8 3.1 %shard_map.121.refs_5_ = bf16[384,512]{1,0:T(8,128)(2,1)} custom-call(s32[1]{0:T(128)} %bitcast.2.core, s32[16]{0:T(128)} %broadcast_add_fusion.1.place, bf16[2,48,512]{2,1,0:T(8,128)(2,1)} %copy-done.17, bf16[2,48,512]{2,1,0:T(8,128)(2,1)} %copy-done.19, bf16[2,48,512]{2,1,0:T(8,128)(2,1)} %copy-done.20, bf16[2,48,512]{2,1,0:T(8,128)(2,1)} %copy-done.22, ...), custom_call_target="tpu_custom_call" | custom-call | tf_op jit(solution)/shard_map/pallas_call | solution.py:118
  189.1 3.0 %collective-permute-start.31 = (bf16[384,512]{1,0:T(8,128)(2,1)}, bf16[384,512]{1,0:T(8,128)(2,1)S(1)}, u32[]{:S(2)}, u32[]{:S(2)}) collective-permute-start(bf16[384,512]{1,0:T(8,128)(2,1)} %shard_map.121.refs_5_), channel_id=1, source_target_pairs={{0,12},{1,13},{2,14},{3,15},{4,0},{5,1},{6,2},{7,3},{8,4},{9,5},{1... | collective-permute-start | bytes 1179656 | tf_op jit(solution)/shard_map/ppermute | solution.py:409
  192.1 9.3 %collective-permute-done.29.refs_6_ = bf16[384,512]{1,0:T(8,128)(2,1)S(1)} collective-permute-done((bf16[384,512]{1,0:T(8,128)(2,1)}, bf16[384,512]{1,0:T(8,128)(2,1)S(1)}, u32[]{:S(2)}, u32[]{:S(2)}) %collective-permute-start.29) | collective-permute-done | bytes 393248 | tf_op jit(solution)/shard_map/ppermute | solution.py:409
  201.6 3.2 %collective-permute-start.32 = (bf16[192,512]{1,0:T(8,128)(2,1)S(1)}, bf16[192,512]{1,0:T(8,128)(2,1)S(1)}, u32[]{:S(2)}, u32[]{:S(2)}) collective-permute-start(bf16[192,512]{1,0:T(8,128)(2,1)S(1)} %slice.48), channel_id=1, source_target_pairs={{0,12},{1,13},{2,14},{3,15},{4,0},{5,1},{6,2},{7,3},{8,4},{9,5},{1... | collective-permute-start | bytes 589832 | tf_op jit(solution)/shard_map/ppermute | solution.py:409
  205.0 3.7 %collective-permute-done.30.refs_7_ = bf16[192,512]{1,0:T(8,128)(2,1)S(1)} collective-permute-done((bf16[192,512]{1,0:T(8,128)(2,1)S(1)}, bf16[192,512]{1,0:T(8,128)(2,1)S(1)}, u32[]{:S(2)}, u32[]{:S(2)}) %collective-permute-start.30) | collective-permute-done | bytes 196640 | tf_op jit(solution)/shard_map/ppermute | solution.py:409
  212.6 6.3 %weight_part.1 = (f32[8,16,512]{2,1,0:T(8,128)}, bf16[8,16,512]{2,1,0:T(8,128)(2,1)}, bf16[8,16,512]{2,1,0:T(8,128)(2,1)}, bf16[8,16,512]{2,1,0:T(8,128)(2,1)}) custom-call(s32[4]{0:T(128)} %and_select_fusion.1.line, bf16[1024,384]{1,0:T(8,128)(2,1)} %get-tuple-element.42.refs_0_, bf16[1024,384]{1,0:T(8,128)(2,1)} %copy-done.1, bf16[1024,384]{1,0:T(8,128)(2,1)} %copy-done.2, ...), custom_call_target="tpu_custom_call" | custom-call | tf_op jit(solution)/shard_map/weight_part/pallas_call | solution.py:338
  218.9 3.1 %collective-permute-start.40 = (bf16[8,16,512]{2,1,0:T(8,128)(2,1)}, bf16[8,16,512]{2,1,0:T(8,128)(2,1)S(1)}, u32[]{:S(2)}, u32[]{:S(2)}) collective-permute-start(bf16[8,16,512]{2,1,0:T(8,128)(2,1)} %get-tuple-element.57), channel_id=1, source_target_pairs={{0,3},{1,0},{2,1},{3,2},{4,7},{5,4},{6,5},{7,6},{8,11},{9,8},{10,9... | collective-permute-start | bytes 393224 | tf_op jit(solution)/shard_map/ppermute | solution.py:412
  223.6 4.9 %collective-permute-done.40 = bf16[8,16,512]{2,1,0:T(8,128)(2,1)S(1)} collective-permute-done((bf16[8,16,512]{2,1,0:T(8,128)(2,1)}, bf16[8,16,512]{2,1,0:T(8,128)(2,1)S(1)}, u32[]{:S(2)}, u32[]{:S(2)}) %collective-permute-start.40) | collective-permute-done | bytes 131104 | tf_op jit(solution)/shard_map/ppermute | solution.py:412
  228.5 1.6 collective-permute-done.39
  230.1 2.0 collective-permute-done.38
  232.1 1.7 add_convert_fusion
  233.8 4.3 %all-to-all-start.1 = ((bf16[8,16,512]{2,1,0:T(8,128)(2,1)}), bf16[8,16,512]{2,1,0:T(8,128)(2,1)S(1)}, u32[]{:S(2)}, u32[]{:S(2)}) async-start(bf16[8,16,512]{2,1,0:T(8,128)(2,1)} %add_convert_fusion), calls=%async_computation.1 | async-start | bytes 262144 | tf_op jit(solution)/shard_map/all_to_all | solution.py:465
  238.1 7.8 %input_gradient.1 = bf16[384,4096]{1,0:T(8,128)(2,1)} custom-call(s32[1]{0:T(128)} %bitcast.2.core, bf16[384,512]{1,0:T(8,128)(2,1)} %get-tuple-element.41.grad_ref, bf16[4096,256]{1,0:T(8,128)(2,1)} %bitcast.69, bf16[4096,256]{1,0:T(8,128)(2,1)} %collective-permute-done.8.other_ref), custom_call_target="tpu_custom_call" | custom-call | flops 1610612736 | bytes 7340032 | tf_op jit(solution)/shard_map/input_gradient/pallas_call | solution.py:168
  245.8 1.5 all-to-all-done.1
  (203 shorter events, 23.9 us)
Async XLA Ops:
  1.7 16.5 %collective-permute-start = (bf16[256,256]{1,0:T(8,128)(2,1)S(1)}, bf16[256,256]{1,0:T(8,128)(2,1)S(1)}, u32[]{:S(2)}, u32[]{:S(2)}) collective-permute-start(bf16[256,256]{1,0:T(8,128)(2,1)S(1)} %get-tuple-element.63), channel_id=1, source_target_pairs={{0,4},{1,5},{2,6},{3,7},{4,8},{5,9},{6,10},{7,11},{8,12},{9,13},{1... | collective-permute-start | bytes 393224 | tf_op jit(solution)/shard_map/ppermute | solution.py:409
  1.8 16.8 %collective-permute-start.2 = (bf16[256,256]{1,0:T(8,128)(2,1)S(1)}, bf16[256,256]{1,0:T(8,128)(2,1)S(1)}, u32[]{:S(2)}, u32[]{:S(2)}) collective-permute-start(bf16[256,256]{1,0:T(8,128)(2,1)S(1)} %get-tuple-element.63), channel_id=1, source_target_pairs={{0,12},{1,13},{2,14},{3,15},{4,0},{5,1},{6,2},{7,3},{8,4},{9,5},{1... | collective-permute-start | bytes 393224 | tf_op jit(solution)/shard_map/ppermute | solution.py:409
  11.2 131.8 %all-to-all-start = ((bf16[16,48,2560]{2,1,0:T(8,128)(2,1)}), bf16[16,48,2560]{2,1,0:T(8,128)(2,1)}, u32[]{:S(2)}, u32[]{:S(2)}) async-start(bf16[16,48,2560]{2,1,0:T(8,128)(2,1)} %outgoing_slots.1), calls=%async_computation | async-start | bytes 7864320 | tf_op jit(solution)/shard_map/all_to_all | solution.py:418
  18.2 5.6 %collective-permute-start.1 = (bf16[128,256]{1,0:T(8,128)(2,1)S(1)}, bf16[128,256]{1,0:T(8,128)(2,1)S(1)}, u32[]{:S(2)}, u32[]{:S(2)}) collective-permute-start(bf16[128,256]{1,0:T(8,128)(2,1)S(1)} %slice.40), channel_id=1, source_target_pairs={{0,4},{1,5},{2,6},{3,7},{4,8},{5,9},{6,10},{7,11},{8,12},{9,13},{1... | collective-permute-start | bytes 196616 | tf_op jit(solution)/shard_map/ppermute | solution.py:409
  18.6 5.2 %collective-permute-start.3 = (bf16[128,256]{1,0:T(8,128)(2,1)S(1)}, bf16[128,256]{1,0:T(8,128)(2,1)S(1)}, u32[]{:S(2)}, u32[]{:S(2)}) collective-permute-start(bf16[128,256]{1,0:T(8,128)(2,1)S(1)} %slice.41), channel_id=1, source_target_pairs={{0,12},{1,13},{2,14},{3,15},{4,0},{5,1},{6,2},{7,3},{8,4},{9,5},{1... | collective-permute-start | bytes 196616 | tf_op jit(solution)/shard_map/ppermute | solution.py:409
  23.9 14.6 %collective-permute-start.4 = (bf16[4,256,256]{2,1,0:T(8,128)(2,1)S(1)}, bf16[4,256,256]{2,1,0:T(8,128)(2,1)S(1)}, u32[]{:S(2)}, u32[]{:S(2)}) collective-permute-start(bf16[4,256,256]{2,1,0:T(8,128)(2,1)S(1)} %bitcast_dynamic-update-slice_fusion.5), channel_id=1, source_target_pairs={{0,1},{1,2},{2,3},{3,0},{4,5},{5,6},{6,7},{7,4},{8,9},{9,10},{10,1... | collective-permute-start | bytes 1572872 | tf_op jit(solution)/shard_map/ppermute | solution.py:412
  25.5 14.4 %collective-permute-start.6 = (bf16[4,256,256]{2,1,0:T(8,128)(2,1)S(1)}, bf16[4,256,256]{2,1,0:T(8,128)(2,1)S(1)}, u32[]{:S(2)}, u32[]{:S(2)}) collective-permute-start(bf16[4,256,256]{2,1,0:T(8,128)(2,1)S(1)} %bitcast_dynamic-update-slice_fusion.5), channel_id=1, source_target_pairs={{0,3},{1,0},{2,1},{3,2},{4,7},{5,4},{6,5},{7,6},{8,11},{9,8},{10,9... | collective-permute-start | bytes 1572872 | tf_op jit(solution)/shard_map/ppermute | solution.py:412
  39.3 8.1 %collective-permute-start.5 = (bf16[2,256,256]{2,1,0:T(8,128)(2,1)S(1)}, bf16[2,256,256]{2,1,0:T(8,128)(2,1)S(1)}, u32[]{:S(2)}, u32[]{:S(2)}) collective-permute-start(bf16[2,256,256]{2,1,0:T(8,128)(2,1)S(1)} %slice.42), channel_id=1, source_target_pairs={{0,1},{1,2},{2,3},{3,0},{4,5},{5,6},{6,7},{7,4},{8,9},{9,10},{10,1... | collective-permute-start | bytes 786440 | tf_op jit(solution)/shard_map/ppermute | solution.py:412
  39.9 7.5 %collective-permute-start.7 = (bf16[2,256,256]{2,1,0:T(8,128)(2,1)S(1)}, bf16[2,256,256]{2,1,0:T(8,128)(2,1)S(1)}, u32[]{:S(2)}, u32[]{:S(2)}) collective-permute-start(bf16[2,256,256]{2,1,0:T(8,128)(2,1)S(1)} %slice.43), channel_id=1, source_target_pairs={{0,3},{1,0},{2,1},{3,2},{4,7},{5,4},{6,5},{7,6},{8,11},{9,8},{10,9... | collective-permute-start | bytes 786440 | tf_op jit(solution)/shard_map/ppermute | solution.py:412
  47.5 4.4 %collective-permute-start.8 = (bf16[4096,256]{1,0:T(8,128)(2,1)S(1)}, bf16[4096,256]{1,0:T(8,128)(2,1)}, u32[]{:S(2)}, u32[]{:S(2)}) collective-permute-start(bf16[4096,256]{1,0:T(8,128)(2,1)S(1)} %bitcast.67), channel_id=1, source_target_pairs={{0,16},{16,0},{32,48},{48,32},{64,80},{80,64},{96,112},{112,96},{1... | collective-permute-start | bytes 6291464 | tf_op jit(solution)/shard_map/ppermute | solution.py:406
  58.5 64.0 %copy-start.41 = (bf16[2,48,512]{2,1,0:T(8,128)(2,1)S(1)}, bf16[2,48,512]{2,1,0:T(8,128)(2,1)}, u32[]{:S(2)}) copy-start(bf16[2,48,512]{2,1,0:T(8,128)(2,1)} %get-tuple-element.35) | copy-start | bytes 294916
  58.5 68.9 %copy-start.38 = (bf16[2,48,512]{2,1,0:T(8,128)(2,1)S(1)}, bf16[2,48,512]{2,1,0:T(8,128)(2,1)}, u32[]{:S(2)}) copy-start(bf16[2,48,512]{2,1,0:T(8,128)(2,1)} %get-tuple-element.36) | copy-start | bytes 294916
  58.5 71.6 %copy-start.37 = (bf16[2,48,512]{2,1,0:T(8,128)(2,1)S(1)}, bf16[2,48,512]{2,1,0:T(8,128)(2,1)}, u32[]{:S(2)}) copy-start(bf16[2,48,512]{2,1,0:T(8,128)(2,1)} %get-tuple-element.37) | copy-start | bytes 294916
  58.6 57.3 %collective-permute-start.9 = (bf16[2,48,512]{2,1,0:T(8,128)(2,1)}, bf16[2,48,512]{2,1,0:T(8,128)(2,1)S(1)}, u32[]{:S(2)}, u32[]{:S(2)}) collective-permute-start(bf16[2,48,512]{2,1,0:T(8,128)(2,1)} %get-tuple-element.31), channel_id=1, source_target_pairs={{0,128},{16,144},{32,160},{48,176},{64,192},{80,208},{96,224},{112... | collective-permute-start | bytes 294920 | tf_op jit(solution)/shard_map/ppermute | solution.py:401
  64.8 71.3 %copy-start.12 = (bf16[2,48,512]{2,1,0:T(8,128)(2,1)S(1)}, bf16[2,48,512]{2,1,0:T(8,128)(2,1)}, u32[]{:S(2)}) copy-start(bf16[2,48,512]{2,1,0:T(8,128)(2,1)} %get-tuple-element.38.refs_7_) | copy-start | bytes 294916
  64.8 72.0 %copy-start.32 = (s32[1,384]{1,0:T(1,128)S(1)}, s32[1,384]{1,0:T(1,128)}, u32[]{:S(2)}) copy-start(s32[1,384]{1,0:T(1,128)} %doc_row.1) | copy-start | bytes 4612
  76.0 63.9 %collective-permute-start.17 = (bf16[1024,384]{1,0:T(8,128)(2,1)}, bf16[1024,384]{1,0:T(8,128)(2,1)S(1)}, u32[]{:S(2)}, u32[]{:S(2)}) collective-permute-start(bf16[1024,384]{1,0:T(8,128)(2,1)} %get-tuple-element.43), channel_id=1, source_target_pairs={{0,4},{1,5},{2,6},{3,7},{4,8},{5,9},{6,10},{7,11},{8,12},{9,13},{1... | collective-permute-start | bytes 2359304 | tf_op jit(solution)/shard_map/ppermute | solution.py:409
  76.1 63.7 %collective-permute-start.18 = (bf16[1024,384]{1,0:T(8,128)(2,1)}, bf16[1024,384]{1,0:T(8,128)(2,1)S(1)}, u32[]{:S(2)}, u32[]{:S(2)}) collective-permute-start(bf16[1024,384]{1,0:T(8,128)(2,1)} %get-tuple-element.44), channel_id=1, source_target_pairs={{0,8},{1,9},{2,10},{3,11},{4,12},{5,13},{6,14},{7,15},{8,0},{9,1},... | collective-permute-start | bytes 2359304 | tf_op jit(solution)/shard_map/ppermute | solution.py:409
  80.2 59.6 %collective-permute-start.19 = (bf16[1024,384]{1,0:T(8,128)(2,1)}, bf16[1024,384]{1,0:T(8,128)(2,1)S(1)}, u32[]{:S(2)}, u32[]{:S(2)}) collective-permute-start(bf16[1024,384]{1,0:T(8,128)(2,1)} %get-tuple-element.45), channel_id=1, source_target_pairs={{0,12},{1,13},{2,14},{3,15},{4,0},{5,1},{6,2},{7,3},{8,4},{9,5},{1... | collective-permute-start | bytes 2359304 | tf_op jit(solution)/shard_map/ppermute | solution.py:409
  80.2 38.8 %collective-permute-start.10 = (bf16[2,48,512]{2,1,0:T(8,128)(2,1)S(1)}, bf16[2,48,512]{2,1,0:T(8,128)(2,1)S(1)}, u32[]{:S(2)}, u32[]{:S(2)}) collective-permute-start(bf16[2,48,512]{2,1,0:T(8,128)(2,1)S(1)} %copy-done.47), channel_id=1, source_target_pairs={{0,96},{16,112},{32,128},{48,144},{64,160},{80,176},{96,192},{112,... | collective-permute-start | bytes 294920 | tf_op jit(solution)/shard_map/ppermute | solution.py:401
  115.9 6.6 %collective-permute-start.11 = (bf16[2,48,512]{2,1,0:T(8,128)(2,1)S(1)}, bf16[2,48,512]{2,1,0:T(8,128)(2,1)S(1)}, u32[]{:S(2)}, u32[]{:S(2)}) collective-permute-start(bf16[2,48,512]{2,1,0:T(8,128)(2,1)S(1)} %copy-done.45), channel_id=1, source_target_pairs={{0,160},{16,176},{32,192},{48,208},{64,224},{80,240},{96,0},{112,1... | collective-permute-start | bytes 294920 | tf_op jit(solution)/shard_map/ppermute | solution.py:401
  119.0 8.5 %collective-permute-start.12 = (bf16[2,48,512]{2,1,0:T(8,128)(2,1)S(1)}, bf16[2,48,512]{2,1,0:T(8,128)(2,1)S(1)}, u32[]{:S(2)}, u32[]{:S(2)}) collective-permute-start(bf16[2,48,512]{2,1,0:T(8,128)(2,1)S(1)} %copy-done.43), channel_id=1, source_target_pairs={{0,64},{16,80},{32,96},{48,112},{64,128},{80,144},{96,160},{112,17... | collective-permute-start | bytes 294920 | tf_op jit(solution)/shard_map/ppermute | solution.py:401
  122.5 7.6 %collective-permute-start.13 = (bf16[2,48,512]{2,1,0:T(8,128)(2,1)S(1)}, bf16[2,48,512]{2,1,0:T(8,128)(2,1)S(1)}, u32[]{:S(2)}, u32[]{:S(2)}) collective-permute-start(bf16[2,48,512]{2,1,0:T(8,128)(2,1)S(1)} %copy-done.41), channel_id=1, source_target_pairs={{0,192},{16,208},{32,224},{48,240},{64,0},{80,16},{96,32},{112,48}... | collective-permute-start | bytes 294920 | tf_op jit(solution)/shard_map/ppermute | solution.py:401
  127.5 5.9 %collective-permute-start.14 = (bf16[2,48,512]{2,1,0:T(8,128)(2,1)S(1)}, bf16[2,48,512]{2,1,0:T(8,128)(2,1)S(1)}, u32[]{:S(2)}, u32[]{:S(2)}) collective-permute-start(bf16[2,48,512]{2,1,0:T(8,128)(2,1)S(1)} %copy-done.38), channel_id=1, source_target_pairs={{0,32},{16,48},{32,64},{48,80},{64,96},{80,112},{96,128},{112,144}... | collective-permute-start | bytes 294920 | tf_op jit(solution)/shard_map/ppermute | solution.py:401
  130.1 5.3 %collective-permute-start.15 = (bf16[2,48,512]{2,1,0:T(8,128)(2,1)S(1)}, bf16[2,48,512]{2,1,0:T(8,128)(2,1)S(1)}, u32[]{:S(2)}, u32[]{:S(2)}) collective-permute-start(bf16[2,48,512]{2,1,0:T(8,128)(2,1)S(1)} %copy-done.37), channel_id=1, source_target_pairs={{0,224},{16,240},{32,0},{48,16},{64,32},{80,48},{96,64},{112,80},{... | collective-permute-start | bytes 294920 | tf_op jit(solution)/shard_map/ppermute | solution.py:401
  136.8 3.2 %collective-permute-start.16 = (bf16[8,2,48,512]{3,2,1,0:T(8,128)(2,1)}, bf16[8,2,48,512]{3,2,1,0:T(8,128)(2,1)}, u32[]{:S(2)}, u32[]{:S(2)}) collective-permute-start(bf16[8,2,48,512]{3,2,1,0:T(8,128)(2,1)} %bitcast_dynamic-update-slice_fusion.16), channel_id=1, source_target_pairs={{0,16},{16,0},{32,48},{48,32},{64,80},{80,64},{96,112},{112,96},{1... | collective-permute-start | bytes 2359304 | tf_op jit(solution)/shard_map/ppermute | solution.py:406
  157.5 11.8 %collective-permute-start.21 = (bf16[2,48,512]{2,1,0:T(8,128)(2,1)}, bf16[2,48,512]{2,1,0:T(8,128)(2,1)S(1)}, u32[]{:S(2)}, u32[]{:S(2)}) collective-permute-start(bf16[2,48,512]{2,1,0:T(8,128)(2,1)} %get-tuple-element.46), channel_id=1, source_target_pairs={{0,128},{16,144},{32,160},{48,176},{64,192},{80,208},{96,224},{112... | collective-permute-start | bytes 294920 | tf_op jit(solution)/shard_map/ppermute | solution.py:401
  159.9 44.9 %collective-permute-start.20 = (bf16[2048,384]{1,0:T(8,128)(2,1)S(1)}, bf16[2048,384]{1,0:T(8,128)(2,1)S(1)}, u32[]{:S(2)}, u32[]{:S(2)}) collective-permute-start(bf16[2048,384]{1,0:T(8,128)(2,1)S(1)} %pad_maximum_fusion), channel_id=1, source_target_pairs={{0,16},{16,0},{32,48},{48,32},{64,80},{80,64},{96,112},{112,96},{1... | collective-permute-start | bytes 4718600 | tf_op jit(solution)/shard_map/ppermute | solution.py:406
  160.2 16.7 %collective-permute-start.22 = (bf16[2,48,512]{2,1,0:T(8,128)(2,1)S(1)}, bf16[2,48,512]{2,1,0:T(8,128)(2,1)S(1)}, u32[]{:S(2)}, u32[]{:S(2)}) collective-permute-start(bf16[2,48,512]{2,1,0:T(8,128)(2,1)S(1)} %copy-done.48), channel_id=1, source_target_pairs={{0,96},{16,112},{32,128},{48,144},{64,160},{80,176},{96,192},{112,... | collective-permute-start | bytes 294920 | tf_op jit(solution)/shard_map/ppermute | solution.py:401
  163.4 13.5 %collective-permute-start.23 = (bf16[2,48,512]{2,1,0:T(8,128)(2,1)S(1)}, bf16[2,48,512]{2,1,0:T(8,128)(2,1)S(1)}, u32[]{:S(2)}, u32[]{:S(2)}) collective-permute-start(bf16[2,48,512]{2,1,0:T(8,128)(2,1)S(1)} %copy-done.46), channel_id=1, source_target_pairs={{0,160},{16,176},{32,192},{48,208},{64,224},{80,240},{96,0},{112,1... | collective-permute-start | bytes 294920 | tf_op jit(solution)/shard_map/ppermute | solution.py:401
  165.2 15.0 %collective-permute-start.24 = (bf16[2,48,512]{2,1,0:T(8,128)(2,1)S(1)}, bf16[2,48,512]{2,1,0:T(8,128)(2,1)S(1)}, u32[]{:S(2)}, u32[]{:S(2)}) collective-permute-start(bf16[2,48,512]{2,1,0:T(8,128)(2,1)S(1)} %copy-done.44), channel_id=1, source_target_pairs={{0,64},{16,80},{32,96},{48,112},{64,128},{80,144},{96,160},{112,17... | collective-permute-start | bytes 294920 | tf_op jit(solution)/shard_map/ppermute | solution.py:401
  169.3 11.1 %collective-permute-start.25 = (bf16[2,48,512]{2,1,0:T(8,128)(2,1)S(1)}, bf16[2,48,512]{2,1,0:T(8,128)(2,1)S(1)}, u32[]{:S(2)}, u32[]{:S(2)}) collective-permute-start(bf16[2,48,512]{2,1,0:T(8,128)(2,1)S(1)} %copy-done.42), channel_id=1, source_target_pairs={{0,192},{16,208},{32,224},{48,240},{64,0},{80,16},{96,32},{112,48}... | collective-permute-start | bytes 294920 | tf_op jit(solution)/shard_map/ppermute | solution.py:401
  176.9 5.9 %collective-permute-start.26 = (bf16[2,48,512]{2,1,0:T(8,128)(2,1)S(1)}, bf16[2,48,512]{2,1,0:T(8,128)(2,1)S(1)}, u32[]{:S(2)}, u32[]{:S(2)}) collective-permute-start(bf16[2,48,512]{2,1,0:T(8,128)(2,1)S(1)} %copy-done.40), channel_id=1, source_target_pairs={{0,32},{16,48},{32,64},{48,80},{64,96},{80,112},{96,128},{112,144}... | collective-permute-start | bytes 294920 | tf_op jit(solution)/shard_map/ppermute | solution.py:401
  176.9 6.3 %collective-permute-start.27 = (bf16[2,48,512]{2,1,0:T(8,128)(2,1)S(1)}, bf16[2,48,512]{2,1,0:T(8,128)(2,1)S(1)}, u32[]{:S(2)}, u32[]{:S(2)}) collective-permute-start(bf16[2,48,512]{2,1,0:T(8,128)(2,1)S(1)} %copy-done.39), channel_id=1, source_target_pairs={{0,224},{16,240},{32,0},{48,16},{64,32},{80,48},{96,64},{112,80},{... | collective-permute-start | bytes 294920 | tf_op jit(solution)/shard_map/ppermute | solution.py:401
  183.2 2.5 %collective-permute-start.28 = (bf16[8,2,48,512]{3,2,1,0:T(8,128)(2,1)S(1)}, bf16[8,2,48,512]{3,2,1,0:T(8,128)(2,1)}, u32[]{:S(2)}, u32[]{:S(2)}) collective-permute-start(bf16[8,2,48,512]{3,2,1,0:T(8,128)(2,1)S(1)} %bitcast_dynamic-update-slice_fusion.8), channel_id=1, source_target_pairs={{0,16},{16,0},{32,48},{48,32},{64,80},{80,64},{96,112},{112,96},{1... | collective-permute-start | bytes 2359304 | tf_op jit(solution)/shard_map/ppermute | solution.py:406
  188.8 12.5 %collective-permute-start.29 = (bf16[384,512]{1,0:T(8,128)(2,1)}, bf16[384,512]{1,0:T(8,128)(2,1)S(1)}, u32[]{:S(2)}, u32[]{:S(2)}) collective-permute-start(bf16[384,512]{1,0:T(8,128)(2,1)} %shard_map.121.refs_5_), channel_id=1, source_target_pairs={{0,4},{1,5},{2,6},{3,7},{4,8},{5,9},{6,10},{7,11},{8,12},{9,13},{1... | collective-permute-start | bytes 1179656 | tf_op jit(solution)/shard_map/ppermute | solution.py:409
  189.1 12.5 %collective-permute-start.31 = (bf16[384,512]{1,0:T(8,128)(2,1)}, bf16[384,512]{1,0:T(8,128)(2,1)S(1)}, u32[]{:S(2)}, u32[]{:S(2)}) collective-permute-start(bf16[384,512]{1,0:T(8,128)(2,1)} %shard_map.121.refs_5_), channel_id=1, source_target_pairs={{0,12},{1,13},{2,14},{3,15},{4,0},{5,1},{6,2},{7,3},{8,4},{9,5},{1... | collective-permute-start | bytes 1179656 | tf_op jit(solution)/shard_map/ppermute | solution.py:409
  192.1 18.2 %collective-permute-start.33 = (bf16[384,512]{1,0:T(8,128)(2,1)}, bf16[384,512]{1,0:T(8,128)(2,1)S(1)}, u32[]{:S(2)}, u32[]{:S(2)}) collective-permute-start(bf16[384,512]{1,0:T(8,128)(2,1)} %shard_map.121.refs_5_), channel_id=1, source_target_pairs={{0,16},{16,0},{32,48},{48,32},{64,80},{80,64},{96,112},{112,96},{1... | collective-permute-start | bytes 1179656 | tf_op jit(solution)/shard_map/ppermute | solution.py:406
  201.4 7.3 %collective-permute-start.30 = (bf16[192,512]{1,0:T(8,128)(2,1)S(1)}, bf16[192,512]{1,0:T(8,128)(2,1)S(1)}, u32[]{:S(2)}, u32[]{:S(2)}) collective-permute-start(bf16[192,512]{1,0:T(8,128)(2,1)S(1)} %slice.47), channel_id=1, source_target_pairs={{0,4},{1,5},{2,6},{3,7},{4,8},{5,9},{6,10},{7,11},{8,12},{9,13},{1... | collective-permute-start | bytes 589832 | tf_op jit(solution)/shard_map/ppermute | solution.py:409
  201.5 8.8 %collective-permute-start.34 = (bf16[384,512]{1,0:T(8,128)(2,1)S(1)}, bf16[384,512]{1,0:T(8,128)(2,1)S(1)}, u32[]{:S(2)}, u32[]{:S(2)}) collective-permute-start(bf16[384,512]{1,0:T(8,128)(2,1)S(1)} %collective-permute-done.29.refs_6_), channel_id=1, source_target_pairs={{0,16},{16,0},{32,48},{48,32},{64,80},{80,64},{96,112},{112,96},{1... | collective-permute-start | bytes 1179656 | tf_op jit(solution)/shard_map/ppermute | solution.py:406
  201.6 8.0 %collective-permute-start.32 = (bf16[192,512]{1,0:T(8,128)(2,1)S(1)}, bf16[192,512]{1,0:T(8,128)(2,1)S(1)}, u32[]{:S(2)}, u32[]{:S(2)}) collective-permute-start(bf16[192,512]{1,0:T(8,128)(2,1)S(1)} %slice.48), channel_id=1, source_target_pairs={{0,12},{1,13},{2,14},{3,15},{4,0},{5,1},{6,2},{7,3},{8,4},{9,5},{1... | collective-permute-start | bytes 589832 | tf_op jit(solution)/shard_map/ppermute | solution.py:409
  204.8 6.3 %collective-permute-start.37 = (bf16[384,512]{1,0:T(8,128)(2,1)S(1)}, bf16[384,512]{1,0:T(8,128)(2,1)S(1)}, u32[]{:S(2)}, u32[]{:S(2)}) collective-permute-start(bf16[384,512]{1,0:T(8,128)(2,1)S(1)} %collective-permute-done.31.refs_9_), channel_id=1, source_target_pairs={{0,16},{16,0},{32,48},{48,32},{64,80},{80,64},{96,112},{112,96},{1... | collective-permute-start | bytes 1179656 | tf_op jit(solution)/shard_map/ppermute | solution.py:406
  208.7 1.6 collective-permute-start.35
  209.6 1.4 collective-permute-start.36
  218.9 9.6 %collective-permute-start.40 = (bf16[8,16,512]{2,1,0:T(8,128)(2,1)}, bf16[8,16,512]{2,1,0:T(8,128)(2,1)S(1)}, u32[]{:S(2)}, u32[]{:S(2)}) collective-permute-start(bf16[8,16,512]{2,1,0:T(8,128)(2,1)} %get-tuple-element.57), channel_id=1, source_target_pairs={{0,3},{1,0},{2,1},{3,2},{4,7},{5,4},{6,5},{7,6},{8,11},{9,8},{10,9... | collective-permute-start | bytes 393224 | tf_op jit(solution)/shard_map/ppermute | solution.py:412
  222.0 8.1 %collective-permute-start.39 = (bf16[8,16,512]{2,1,0:T(8,128)(2,1)}, bf16[8,16,512]{2,1,0:T(8,128)(2,1)S(1)}, u32[]{:S(2)}, u32[]{:S(2)}) collective-permute-start(bf16[8,16,512]{2,1,0:T(8,128)(2,1)} %get-tuple-element.56), channel_id=1, source_target_pairs={{0,2},{1,3},{2,0},{3,1},{4,6},{5,7},{6,4},{7,5},{8,10},{9,11},{10,... | collective-permute-start | bytes 393224 | tf_op jit(solution)/shard_map/ppermute | solution.py:412
  222.6 9.5 %collective-permute-start.38 = (bf16[8,16,512]{2,1,0:T(8,128)(2,1)}, bf16[8,16,512]{2,1,0:T(8,128)(2,1)S(1)}, u32[]{:S(2)}, u32[]{:S(2)}) collective-permute-start(bf16[8,16,512]{2,1,0:T(8,128)(2,1)} %get-tuple-element.55), channel_id=1, source_target_pairs={{0,1},{1,2},{2,3},{3,0},{4,5},{5,6},{6,7},{7,4},{8,9},{9,10},{10,1... | collective-permute-start | bytes 393224 | tf_op jit(solution)/shard_map/ppermute | solution.py:412
  233.8 13.5 %all-to-all-start.1 = ((bf16[8,16,512]{2,1,0:T(8,128)(2,1)}), bf16[8,16,512]{2,1,0:T(8,128)(2,1)S(1)}, u32[]{:S(2)}, u32[]{:S(2)}) async-start(bf16[8,16,512]{2,1,0:T(8,128)(2,1)} %add_convert_fusion), calls=%async_computation.1 | async-start | bytes 262144 | tf_op jit(solution)/shard_map/all_to_all | solution.py:465
  (45 other events, 480.4 us)

commit v4 on v3

--- a/solution.py
+++ b/solution.py
@@ -1,5 +1,3 @@
-import functools
-
 import jax
 import jax.numpy as jnp
 from jax import lax
@@ -16,32 +14,32 @@
 QUERY_TILE = 128
 
 
-def outgoing_kernel(send, q_ref, k_ref, out_ref):
-    width = q_ref.shape[1]
-    out_ref[0, :, :width] = q_ref[...]
-    out_ref[0, :, width:] = k_ref[...]
-
-
-def outgoing_slots(send, queries, key_rows, peers):
-    rows, width = queries.shape
-    key_width = key_rows.shape[1]
-    blocks = rows // BLOCK_ROWS
+def outgoing_kernel(send, *refs):
+    *sources, out = refs
+    at = 0
+    for ref in sources:
+        out[0, :, at : at + ref.shape[1]] = ref[...]
+        at += ref.shape[1]
+
+
+def outgoing_slots(send, sources, peers):
+    blocks = send.shape[0]
+    width = sum(columns for _, columns, _ in sources)
+    dtype = sources[0][0].dtype
     return pl.pallas_call(
         outgoing_kernel,
         grid_spec=pltpu.PrefetchScalarGridSpec(
             num_scalar_prefetch=1,
             grid=(blocks,),
             in_specs=[
-                pl.BlockSpec((BLOCK_ROWS, width), lambda b, send: (b, 0)),
-                pl.BlockSpec((BLOCK_ROWS, key_width), lambda b, send: (b, 0)),
-            ],
-            out_specs=pl.BlockSpec(
-                (1, BLOCK_ROWS, width + key_width), lambda b, send: (send[b], 0, 0)
-            ),
-        ),
-        out_shape=jax.ShapeDtypeStruct((peers, BLOCK_ROWS, width + key_width), queries.dtype),
+                pl.BlockSpec((BLOCK_ROWS, columns), lambda b, send, at=at: (b, at))
+                for _, columns, at in sources
+            ],
+            out_specs=pl.BlockSpec((1, BLOCK_ROWS, width), lambda b, send: (send[b], 0, 0)),
+        ),
+        out_shape=jax.ShapeDtypeStruct((peers, BLOCK_ROWS, width), dtype),
         name="outgoing_slots",
-    )(send, queries, key_rows)
+    )(send, *(array for array, _, _ in sources))
 
 
 def halves(core, ref, width):
@@ -128,29 +126,49 @@
     )(core, place, *own, swapped)
 
 
-def turn_kernel(column, line, in_ref, *rest):
-    outs, turned = rest[:-1], rest[-1]
-    turned[...] = in_ref[...].T.reshape(turned.shape)
-    for o, out in enumerate(outs):
-        out[...] = turned[line[o]]
-
-
-def turn_columns(column, line, array, tile):
+def pick_kernel(column, in_ref, out_ref):
+    out_ref[...] = in_ref[...]
+
+
+def pick_columns(column, array, tile):
     rows = array.shape[0]
-    steps, lines = column.shape[0], line.shape[0]
-    share = tile // lines
+    steps = column.shape[0]
+    return pl.pallas_call(
+        pick_kernel,
+        grid_spec=pltpu.PrefetchScalarGridSpec(
+            num_scalar_prefetch=1,
+            grid=(steps,),
+            in_specs=[pl.BlockSpec((rows, tile), lambda z, column: (0, column[z]))],
+            out_specs=pl.BlockSpec((rows, tile), lambda z, column: (0, z)),
+        ),
+        out_shape=jax.ShapeDtypeStruct((rows, tile * steps), array.dtype),
+        name="pick_columns",
+    )(column, array)
+
+
+def turn_kernel(column, own_ref, got_ref, out_ref):
+    rows = own_ref.shape[0]
+    out_ref[:, :rows] = own_ref[...].T
+    out_ref[:, rows:] = got_ref[...].T
+
+
+def turn_columns(column, array, got, tile):
+    rows = array.shape[0]
+    steps = column.shape[0]
     return pl.pallas_call(
         turn_kernel,
         grid_spec=pltpu.PrefetchScalarGridSpec(
-            num_scalar_prefetch=2,
+            num_scalar_prefetch=1,
             grid=(steps,),
-            in_specs=[pl.BlockSpec((rows, tile), lambda z, column, line: (0, column[z]))],
-            out_specs=[pl.BlockSpec((share, rows), lambda z, column, line: (z, 0))] * lines,
-            scratch_shapes=[pltpu.VMEM((lines, share, rows), array.dtype)],
-        ),
-        out_shape=[jax.ShapeDtypeStruct((share * steps, rows), array.dtype)] * lines,
+            in_specs=[
+                pl.BlockSpec((rows, tile), lambda z, column: (0, column[z])),
+                pl.BlockSpec((rows, tile), lambda z, column: (0, z)),
+            ],
+            out_specs=pl.BlockSpec((tile, 2 * rows), lambda z, column: (z, 0)),
+        ),
+        out_shape=jax.ShapeDtypeStruct((tile * steps, 2 * rows), array.dtype),
         name="turn_columns",
-    )(column, line, array)
+    )(column, array, got)
 
 
 def input_grad_kernel(core, grad_ref, own_ref, other_ref, out_ref):
@@ -187,11 +205,8 @@
     )(core, value_grad, own, other)
 
 
-def attention_kernel(
-    take, back_block, q_ref, k_ref, v_ref, grad_ref, doc_row, doc_col,
-    query_grad, key_grad, value_grad, *rest,
-):
-    returning = rest[:-5]
+def attention_kernel(take, q_ref, k_ref, v_ref, grad_ref, doc_row, doc_col, *rest):
+    query_grad, key_grad, value_grad, returning = rest[-9:-5]
     q_rows, k_rows, bias, key_total, value_total = rest[-5:]
     rows = grad_ref.shape[0]
     blocks = rows // BLOCK_ROWS
@@ -246,37 +261,38 @@
         value_total[:reach, :] += lax.dot_general(half, g, tn, preferred_element_type=jnp.float32)
     key_grad[...] = key_total[...].astype(key_grad.dtype)
     value_grad[...] = value_total[...].astype(value_grad.dtype)
-    for o, out in enumerate(returning):
-        for c in range(out.shape[0]):
-            first = pl.multiple_of(back_block[2 * o + c] * BLOCK_ROWS, 16)
-            out[c] = value_total[pl.ds(first, BLOCK_ROWS), :].astype(out.dtype)
-
-
-def attention(take, back_block, arrived, packed_v, out_grad, doc_ids):
-    peers = arrived.shape[0]
+    returning[...] = jnp.zeros_like(returning)
+    for p in range(blocks):
+        place = slice(p * BLOCK_ROWS, (p + 1) * BLOCK_ROWS)
+        returning[take[p]] = value_total[place, :].astype(returning.dtype)
+
+
+def attention(take, arrived_q, arrived_k, packed_v, out_grad, doc_ids, first, count, key_at, done):
+    peers = arrived_q.shape[0]
     rows = out_grad.shape[0]
     wide = GROUP * HEAD_DIM
-    first_key = HEADS
     bf16 = jnp.bfloat16
+    slot = (peers, BLOCK_ROWS, HEAD_DIM)
     return pl.pallas_call(
         attention_kernel,
         grid_spec=pltpu.PrefetchScalarGridSpec(
-            num_scalar_prefetch=2,
-            grid=(KV_HEADS,),
-            in_specs=[
-                pl.BlockSpec((peers, BLOCK_ROWS, wide), lambda g, *_: (0, 0, g)),
-                pl.BlockSpec((peers, BLOCK_ROWS, HEAD_DIM), lambda g, *_: (0, 0, first_key + g)),
-                pl.BlockSpec((rows, HEAD_DIM), lambda g, *_: (0, g)),
-                pl.BlockSpec((rows, wide), lambda g, *_: (0, g)),
-                pl.BlockSpec((1, rows), lambda g, *_: (0, 0)),
-                pl.BlockSpec((rows, 1), lambda g, *_: (0, 0)),
-            ],
+            num_scalar_prefetch=1,
+            grid=(count,),
+            in_specs=[
+                pl.BlockSpec((peers, BLOCK_ROWS, wide), lambda g, take: (0, 0, g)),
+                pl.BlockSpec(slot, lambda g, take: (0, 0, key_at + first + g)),
+                pl.BlockSpec((rows, HEAD_DIM), lambda g, take: (0, first + g)),
+                pl.BlockSpec((rows, wide), lambda g, take: (0, first + g)),
+                pl.BlockSpec((1, rows), lambda g, take: (0, 0)),
+                pl.BlockSpec((rows, 1), lambda g, take: (0, 0)),
+            ]
+            + [pl.BlockSpec(memory_space=pl.ANY)] * len(done),
             out_specs=[
-                pl.BlockSpec((rows, wide), lambda g, *_: (0, g)),
-                pl.BlockSpec((rows, HEAD_DIM), lambda g, *_: (0, g)),
-                pl.BlockSpec((rows, HEAD_DIM), lambda g, *_: (0, g)),
-            ]
-            + [pl.BlockSpec((2, BLOCK_ROWS, HEAD_DIM), lambda g, *_: (0, 0, g))] * (peers // 2),
+                pl.BlockSpec((rows, wide), lambda g, take: (0, first + g)),
+                pl.BlockSpec((rows, HEAD_DIM), lambda g, take: (0, first + g)),
+                pl.BlockSpec((rows, HEAD_DIM), lambda g, take: (0, first + g)),
+                pl.BlockSpec(slot, lambda g, take: (0, 0, first + g)),
+            ],
             scratch_shapes=[
                 pltpu.VMEM((rows, wide), bf16),
                 pltpu.VMEM((rows, HEAD_DIM), bf16),
@@ -289,70 +305,59 @@
             jax.ShapeDtypeStruct((rows, KV_HEADS * wide), bf16),
             jax.ShapeDtypeStruct((rows, KV_HEADS * HEAD_DIM), bf16),
             jax.ShapeDtypeStruct((rows, KV_HEADS * HEAD_DIM), bf16),
-        ]
-        + [jax.ShapeDtypeStruct((2, BLOCK_ROWS, KV_HEADS * HEAD_DIM), bf16)] * (peers // 2),
+            jax.ShapeDtypeStruct((peers, BLOCK_ROWS, KV_HEADS * HEAD_DIM), bf16),
+        ],
+        input_output_aliases={7 + i: i for i in range(len(done))},
+        cost_estimate=pl.CostEstimate(
+            flops=12 * rows * rows * HEAD_DIM * GROUP * count,
+            bytes_accessed=10 * rows * wide * count,
+            transcendentals=rows * rows * GROUP * count,
+        ),
         name="attention_backward",
-    )(take, back_block, arrived, arrived, packed_v, out_grad, doc_ids, doc_ids.reshape(rows, 1))
-
-
-def weight_kernel(loads, line, *refs):
-    pieces = len(loads)
-    own = pieces // 2
-    sources = refs[: own + 1 + sum(loads)]
-    stay, *leave = refs[len(sources) : -4]
-    left, right, total, sems = refs[-4:]
-    depth, rows = left.shape[1:]
-    at = own + 1
-    for i, parts in enumerate(loads):
-        part = sources[min(i, own)].at[pl.ds(max(i - own, 0) * depth, depth)]
-        pltpu.make_async_copy(part, left.at[i], sems.at[i, 0]).start()
-        for j in range(parts):
-            place = pl.ds(j * (rows // parts), rows // parts)
-            pltpu.make_async_copy(sources[at], right.at[i, place], sems.at[i, 1]).start()
-            at += 1
-    total[...] = jnp.zeros_like(total)
-
-    def add(i, _):
-        pltpu.make_async_copy(left.at[i], left.at[i], sems.at[i, 0]).wait()
-        pltpu.make_async_copy(right.at[i], right.at[i], sems.at[i, 1]).wait()
-        part = jnp.dot(left[i], right[i], preferred_element_type=jnp.float32)
-        total[...] += part.reshape(total.shape)
-        return 0
-
-    lax.fori_loop(0, pieces, add, 0)
-    stay[...] = total[:, line[0]]
-    for o, out in enumerate(leave):
-        out[...] = total[:, line[o + 1]].astype(out.dtype)
-
-
-def weight_part(line, turned, homes, steps):
-    rows = turned[0].shape[1]
-    depth = turned[0].shape[0] // 2
-    width = homes[0][0].shape[1]
-    pieces, lines = len(homes), line.shape[0]
-    share = depth // steps // lines
-    shape = (steps, share, width)
-    loads = tuple(len(parts) for parts in homes)
-    flat = [part for parts in homes for part in parts]
-    bf16 = jnp.bfloat16
-    return pl.pallas_call(
-        functools.partial(weight_kernel, loads),
-        grid_spec=pltpu.PrefetchScalarGridSpec(
-            num_scalar_prefetch=1,
-            grid=(1,),
-            in_specs=[pl.BlockSpec(memory_space=pl.ANY)] * (len(turned) + len(flat)),
-            out_specs=[pl.BlockSpec(shape, lambda k, line: (0, 0, 0))] * lines,
-            scratch_shapes=[
-                pltpu.VMEM((pieces, depth, rows), bf16),
-                pltpu.VMEM((pieces, rows, width), bf16),
-                pltpu.VMEM((steps, lines, share, width), jnp.float32),
-                pltpu.SemaphoreType.DMA((pieces, 2)),
-            ],
-        ),
-        out_shape=[jax.ShapeDtypeStruct(shape, jnp.float32)]
-        + [jax.ShapeDtypeStruct(shape, bf16)] * (lines - 1),
+    )(take, arrived_q, arrived_k, packed_v, out_grad, doc_ids, doc_ids.reshape(rows, 1), *done)
+
+
+def weight_kernel(send, turned_ref, landed_ref, swapped_ref, out_ref, home):
+    rows = home.shape[0] // 2
+
+    @pl.when(pl.program_id(0) == 0)
+    def _():
+        for b in range(rows // BLOCK_ROWS):
+            place = slice(b * BLOCK_ROWS, (b + 1) * BLOCK_ROWS)
+            home[place, :] = landed_ref[send[0, b]]
+        for b in range(rows // BLOCK_ROWS):
+            place = slice(rows + b * BLOCK_ROWS, rows + (b + 1) * BLOCK_ROWS)
+            home[place, :] = swapped_ref[send[1, b]]
+
+    part = jnp.dot(turned_ref[...], home[...], preferred_element_type=jnp.float32)
+    columns, share, inner, width = out_ref.shape
+    part = part.reshape(share, columns, inner, width).astype(out_ref.dtype)
+    for i in range(share):
+        out_ref[:, i] = part[i]
+
+
+def weight_part(send, turned, landed, swapped, columns, steps):
+    depth, rows = turned.shape
+    peers, _, width = landed.shape
+    inner = depth // steps // columns
+    share = 4
+    tile = share * inner * columns
+    return pl.pallas_call(
+        weight_kernel,
+        grid_spec=pltpu.PrefetchScalarGridSpec(
+            num_scalar_prefetch=1,
+            grid=(steps // share,),
+            in_specs=[
+                pl.BlockSpec((tile, rows), lambda z, send: (z, 0)),
+                pl.BlockSpec((peers, BLOCK_ROWS, width), lambda z, send: (0, 0, 0)),
+                pl.BlockSpec((peers, BLOCK_ROWS, width), lambda z, send: (0, 0, 0)),
+            ],
+            out_specs=pl.BlockSpec((columns, share, inner, width), lambda z, send: (0, z, 0, 0)),
+            scratch_shapes=[pltpu.VMEM((rows, width), jnp.bfloat16)],
+        ),
+        out_shape=jax.ShapeDtypeStruct((columns, steps, inner, width), jnp.bfloat16),
         name="weight_part",
-    )(line, *turned, *flat)
+    )(send, turned, landed, swapped)
 
 
 def ring(count, step, stride=1):
@@ -414,8 +419,12 @@
     def which(table, devices):
         return jnp.sum(jnp.where(table[None, :] == devices[:, None], number + 1, 0), axis=1) - 1
 
-    slots = outgoing_slots(send, queries, key_rows, dp_count)
-    arrived = lax.all_to_all(slots, "dp", 0, 0, tiled=True)
+    wide = queries.shape[1] // 2
+    keys = key_rows.shape[1]
+    slots = outgoing_slots(send, [(queries, wide, 0), (key_rows, keys, 0)], dp_count)
+    arrived_one = lax.all_to_all(slots, "dp", 0, 0, tiled=True)
+    slots = outgoing_slots(send, [(queries, wide, 1)], dp_count)
+    arrived_two = lax.all_to_all(slots, "dp", 0, 0, tiled=True)
 
     width = value_weight.shape[1] // 2
     half = lax.dynamic_slice_in_dim(value_weight, core * width, width, axis=1)
@@ -429,8 +438,7 @@
     origin = (plane_at + planes - hop_steps) % planes * 2
     origin = jnp.concatenate([origin + core, origin + 1 - core])
     block = jnp.maximum(which(send, onward), 0)
-    back_block = jnp.maximum(which(take, onward), 0)
-    place, home_place = which(take, origin), which(send, origin)
+    place = which(take, origin)
     leaving = value_blocks(core_of, block, normed, own, other)
     landed = along_z(leaving)
     (swapped,) = swap([jnp.stack(landed)])
@@ -438,32 +446,31 @@
 
     column = 2 * jnp.arange(planes, dtype=jnp.int32)
     tile = depth // dp_count
-    x_line = (x + jnp.arange(side, dtype=jnp.int32)) % side
-    columns = jnp.concatenate([column + core, column + 1 - core])
-    turned = turn_columns(columns, x_line, normed, tile)
-    turned = [along_x(a, d) if d else a for d, a in enumerate(turned)]
-
-    query_grad, key_grad, value_grad, *returning = attention(
-        take, back_block, arrived, packed_v, out_grad, doc_ids
+    picked = pick_columns(column + 1 - core, normed, tile)
+    (got,) = swap([picked])
+    turned = turn_columns(column + core, normed, got, tile)
+    (partner,) = swap([send_to])
+    sends = jnp.concatenate([send_to, partner], axis=0)
+
+    half_groups = KV_HEADS // 2
+    key_at = wide // HEAD_DIM
+    done = attention(
+        take, arrived_one, arrived_one, packed_v, out_grad, doc_ids,
+        0, half_groups, key_at, (),
     )
-    landed = along_z(returning)
-    (swapped,) = swap([jnp.stack(landed)])
-    home = pack(core_of, home_place, landed, swapped, rows)
-    cut = rows // 2
-    before, after = along_x(home, 1), along_x(home, -1)
-    top, low = along_x(before[:cut], 1), along_x(after[cut:], -1)
-    homes = [(home,), (before,), (top, low), (after,)]
-    homes += [tuple(swap(parts)) for parts in homes]
-    theirs = jnp.concatenate([a[a.shape[0] // 2 :] for a in turned])
-    turned += swap([theirs])
-
-    y_line = (y + jnp.arange(side, dtype=jnp.int32)) % side
-    stay, *leave = weight_part(y_line, turned, homes, planes)
-    leave = [along_y(a, d + 1) for d, a in enumerate(leave)]
-    plane = (stay + sum(a.astype(jnp.float32) for a in leave)).astype(jnp.bfloat16)
+    query_grad, key_grad, value_grad, returning = attention(
+        take, arrived_two, arrived_one, packed_v, out_grad, doc_ids,
+        half_groups, half_groups, key_at, done,
+    )
+    landed = lax.all_to_all(returning, "dp", 0, 0, tiled=True)
+    (swapped,) = swap([landed])
+    input_grad = input_gradient(core_of, value_grad, own, other)
+
+    chip = weight_part(sends, turned, landed, swapped, fsdp_count, planes)
+    chips = lax.all_to_all(chip, "fsdp", 0, 0, tiled=True)
+    plane = jnp.sum(chips.astype(jnp.float32), axis=0).astype(jnp.bfloat16)
     groups = [list(range(c, dp_count, 2)) for c in range(2)]
     parts = lax.all_to_all(plane, "dp", 0, 0, axis_index_groups=groups, tiled=True)
-    input_grad = input_gradient(core_of, value_grad, own, other)
     weight_grad = jnp.sum(parts.astype(jnp.float32), axis=0) * grad_scale
     return (query_grad, key_grad, input_grad, weight_grad)
 

time: 252 us -> 254 us (level)
  blocking collectives: 0 us -> 34.7 us
  starting transfers between devices: 73 us -> 53.9 us
  waiting for transfers between devices: 95.5 us -> 78 us
  Pallas kernels: 58.6 us -> 65.3 us
    all_to_all x0 -> x1, blocking collectives: none -> 34.7 us  [local(): chips = lax.all_to_all(chip, 'fsdp', 0, 0, tiled=True)]
    all_to_all x1 -> x3, waiting for transfers between devices: 0.01 us -> 28.9 us  [the longest x1 15.3 us: local(): arrived_one = lax.all_to_all(slots, 'dp', 0, 0, tiled=True)]
    ppermute x14 -> x7, waiting for transfers between devices: 49.8 us -> 30.4 us  [along_z(): lax.ppermute(a, 'dp', ring((dp_count, planes), d, 2))]
    ppermute x14 -> x7, starting transfers between devices: 32.3 us -> 18.1 us  [along_z(): lax.ppermute(a, 'dp', ring((dp_count, planes), d, 2))]
    ppermute x11 -> x4, waiting for transfers between devices: 16.1 us -> 2.22 us  [along_x(): return lax.ppermute(array, 'fsdp', ring((fsdp_count, side), step, side))]
    ppermute x7 -> x4, waiting for transfers between devices: 24.2 us -> 13 us  [along_y(): return lax.ppermute(array, 'fsdp', ring((fsdp_count, side), step, 1))]
    ppermute x11 -> x4, starting transfers between devices: 17.4 us -> 6.7 us  [along_x(): return lax.ppermute(array, 'fsdp', ring((fsdp_count, side), step, side))]
    all_to_all x1 -> x3, starting transfers between devices: 6.92 us -> 16.2 us  [the longest x1 6.86 us: local(): arrived_one = lax.all_to_all(slots, 'dp', 0, 0, tiled=True)]
  transfers between devices with their start and end apart: 43 -> 24, of which waited for: 23 -> 13; matrix products, arithmetic and copies ran while one was open for 5% -> 5% of each run, Pallas kernels for 15% -> 20%
where the time goes in v4:
time: 254 us; the launch traced here: 251 us
  waiting for transfers between devices  78 us (31%)
  Pallas kernels  65.3 us (26%)
  starting transfers between devices  53.9 us (21%)
  blocking collectives  34.7 us (14%)
  local copies, waits for them, and re-layouts  13.5 us (5%)
  other arithmetic  4.67 us (2%)
    all_to_all x1, blocking collectives, local(): chips = lax.all_to_all(chip, 'fsdp', 0, 0, tiled=True)  34.7 us
    ppermute x7, waiting for transfers between devices, along_z(): lax.ppermute(a, 'dp', ring((dp_count, planes), d, 2))  30.4 us
    ppermute x7, starting transfers between devices, along_z(): lax.ppermute(a, 'dp', ring((dp_count, planes), d, 2))  18.1 us
    pallas_call x2, Pallas kernels, attention(): pl.pallas_call(attention_kernel, grid_spec=pltpu.PrefetchScalarGridSpec(n...  17.2 us
    all_to_all x1, waiting for transfers between devices, local(): arrived_one = lax.all_to_all(slots, 'dp', 0, 0, tiled=True)  15.3 us
    all_to_all x1, waiting for transfers between devices, local(): landed = lax.all_to_all(returning, 'dp', 0, 0, tiled=True)  13.6 us
    ppermute x4, waiting for transfers between devices, along_y(): return lax.ppermute(array, 'fsdp', ring((fsdp_count, side), step, 1))  13 us
    pallas_call x2, Pallas kernels, outgoing_slots(): pl.pallas_call(outgoing_kernel, grid_spec=pltpu.PrefetchScalarGridSpec(nu...  11.5 us
  transfers between devices with their start and end apart: 24, of which 13 were waited for; matrix products, arithmetic and copies ran while one was open for 5% of the time, Pallas kernels for 20%

profile of v4, /device:TPU:0, one launch (start us, length us, event | category | flops | bytes accessed | tf_op | source)
XLA Modules:
  0.0 251.2 jit_solution(10085372666868224965)
XLA Ops:
  0.7 0.9 bitcast_dynamic-update-slice_fusion.7
  1.8 3.2 %collective-permute-start.2 = (bf16[256,256]{1,0:T(8,128)(2,1)S(1)}, bf16[256,256]{1,0:T(8,128)(2,1)S(1)}, u32[]{:S(2)}, u32[]{:S(2)}) collective-permute-start(bf16[256,256]{1,0:T(8,128)(2,1)S(1)} %get-tuple-element.39), channel_id=1, source_target_pairs={{0,12},{1,13},{2,14},{3,15},{4,0},{5,1},{6,2},{7,3},{8,4},{9,5},{1... | collective-permute-start | bytes 393224 | tf_op jit(solution)/shard_map/ppermute | solution.py:414
  5.0 5.8 %outgoing_slots.3 = bf16[16,48,1536]{2,1,0:T(8,128)(2,1)} custom-call(s32[8]{0:T(128)} %bitcast.52, bf16[384,2048]{1,0:T(8,128)(2,1)} %refs_0_.3, bf16[384,512]{1,0:T(8,128)(2,1)} %refs_1_.1), custom_call_target="tpu_custom_call" | custom-call | tf_op jit(solution)/shard_map/outgoing_slots/pallas_call | solution.py:29
  10.8 6.9 %all-to-all-start.1 = ((bf16[16,48,1536]{2,1,0:T(8,128)(2,1)}), bf16[16,48,1536]{2,1,0:T(8,128)(2,1)S(1)}, u32[]{:S(2)}, u32[]{:S(2)}) async-start(bf16[16,48,1536]{2,1,0:T(8,128)(2,1)} %outgoing_slots.3), calls=%async_computation.1 | async-start | bytes 4718592 | tf_op jit(solution)/shard_map/all_to_all | solution.py:425
  18.1 3.0 %collective-permute-start.3 = (bf16[128,256]{1,0:T(8,128)(2,1)S(1)}, bf16[128,256]{1,0:T(8,128)(2,1)S(1)}, u32[]{:S(2)}, u32[]{:S(2)}) collective-permute-start(bf16[128,256]{1,0:T(8,128)(2,1)S(1)} %slice.17), channel_id=1, source_target_pairs={{0,12},{1,13},{2,14},{3,15},{4,0},{5,1},{6,2},{7,3},{8,4},{9,5},{1... | collective-permute-start | bytes 196616 | tf_op jit(solution)/shard_map/ppermute | solution.py:414
  21.2 2.2 collective-permute-done.1
  23.5 1.7 collective-permute-start.4
  25.1 1.7 collective-permute-start.6
  26.8 11.5 %collective-permute-done.4 = bf16[4,256,256]{2,1,0:T(8,128)(2,1)} collective-permute-done((bf16[4,256,256]{2,1,0:T(8,128)(2,1)S(1)}, bf16[4,256,256]{2,1,0:T(8,128)(2,1)}, u32[]{:S(2)}, u32[]{:S(2)}) %collective-permute-start.4) | collective-permute-done | bytes 524320 | tf_op jit(solution)/shard_map/ppermute | solution.py:417
  38.2 1.0 slice.18
  39.6 1.6 broadcast_in_dim.53
  41.2 0.8 bitcast_dynamic-update-slice_fusion.1
  42.0 3.0 %collective-permute-start.7 = (bf16[2,256,256]{2,1,0:T(8,128)(2,1)S(1)}, bf16[2,256,256]{2,1,0:T(8,128)(2,1)S(1)}, u32[]{:S(2)}, u32[]{:S(2)}) collective-permute-start(bf16[2,256,256]{2,1,0:T(8,128)(2,1)S(1)} %slice.19), channel_id=1, source_target_pairs={{0,3},{1,0},{2,1},{3,2},{4,7},{5,4},{6,5},{7,6},{8,11},{9,8},{10,9... | collective-permute-start | bytes 786440 | tf_op jit(solution)/shard_map/ppermute | solution.py:417
  45.0 1.9 bitcast_dynamic-update-slice_fusion
  48.1 1.0 collective-permute-done.7
  49.9 0.8 bitcast_dynamic-update-slice_fusion.2
  50.7 5.7 %outgoing_slots.2 = bf16[16,48,1024]{2,1,0:T(8,128)(2,1)} custom-call(s32[8]{0:T(128)} %bitcast.53, bf16[384,2048]{1,0:T(8,128)(2,1)} %refs_0_.3), custom_call_target="tpu_custom_call" | custom-call | tf_op jit(solution)/shard_map/outgoing_slots/pallas_call | solution.py:29
  57.3 15.3 %all-to-all-done.1.q_ref.k_ref = bf16[16,48,1536]{2,1,0:T(8,128)(2,1)S(1)} async-done(((bf16[16,48,1536]{2,1,0:T(8,128)(2,1)}), bf16[16,48,1536]{2,1,0:T(8,128)(2,1)S(1)}, u32[]{:S(2)}, u32[]{:S(2)}) %all-to-all-start.1) | async-done | bytes 2359328 | tf_op jit(solution)/shard_map/all_to_all | solution.py:425
  72.6 4.6 %all-to-all-start = ((bf16[16,48,1024]{2,1,0:T(8,128)(2,1)}), bf16[16,48,1024]{2,1,0:T(8,128)(2,1)}, u32[]{:S(2)}, u32[]{:S(2)}) async-start(bf16[16,48,1024]{2,1,0:T(8,128)(2,1)} %outgoing_slots.2), calls=%async_computation | async-start | bytes 3145728 | tf_op jit(solution)/shard_map/all_to_all | solution.py:427
  77.3 6.6 %value_blocks.1 = (bf16[2,48,512]{2,1,0:T(8,128)(2,1)}, bf16[2,48,512]{2,1,0:T(8,128)(2,1)}, bf16[2,48,512]{2,1,0:T(8,128)(2,1)}, bf16[2,48,512]{2,1,0:T(8,128)(...) custom-call(s32[1]{0:T(128)} %bitcast.2.core, ...), custom_call_target="tpu_custom_call" | custom-call | flops 1610612736 | bytes 7340032 | tf_op jit(solution)/shard_map/value_blocks/pallas_call | solution.py:78
  83.9 5.9 %collective-permute-start.9 = (bf16[2,48,512]{2,1,0:T(8,128)(2,1)}, bf16[2,48,512]{2,1,0:T(8,128)(2,1)S(1)}, u32[]{:S(2)}, u32[]{:S(2)}) collective-permute-start(bf16[2,48,512]{2,1,0:T(8,128)(2,1)} %get-tuple-element.20), channel_id=1, source_target_pairs={{0,128},{16,144},{32,160},{48,176},{64,192},{80,208},{96,224},{112... | collective-permute-start | bytes 294920 | tf_op jit(solution)/shard_map/ppermute | solution.py:406
  90.3 4.5 %collective-permute-start.11 = (bf16[2,48,512]{2,1,0:T(8,128)(2,1)}, bf16[2,48,512]{2,1,0:T(8,128)(2,1)S(1)}, u32[]{:S(2)}, u32[]{:S(2)}) collective-permute-start(bf16[2,48,512]{2,1,0:T(8,128)(2,1)} %get-tuple-element.22), channel_id=1, source_target_pairs={{0,160},{16,176},{32,192},{48,208},{64,224},{80,240},{96,0},{112,1... | collective-permute-start | bytes 294920 | tf_op jit(solution)/shard_map/ppermute | solution.py:406
  95.3 3.6 %collective-permute-start.13 = (bf16[2,48,512]{2,1,0:T(8,128)(2,1)}, bf16[2,48,512]{2,1,0:T(8,128)(2,1)S(1)}, u32[]{:S(2)}, u32[]{:S(2)}) collective-permute-start(bf16[2,48,512]{2,1,0:T(8,128)(2,1)} %get-tuple-element.24), channel_id=1, source_target_pairs={{0,192},{16,208},{32,224},{48,240},{64,0},{80,16},{96,32},{112,48}... | collective-permute-start | bytes 294920 | tf_op jit(solution)/shard_map/ppermute | solution.py:406
  98.9 27.5 %collective-permute-done.9.refs_0_ = bf16[2,48,512]{2,1,0:T(8,128)(2,1)S(1)} collective-permute-done((bf16[2,48,512]{2,1,0:T(8,128)(2,1)}, bf16[2,48,512]{2,1,0:T(8,128)(2,1)S(1)}, u32[]{:S(2)}, u32[]{:S(2)}) %collective-permute-start.9) | collective-permute-done | bytes 98336 | tf_op jit(solution)/shard_map/ppermute | solution.py:406
  126.7 3.1 %collective-permute-start.15 = (bf16[2,48,512]{2,1,0:T(8,128)(2,1)}, bf16[2,48,512]{2,1,0:T(8,128)(2,1)S(1)}, u32[]{:S(2)}, u32[]{:S(2)}) collective-permute-start(bf16[2,48,512]{2,1,0:T(8,128)(2,1)} %get-tuple-element.26), channel_id=1, source_target_pairs={{0,224},{16,240},{32,0},{48,16},{64,32},{80,48},{96,64},{112,80},{... | collective-permute-start | bytes 294920 | tf_op jit(solution)/shard_map/ppermute | solution.py:406
  129.8 1.3 collective-permute-done.12.refs_3_
  131.1 1.3 collective-permute-done.14.refs_5_
  132.5 0.9 bitcast_dynamic-update-slice_fusion.8
  133.5 0.8 copy.32.doc_col
  134.8 0.9 collective-permute-done.16.refs_8_
  135.8 0.9 copy-done.3
  136.7 3.1 %shard_map.120.v_ref = bf16[384,512]{1,0:T(8,128)(2,1)} custom-call(s32[1]{0:T(128)} %bitcast.2.core, s32[16]{0:T(128)} %broadcast_add_fusion.place, bf16[2,48,512]{2,1,0:T(8,128)(2,1)} %copy-done.5, bf16[2,48,512]{2,1,0:T(8,128)(2,1)} %copy-done.6, bf16[2,48,512]{2,1,0:T(8,128)(2,1)} %copy-done.7, bf16[2,48,512]{2,1,0:T(8,128)(2,1)} %copy-done.8, ...), custom_call_target="tpu_custom_call" | custom-call | tf_op jit(solution)/shard_map/pallas_call | solution.py:116
  139.8 8.6 %attention_backward.2 = (bf16[384,2048]{1,0:T(8,128)(2,1)}, bf16[384,512]{1,0:T(8,128)(2,1)}, bf16[384,512]{1,0:T(8,128)(2,1)}, bf16[16,48,512]{2,1,0:T(8,128)(2,1)}) custom-call(s32[8]{0:T(128)} %bitcast.55, bf16[16,48,1536]{2,1,0:T(8,128)(2,1)} %copy-done, bf16[16,48,1536]{2,1,0:T(8,128)(2,1)} %copy-done, bf16[384,512]{1,0:T(8,128)(2,1)} %shard_map.120.v_ref, ...), custom_call_target="tpu_custom_call" | custom-call | flops 1811939328 | bytes 3932160 | tf_op jit(solution)/shard_map/attention_backward/pallas_call | solution.py:276
  148.4 8.6 %attention_backward.3 = (bf16[384,2048]{1,0:T(8,128)(2,1)}, bf16[384,512]{1,0:T(8,128)(2,1)}, bf16[384,512]{1,0:T(8,128)(2,1)}, bf16[16,48,512]{2,1,0:T(8,128)(2,1)}) custom-call(s32[8]{0:T(128)} %bitcast.56, bf16[16,48,1024]{2,1,0:T(8,128)(2,1)} %all-to-all-done.q_ref, ...), custom_call_target="tpu_custom_call", output_to_operand_aliasing={{0}: (7, {}), {1}: (8, {}), {2}: (9, {}), {3}: (10, {})} | custom-call | flops 1811939328 | bytes 3932160 | tf_op jit(solution)/shard_map/attention_backward/pallas_call | solution.py:276
  157.0 4.7 %all-to-all-start.2 = ((bf16[16,48,512]{2,1,0:T(8,128)(2,1)}), bf16[16,48,512]{2,1,0:T(8,128)(2,1)S(1)}, u32[]{:S(2)}, u32[]{:S(2)}) async-start(bf16[16,48,512]{2,1,0:T(8,128)(2,1)} %get-tuple-element.35), calls=%async_computation.2 | async-start | bytes 1572864 | tf_op jit(solution)/shard_map/all_to_all | solution.py:465
  162.3 6.1 %pick_columns.1 = bf16[384,2048]{1,0:T(8,128)(2,1)} custom-call(s32[8]{0:T(128)} %add_subtract_fusion.column, bf16[384,4096]{1,0:T(8,128)(2,1)} %own_ref.1), custom_call_target="tpu_custom_call" | custom-call | tf_op jit(solution)/shard_map/pick_columns/pallas_call | solution.py:136
  168.8 13.6 %all-to-all-done.2.landed_ref = bf16[16,48,512]{2,1,0:T(8,128)(2,1)S(1)} async-done(((bf16[16,48,512]{2,1,0:T(8,128)(2,1)}), bf16[16,48,512]{2,1,0:T(8,128)(2,1)S(1)}, u32[]{:S(2)}, u32[]{:S(2)}) %all-to-all-start.2) | async-done | bytes 786464 | tf_op jit(solution)/shard_map/all_to_all | solution.py:465
  182.3 2.5 %collective-permute-start.19 = (bf16[16,48,512]{2,1,0:T(8,128)(2,1)S(1)}, bf16[16,48,512]{2,1,0:T(8,128)(2,1)S(1)}, u32[]{:S(2)}, u32[]{:S(2)}) collective-permute-start(bf16[16,48,512]{2,1,0:T(8,128)(2,1)S(1)} %all-to-all-done.2.landed_ref), channel_id=1, source_target_pairs={{0,16},{16,0},{32,48},{48,32},{64,80},{80,64},{96,112},{112,96},{1... | collective-permute-start | bytes 2359304 | tf_op jit(solution)/shard_map/ppermute | solution.py:411
  185.5 1.3 collective-permute-done.17
  187.4 1.2 copy-done.2
  188.5 7.4 %turn_columns.1.turned_ref = bf16[2048,768]{1,0:T(8,128)(2,1)} custom-call(s32[8]{0:T(128)} %fusion.4.column, bf16[384,4096]{1,0:T(8,128)(2,1)} %own_ref.1, bf16[384,2048]{1,0:T(8,128)(2,1)} %copy-done.2), custom_call_target="tpu_custom_call" | custom-call | tf_op jit(solution)/shard_map/turn_columns/pallas_call | solution.py:158
  196.0 0.9 copy-done.4
  196.9 5.6 %weight_part.1 = bf16[16,8,16,512]{3,2,1,0:T(8,128)(2,1)} custom-call(s32[2,8]{1,0:T(2,128)} %pad_add_fusion.send, bf16[2048,768]{1,0:T(8,128)(2,1)} %turn_columns.1.turned_ref, bf16[16,48,512]{2,1,0:T(8,128)(2,1)} %copy-done.1, bf16[16,48,512]{2,1,0:T(8,128)(2,1)} %copy-done.4), custom_call_target="tpu_custom_call" | custom-call | tf_op jit(solution)/shard_map/weight_part/pallas_call | solution.py:345
  202.5 34.7 %all_to_all.25 = bf16[16,8,16,512]{3,2,1,0:T(8,128)(2,1)S(1)} all-to-all(bf16[16,8,16,512]{3,2,1,0:T(8,128)(2,1)} %weight_part.1), channel_id=1, replica_groups=mesh['dp'=16,'fsdp'=16] {'fsdp'}, dimensions={0} | all-to-all | bytes 4194304 | tf_op jit(solution)/shard_map/all_to_all | solution.py:470
  237.2 1.1 reduce_sum.41
  238.2 3.4 %all-to-all-start.4 = ((bf16[8,16,512]{2,1,0:T(8,128)(2,1)}), bf16[8,16,512]{2,1,0:T(8,128)(2,1)S(1)}, u32[]{:S(2)}, u32[]{:S(2)}) async-start(bf16[8,16,512]{2,1,0:T(8,128)(2,1)} %reduce_sum.41), calls=%async_computation.4 | async-start | bytes 262144 | tf_op jit(solution)/shard_map/all_to_all | solution.py:473
  241.6 7.8 %input_gradient.1 = bf16[384,4096]{1,0:T(8,128)(2,1)} custom-call(s32[1]{0:T(128)} %bitcast.2.core, bf16[384,512]{1,0:T(8,128)(2,1)} %get-tuple-element.34.grad_ref, bf16[4096,256]{1,0:T(8,128)(2,1)} %bitcast.18.own_ref, bf16[4096,256]{1,0:T(8,128)(2,1)} %collective-permute-done.8.other_ref), custom_call_target="tpu_custom_call" | custom-call | flops 1610612736 | bytes 7340032 | tf_op jit(solution)/shard_map/input_gradient/pallas_call | solution.py:186
  249.4 1.2 all-to-all-done.4
  (86 shorter events, 8.6 us)
Async XLA Ops:
  1.7 16.1 %collective-permute-start = (bf16[256,256]{1,0:T(8,128)(2,1)S(1)}, bf16[256,256]{1,0:T(8,128)(2,1)S(1)}, u32[]{:S(2)}, u32[]{:S(2)}) collective-permute-start(bf16[256,256]{1,0:T(8,128)(2,1)S(1)} %get-tuple-element.39), channel_id=1, source_target_pairs={{0,4},{1,5},{2,6},{3,7},{4,8},{5,9},{6,10},{7,11},{8,12},{9,13},{1... | collective-permute-start | bytes 393224 | tf_op jit(solution)/shard_map/ppermute | solution.py:414
  1.8 16.4 %collective-permute-start.2 = (bf16[256,256]{1,0:T(8,128)(2,1)S(1)}, bf16[256,256]{1,0:T(8,128)(2,1)S(1)}, u32[]{:S(2)}, u32[]{:S(2)}) collective-permute-start(bf16[256,256]{1,0:T(8,128)(2,1)S(1)} %get-tuple-element.39), channel_id=1, source_target_pairs={{0,12},{1,13},{2,14},{3,15},{4,0},{5,1},{6,2},{7,3},{8,4},{9,5},{1... | collective-permute-start | bytes 393224 | tf_op jit(solution)/shard_map/ppermute | solution.py:414
  10.8 61.8 %all-to-all-start.1 = ((bf16[16,48,1536]{2,1,0:T(8,128)(2,1)}), bf16[16,48,1536]{2,1,0:T(8,128)(2,1)S(1)}, u32[]{:S(2)}, u32[]{:S(2)}) async-start(bf16[16,48,1536]{2,1,0:T(8,128)(2,1)} %outgoing_slots.3), calls=%async_computation.1 | async-start | bytes 4718592 | tf_op jit(solution)/shard_map/all_to_all | solution.py:425
  17.8 5.6 %collective-permute-start.1 = (bf16[128,256]{1,0:T(8,128)(2,1)S(1)}, bf16[128,256]{1,0:T(8,128)(2,1)S(1)}, u32[]{:S(2)}, u32[]{:S(2)}) collective-permute-start(bf16[128,256]{1,0:T(8,128)(2,1)S(1)} %slice.16), channel_id=1, source_target_pairs={{0,4},{1,5},{2,6},{3,7},{4,8},{5,9},{6,10},{7,11},{8,12},{9,13},{1... | collective-permute-start | bytes 196616 | tf_op jit(solution)/shard_map/ppermute | solution.py:414
  18.1 5.3 %collective-permute-start.3 = (bf16[128,256]{1,0:T(8,128)(2,1)S(1)}, bf16[128,256]{1,0:T(8,128)(2,1)S(1)}, u32[]{:S(2)}, u32[]{:S(2)}) collective-permute-start(bf16[128,256]{1,0:T(8,128)(2,1)S(1)} %slice.17), channel_id=1, source_target_pairs={{0,12},{1,13},{2,14},{3,15},{4,0},{5,1},{6,2},{7,3},{8,4},{9,5},{1... | collective-permute-start | bytes 196616 | tf_op jit(solution)/shard_map/ppermute | solution.py:414
  23.5 14.8 %collective-permute-start.4 = (bf16[4,256,256]{2,1,0:T(8,128)(2,1)S(1)}, bf16[4,256,256]{2,1,0:T(8,128)(2,1)}, u32[]{:S(2)}, u32[]{:S(2)}) collective-permute-start(bf16[4,256,256]{2,1,0:T(8,128)(2,1)S(1)} %bitcast_dynamic-update-slice_fusion.5), channel_id=1, source_target_pairs={{0,1},{1,2},{2,3},{3,0},{4,5},{5,6},{6,7},{7,4},{8,9},{9,10},{10,1... | collective-permute-start | bytes 1572872 | tf_op jit(solution)/shard_map/ppermute | solution.py:417
  25.1 16.9 %collective-permute-start.6 = (bf16[4,256,256]{2,1,0:T(8,128)(2,1)S(1)}, bf16[4,256,256]{2,1,0:T(8,128)(2,1)S(1)}, u32[]{:S(2)}, u32[]{:S(2)}) collective-permute-start(bf16[4,256,256]{2,1,0:T(8,128)(2,1)S(1)} %bitcast_dynamic-update-slice_fusion.5), channel_id=1, source_target_pairs={{0,3},{1,0},{2,1},{3,2},{4,7},{5,4},{6,5},{7,6},{8,11},{9,8},{10,9... | collective-permute-start | bytes 1572872 | tf_op jit(solution)/shard_map/ppermute | solution.py:417
  39.2 8.2 %collective-permute-start.5 = (bf16[2,256,256]{2,1,0:T(8,128)(2,1)S(1)}, bf16[2,256,256]{2,1,0:T(8,128)(2,1)S(1)}, u32[]{:S(2)}, u32[]{:S(2)}) collective-permute-start(bf16[2,256,256]{2,1,0:T(8,128)(2,1)S(1)} %slice.18), channel_id=1, source_target_pairs={{0,1},{1,2},{2,3},{3,0},{4,5},{5,6},{6,7},{7,4},{8,9},{9,10},{10,1... | collective-permute-start | bytes 786440 | tf_op jit(solution)/shard_map/ppermute | solution.py:417
  42.0 7.1 %collective-permute-start.7 = (bf16[2,256,256]{2,1,0:T(8,128)(2,1)S(1)}, bf16[2,256,256]{2,1,0:T(8,128)(2,1)S(1)}, u32[]{:S(2)}, u32[]{:S(2)}) collective-permute-start(bf16[2,256,256]{2,1,0:T(8,128)(2,1)S(1)} %slice.19), channel_id=1, source_target_pairs={{0,3},{1,0},{2,1},{3,2},{4,7},{5,4},{6,5},{7,6},{8,11},{9,8},{10,9... | collective-permute-start | bytes 786440 | tf_op jit(solution)/shard_map/ppermute | solution.py:417
  49.9 6.5 %copy-start.16 = (s32[8]{0:T(128)S(1)}, s32[8]{0:T(128)}, u32[]{:S(2)}) copy-start(s32[8]{0:T(128)} %constant.141.clone) | copy-start | bytes 100
  49.9 6.7 %copy-start.15 = (s32[8]{0:T(128)S(1)}, s32[8]{0:T(128)}, u32[]{:S(2)}) copy-start(s32[8]{0:T(128)} %constant.149) | copy-start | bytes 100
  49.9 6.8 %copy-start.13 = (s32[1,8]{1,0:T(1,128)S(1)}, s32[1,8]{1,0:T(1,128)}, u32[]{:S(2)}) copy-start(s32[1,8]{1,0:T(1,128)} %param.15) | copy-start | bytes 100
  49.9 6.8 %copy-start.14 = (s32[1,8]{1,0:T(1,128)S(1)}, s32[1,8]{1,0:T(1,128)}, u32[]{:S(2)}) copy-start(s32[1,8]{1,0:T(1,128)} %param.16) | copy-start | bytes 100
  50.7 26.5 %collective-permute-start.8 = (bf16[4096,256]{1,0:T(8,128)(2,1)}, bf16[4096,256]{1,0:T(8,128)(2,1)}, u32[]{:S(2)}, u32[]{:S(2)}) collective-permute-start(bf16[4096,256]{1,0:T(8,128)(2,1)} %bitcast.18.own_ref), channel_id=1, source_target_pairs={{0,16},{16,0},{32,48},{48,32},{64,80},{80,64},{96,112},{112,96},{1... | collective-permute-start | bytes 6291464 | tf_op jit(solution)/shard_map/ppermute | solution.py:411
  72.6 11.2 %copy-start = (bf16[16,48,1536]{2,1,0:T(8,128)(2,1)}, bf16[16,48,1536]{2,1,0:T(8,128)(2,1)S(1)}, u32[]{:S(2)}) copy-start(bf16[16,48,1536]{2,1,0:T(8,128)(2,1)S(1)} %all-to-all-done.1.q_ref.k_ref) | copy-start | bytes 7077892
  72.6 75.8 %all-to-all-start = ((bf16[16,48,1024]{2,1,0:T(8,128)(2,1)}), bf16[16,48,1024]{2,1,0:T(8,128)(2,1)}, u32[]{:S(2)}, u32[]{:S(2)}) async-start(bf16[16,48,1024]{2,1,0:T(8,128)(2,1)} %outgoing_slots.2), calls=%async_computation | async-start | bytes 3145728 | tf_op jit(solution)/shard_map/all_to_all | solution.py:427
  77.3 56.2 %copy-start.12 = (s32[1,384]{1,0:T(1,128)S(1)}, s32[1,384]{1,0:T(1,128)}, u32[]{:S(2)}) copy-start(s32[1,384]{1,0:T(1,128)} %doc_row.3) | copy-start | bytes 4612
  83.9 42.6 %collective-permute-start.9 = (bf16[2,48,512]{2,1,0:T(8,128)(2,1)}, bf16[2,48,512]{2,1,0:T(8,128)(2,1)S(1)}, u32[]{:S(2)}, u32[]{:S(2)}) collective-permute-start(bf16[2,48,512]{2,1,0:T(8,128)(2,1)} %get-tuple-element.20), channel_id=1, source_target_pairs={{0,128},{16,144},{32,160},{48,176},{64,192},{80,208},{96,224},{112... | collective-permute-start | bytes 294920 | tf_op jit(solution)/shard_map/ppermute | solution.py:406
  89.7 37.0 %collective-permute-start.10 = (bf16[2,48,512]{2,1,0:T(8,128)(2,1)}, bf16[2,48,512]{2,1,0:T(8,128)(2,1)S(1)}, u32[]{:S(2)}, u32[]{:S(2)}) collective-permute-start(bf16[2,48,512]{2,1,0:T(8,128)(2,1)} %get-tuple-element.21), channel_id=1, source_target_pairs={{0,96},{16,112},{32,128},{48,144},{64,160},{80,176},{96,192},{112,... | collective-permute-start | bytes 294920 | tf_op jit(solution)/shard_map/ppermute | solution.py:406
  90.3 39.5 %collective-permute-start.11 = (bf16[2,48,512]{2,1,0:T(8,128)(2,1)}, bf16[2,48,512]{2,1,0:T(8,128)(2,1)S(1)}, u32[]{:S(2)}, u32[]{:S(2)}) collective-permute-start(bf16[2,48,512]{2,1,0:T(8,128)(2,1)} %get-tuple-element.22), channel_id=1, source_target_pairs={{0,160},{16,176},{32,192},{48,208},{64,224},{80,240},{96,0},{112,1... | collective-permute-start | bytes 294920 | tf_op jit(solution)/shard_map/ppermute | solution.py:406
  94.8 36.3 %collective-permute-start.12 = (bf16[2,48,512]{2,1,0:T(8,128)(2,1)}, bf16[2,48,512]{2,1,0:T(8,128)(2,1)S(1)}, u32[]{:S(2)}, u32[]{:S(2)}) collective-permute-start(bf16[2,48,512]{2,1,0:T(8,128)(2,1)} %get-tuple-element.23), channel_id=1, source_target_pairs={{0,64},{16,80},{32,96},{48,112},{64,128},{80,144},{96,160},{112,17... | collective-permute-start | bytes 294920 | tf_op jit(solution)/shard_map/ppermute | solution.py:406
  95.3 35.8 %collective-permute-start.13 = (bf16[2,48,512]{2,1,0:T(8,128)(2,1)}, bf16[2,48,512]{2,1,0:T(8,128)(2,1)S(1)}, u32[]{:S(2)}, u32[]{:S(2)}) collective-permute-start(bf16[2,48,512]{2,1,0:T(8,128)(2,1)} %get-tuple-element.24), channel_id=1, source_target_pairs={{0,192},{16,208},{32,224},{48,240},{64,0},{80,16},{96,32},{112,48}... | collective-permute-start | bytes 294920 | tf_op jit(solution)/shard_map/ppermute | solution.py:406
  126.4 9.3 %copy-start.5 = (bf16[2,48,512]{2,1,0:T(8,128)(2,1)}, bf16[2,48,512]{2,1,0:T(8,128)(2,1)S(1)}, u32[]{:S(2)}) copy-start(bf16[2,48,512]{2,1,0:T(8,128)(2,1)S(1)} %collective-permute-done.9.refs_0_) | copy-start | bytes 294916
  126.4 6.0 %collective-permute-start.14 = (bf16[2,48,512]{2,1,0:T(8,128)(2,1)}, bf16[2,48,512]{2,1,0:T(8,128)(2,1)S(1)}, u32[]{:S(2)}, u32[]{:S(2)}) collective-permute-start(bf16[2,48,512]{2,1,0:T(8,128)(2,1)} %get-tuple-element.25), channel_id=1, source_target_pairs={{0,32},{16,48},{32,64},{48,80},{64,96},{80,112},{96,128},{112,144}... | collective-permute-start | bytes 294920 | tf_op jit(solution)/shard_map/ppermute | solution.py:406
  126.7 9.0 %copy-start.6 = (bf16[2,48,512]{2,1,0:T(8,128)(2,1)}, bf16[2,48,512]{2,1,0:T(8,128)(2,1)S(1)}, u32[]{:S(2)}) copy-start(bf16[2,48,512]{2,1,0:T(8,128)(2,1)S(1)} %collective-permute-done.10.refs_1_) | copy-start | bytes 294916
  126.7 5.8 %collective-permute-start.15 = (bf16[2,48,512]{2,1,0:T(8,128)(2,1)}, bf16[2,48,512]{2,1,0:T(8,128)(2,1)S(1)}, u32[]{:S(2)}, u32[]{:S(2)}) collective-permute-start(bf16[2,48,512]{2,1,0:T(8,128)(2,1)} %get-tuple-element.26), channel_id=1, source_target_pairs={{0,224},{16,240},{32,0},{48,16},{64,32},{80,48},{96,64},{112,80},{... | collective-permute-start | bytes 294920 | tf_op jit(solution)/shard_map/ppermute | solution.py:406
  129.8 6.0 %copy-start.7 = (bf16[2,48,512]{2,1,0:T(8,128)(2,1)}, bf16[2,48,512]{2,1,0:T(8,128)(2,1)S(1)}, u32[]{:S(2)}) copy-start(bf16[2,48,512]{2,1,0:T(8,128)(2,1)S(1)} %collective-permute-done.11.refs_2_) | copy-start | bytes 294916
  131.1 4.7 %copy-start.8 = (bf16[2,48,512]{2,1,0:T(8,128)(2,1)}, bf16[2,48,512]{2,1,0:T(8,128)(2,1)S(1)}, u32[]{:S(2)}) copy-start(bf16[2,48,512]{2,1,0:T(8,128)(2,1)S(1)} %collective-permute-done.12.refs_3_) | copy-start | bytes 294916
  131.1 4.7 %copy-start.9 = (bf16[2,48,512]{2,1,0:T(8,128)(2,1)}, bf16[2,48,512]{2,1,0:T(8,128)(2,1)S(1)}, u32[]{:S(2)}) copy-start(bf16[2,48,512]{2,1,0:T(8,128)(2,1)S(1)} %collective-permute-done.13.refs_4_) | copy-start | bytes 294916
  132.5 3.3 %copy-start.10 = (bf16[2,48,512]{2,1,0:T(8,128)(2,1)}, bf16[2,48,512]{2,1,0:T(8,128)(2,1)S(1)}, u32[]{:S(2)}) copy-start(bf16[2,48,512]{2,1,0:T(8,128)(2,1)S(1)} %collective-permute-done.14.refs_5_) | copy-start | bytes 294916
  132.5 3.3 %copy-start.11 = (bf16[2,48,512]{2,1,0:T(8,128)(2,1)}, bf16[2,48,512]{2,1,0:T(8,128)(2,1)S(1)}, u32[]{:S(2)}) copy-start(bf16[2,48,512]{2,1,0:T(8,128)(2,1)S(1)} %collective-permute-done.15.refs_6_) | copy-start | bytes 294916
  133.5 2.3 collective-permute-start.16
  135.8 0.9 copy-start.3
  157.0 25.3 %all-to-all-start.2 = ((bf16[16,48,512]{2,1,0:T(8,128)(2,1)}), bf16[16,48,512]{2,1,0:T(8,128)(2,1)S(1)}, u32[]{:S(2)}, u32[]{:S(2)}) async-start(bf16[16,48,512]{2,1,0:T(8,128)(2,1)} %get-tuple-element.35), calls=%async_computation.2 | async-start | bytes 1572864 | tf_op jit(solution)/shard_map/all_to_all | solution.py:465
  168.4 19.0 %collective-permute-start.18 = (bf16[384,2048]{1,0:T(8,128)(2,1)}, bf16[384,2048]{1,0:T(8,128)(2,1)S(1)}, u32[]{:S(2)}, u32[]{:S(2)}) collective-permute-start(bf16[384,2048]{1,0:T(8,128)(2,1)} %pick_columns.1), channel_id=1, source_target_pairs={{0,16},{16,0},{32,48},{48,32},{64,80},{80,64},{96,112},{112,96},{1... | collective-permute-start | bytes 4718600 | tf_op jit(solution)/shard_map/ppermute | solution.py:411
  182.3 13.6 %copy-start.1 = (bf16[16,48,512]{2,1,0:T(8,128)(2,1)}, bf16[16,48,512]{2,1,0:T(8,128)(2,1)S(1)}, u32[]{:S(2)}) copy-start(bf16[16,48,512]{2,1,0:T(8,128)(2,1)S(1)} %all-to-all-done.2.landed_ref) | copy-start | bytes 2359300
  182.3 13.6 %collective-permute-start.19 = (bf16[16,48,512]{2,1,0:T(8,128)(2,1)S(1)}, bf16[16,48,512]{2,1,0:T(8,128)(2,1)S(1)}, u32[]{:S(2)}, u32[]{:S(2)}) collective-permute-start(bf16[16,48,512]{2,1,0:T(8,128)(2,1)S(1)} %all-to-all-done.2.landed_ref), channel_id=1, source_target_pairs={{0,16},{16,0},{32,48},{48,32},{64,80},{80,64},{96,112},{112,96},{1... | collective-permute-start | bytes 2359304 | tf_op jit(solution)/shard_map/ppermute | solution.py:411
  184.9 1.9 collective-permute-start.17
  187.4 1.2 copy-start.2
  195.9 0.9 copy-start.4
  238.2 12.4 %all-to-all-start.4 = ((bf16[8,16,512]{2,1,0:T(8,128)(2,1)}), bf16[8,16,512]{2,1,0:T(8,128)(2,1)S(1)}, u32[]{:S(2)}, u32[]{:S(2)}) async-start(bf16[8,16,512]{2,1,0:T(8,128)(2,1)} %reduce_sum.41), calls=%async_computation.4 | async-start | bytes 262144 | tf_op jit(solution)/shard_map/all_to_all | solution.py:473

commit v5 on v4

--- a/solution.py
+++ b/solution.py
@@ -1,3 +1,5 @@
+import functools
+
 import jax
 import jax.numpy as jnp
 from jax import lax
@@ -99,9 +101,9 @@
 
 
 def pack_kernel(core, place, *refs):
-    *own, swapped, out = refs
-    sources = [ref.at[core[0]] for ref in own]
-    sources += [swapped.at[o, core[0]] for o in range(swapped.shape[0])]
+    out = refs[-1]
+    *own, swapped = refs[:-1]
+    sources = [ref.at[core[0]] for ref in own] + [swapped.at[o] for o in range(swapped.shape[0])]
     for o, ref in enumerate(sources):
 
         @pl.when(place[o] >= 0)
@@ -111,7 +113,7 @@
 
 
 def pack(core, place, own, swapped, rows):
-    width = swapped.shape[3]
+    width = swapped.shape[2]
     shape = (2, BLOCK_ROWS, width)
     return pl.pallas_call(
         pack_kernel,
@@ -119,10 +121,11 @@
             num_scalar_prefetch=2,
             grid=(1,),
             in_specs=[pl.BlockSpec(shape, lambda k, *_: (0, 0, 0))] * len(own)
-            + [pl.BlockSpec((len(own),) + shape, lambda k, *_: (0, 0, 0, 0))],
+            + [pl.BlockSpec(swapped.shape, lambda k, *_: (0, 0, 0))],
             out_specs=pl.BlockSpec((rows, width), lambda k, *_: (0, 0)),
         ),
         out_shape=jax.ShapeDtypeStruct((rows, width), swapped.dtype),
+        name="pack_values",
     )(core, place, *own, swapped)
 
 
@@ -205,8 +208,8 @@
     )(core, value_grad, own, other)
 
 
-def attention_kernel(take, q_ref, k_ref, v_ref, grad_ref, doc_row, doc_col, *rest):
-    query_grad, key_grad, value_grad, returning = rest[-9:-5]
+def attention_kernel(kept, take, back_block, q_ref, k_ref, v_ref, grad_ref, doc_row, doc_col, *rest):
+    query_grad, key_grad, value_grad, *returning = rest[kept:-5]
     q_rows, k_rows, bias, key_total, value_total = rest[-5:]
     rows = grad_ref.shape[0]
     blocks = rows // BLOCK_ROWS
@@ -261,38 +264,46 @@
         value_total[:reach, :] += lax.dot_general(half, g, tn, preferred_element_type=jnp.float32)
     key_grad[...] = key_total[...].astype(key_grad.dtype)
     value_grad[...] = value_total[...].astype(value_grad.dtype)
-    returning[...] = jnp.zeros_like(returning)
-    for p in range(blocks):
-        place = slice(p * BLOCK_ROWS, (p + 1) * BLOCK_ROWS)
-        returning[take[p]] = value_total[place, :].astype(returning.dtype)
-
-
-def attention(take, arrived_q, arrived_k, packed_v, out_grad, doc_ids, first, count, key_at, done):
+    if len(returning) > 1:
+        for o, out in enumerate(returning):
+            for c in range(out.shape[0]):
+                first = pl.multiple_of(back_block[2 * o + c] * BLOCK_ROWS, 16)
+                out[c] = value_total[pl.ds(first, BLOCK_ROWS), :].astype(out.dtype)
+    else:
+        for p in range(blocks):
+            place = slice(p * BLOCK_ROWS, (p + 1) * BLOCK_ROWS)
+            returning[0][take[p]] = value_total[place, :].astype(returning[0].dtype)
+
+
+def attention(
+    take, back, arrived_q, arrived_k, packed_v, out_grad, doc_ids, first, count, key_at, done, parts
+):
     peers = arrived_q.shape[0]
     rows = out_grad.shape[0]
     wide = GROUP * HEAD_DIM
     bf16 = jnp.bfloat16
     slot = (peers, BLOCK_ROWS, HEAD_DIM)
-    return pl.pallas_call(
-        attention_kernel,
-        grid_spec=pltpu.PrefetchScalarGridSpec(
-            num_scalar_prefetch=1,
+    part = (peers // parts, BLOCK_ROWS)
+    return pl.pallas_call(
+        functools.partial(attention_kernel, len(done)),
+        grid_spec=pltpu.PrefetchScalarGridSpec(
+            num_scalar_prefetch=2,
             grid=(count,),
             in_specs=[
-                pl.BlockSpec((peers, BLOCK_ROWS, wide), lambda g, take: (0, 0, g)),
-                pl.BlockSpec(slot, lambda g, take: (0, 0, key_at + first + g)),
-                pl.BlockSpec((rows, HEAD_DIM), lambda g, take: (0, first + g)),
-                pl.BlockSpec((rows, wide), lambda g, take: (0, first + g)),
-                pl.BlockSpec((1, rows), lambda g, take: (0, 0)),
-                pl.BlockSpec((rows, 1), lambda g, take: (0, 0)),
+                pl.BlockSpec((peers, BLOCK_ROWS, wide), lambda g, *_: (0, 0, g)),
+                pl.BlockSpec(slot, lambda g, *_: (0, 0, key_at + first + g)),
+                pl.BlockSpec((rows, HEAD_DIM), lambda g, *_: (0, first + g)),
+                pl.BlockSpec((rows, wide), lambda g, *_: (0, first + g)),
+                pl.BlockSpec((1, rows), lambda g, *_: (0, 0)),
+                pl.BlockSpec((rows, 1), lambda g, *_: (0, 0)),
             ]
             + [pl.BlockSpec(memory_space=pl.ANY)] * len(done),
             out_specs=[
-                pl.BlockSpec((rows, wide), lambda g, take: (0, first + g)),
-                pl.BlockSpec((rows, HEAD_DIM), lambda g, take: (0, first + g)),
-                pl.BlockSpec((rows, HEAD_DIM), lambda g, take: (0, first + g)),
-                pl.BlockSpec(slot, lambda g, take: (0, 0, first + g)),
-            ],
+                pl.BlockSpec((rows, wide), lambda g, *_: (0, first + g)),
+                pl.BlockSpec((rows, HEAD_DIM), lambda g, *_: (0, first + g)),
+                pl.BlockSpec((rows, HEAD_DIM), lambda g, *_: (0, first + g)),
+            ]
+            + [pl.BlockSpec(part + (HEAD_DIM,), lambda g, *_: (0, 0, g))] * parts,
             scratch_shapes=[
                 pltpu.VMEM((rows, wide), bf16),
                 pltpu.VMEM((rows, HEAD_DIM), bf16),
@@ -305,29 +316,41 @@
             jax.ShapeDtypeStruct((rows, KV_HEADS * wide), bf16),
             jax.ShapeDtypeStruct((rows, KV_HEADS * HEAD_DIM), bf16),
             jax.ShapeDtypeStruct((rows, KV_HEADS * HEAD_DIM), bf16),
-            jax.ShapeDtypeStruct((peers, BLOCK_ROWS, KV_HEADS * HEAD_DIM), bf16),
-        ],
-        input_output_aliases={7 + i: i for i in range(len(done))},
+        ]
+        + [jax.ShapeDtypeStruct(part + (count * HEAD_DIM,), bf16)] * parts,
+        input_output_aliases={8 + i: i for i in range(len(done))},
         cost_estimate=pl.CostEstimate(
             flops=12 * rows * rows * HEAD_DIM * GROUP * count,
             bytes_accessed=10 * rows * wide * count,
             transcendentals=rows * rows * GROUP * count,
         ),
         name="attention_backward",
-    )(take, arrived_q, arrived_k, packed_v, out_grad, doc_ids, doc_ids.reshape(rows, 1), *done)
-
-
-def weight_kernel(send, turned_ref, landed_ref, swapped_ref, out_ref, home):
+    )(
+        take, back, arrived_q, arrived_k, packed_v, out_grad, doc_ids, doc_ids.reshape(rows, 1),
+        *done,
+    )
+
+
+def weight_kernel(table, core, turned_ref, *refs):
+    *landed, out_ref, home = refs
     rows = home.shape[0] // 2
 
     @pl.when(pl.program_id(0) == 0)
     def _():
-        for b in range(rows // BLOCK_ROWS):
-            place = slice(b * BLOCK_ROWS, (b + 1) * BLOCK_ROWS)
-            home[place, :] = landed_ref[send[0, b]]
-        for b in range(rows // BLOCK_ROWS):
-            place = slice(rows + b * BLOCK_ROWS, rows + (b + 1) * BLOCK_ROWS)
-            home[place, :] = swapped_ref[send[1, b]]
+        if len(landed) == 2:
+            for half in range(2):
+                for b in range(rows // BLOCK_ROWS):
+                    place = slice(half * rows + b * BLOCK_ROWS, half * rows + (b + 1) * BLOCK_ROWS)
+                    home[place, :] = landed[half][table[half, b]]
+        else:
+            for half in range(2):
+                slot = core[0] if half == 0 else 1 - core[0]
+                for o, ref in enumerate(landed):
+
+                    @pl.when(table[half, o] >= 0)
+                    def _():
+                        at = half * rows + table[half, o] * BLOCK_ROWS
+                        home[pl.ds(pl.multiple_of(at, 16), BLOCK_ROWS), :] = ref[slot]
 
     part = jnp.dot(turned_ref[...], home[...], preferred_element_type=jnp.float32)
     columns, share, inner, width = out_ref.shape
@@ -336,28 +359,27 @@
         out_ref[:, i] = part[i]
 
 
-def weight_part(send, turned, landed, swapped, columns, steps):
+def weight_part(table, core, turned, landed, columns, steps):
     depth, rows = turned.shape
-    peers, _, width = landed.shape
+    width = landed[0].shape[2]
     inner = depth // steps // columns
     share = 4
     tile = share * inner * columns
     return pl.pallas_call(
         weight_kernel,
         grid_spec=pltpu.PrefetchScalarGridSpec(
-            num_scalar_prefetch=1,
+            num_scalar_prefetch=2,
             grid=(steps // share,),
-            in_specs=[
-                pl.BlockSpec((tile, rows), lambda z, send: (z, 0)),
-                pl.BlockSpec((peers, BLOCK_ROWS, width), lambda z, send: (0, 0, 0)),
-                pl.BlockSpec((peers, BLOCK_ROWS, width), lambda z, send: (0, 0, 0)),
-            ],
-            out_specs=pl.BlockSpec((columns, share, inner, width), lambda z, send: (0, z, 0, 0)),
+            in_specs=[pl.BlockSpec((tile, rows), lambda z, *_: (z, 0))]
+            + [pl.BlockSpec(array.shape, lambda z, *_: (0, 0, 0)) for array in landed],
+            out_specs=pl.BlockSpec(
+                (columns, share, inner, width), lambda z, *_: (0, z, 0, 0)
+            ),
             scratch_shapes=[pltpu.VMEM((rows, width), jnp.bfloat16)],
         ),
         out_shape=jax.ShapeDtypeStruct((columns, steps, inner, width), jnp.bfloat16),
         name="weight_part",
-    )(send, turned, landed, swapped)
+    )(table, core, turned, *landed)
 
 
 def ring(count, step, stride=1):
@@ -372,13 +394,17 @@
     return sorted(range(count), key=lambda d: -min(d, count - d))
 
 
-def gather_ring(array, at, size, shift):
+def gather_ring(array, at, size, shift, relay):
     cut = array.shape[0] // 2
     before, after = shift(array, 1), shift(array, -1)
-    top, low = shift(before[:cut], 1), shift(after[cut:], -1)
+    if relay:
+        far = [(0, shift(before[:cut], 1)), (cut, shift(after[cut:], -1))]
+    else:
+        far = [(0, shift(array, 2))]
+    pieces = [(0, 0, array), (1, 0, before), (3, 0, after)] + [(2, row, part) for row, part in far]
     out = jnp.zeros((size,) + array.shape, array.dtype)
     none = (0,) * (array.ndim - 1)
-    for step, row, piece in ((0, 0, array), (1, 0, before), (2, 0, top), (2, cut, low), (3, 0, after)):
+    for step, row, piece in pieces:
         out = lax.dynamic_update_slice(out, piece[None], ((at + size - step) % size, row) + none)
     return out
 
@@ -429,8 +455,8 @@
     width = value_weight.shape[1] // 2
     half = lax.dynamic_slice_in_dim(value_weight, core * width, width, axis=1)
     x, y = fsdp // side, fsdp % side
-    line = gather_ring(half, x, side, along_x)
-    own = gather_ring(line, y, side, along_y)
+    line = gather_ring(half, x, side, along_x, False)
+    own = gather_ring(line, y, side, along_y, True)
     own = jnp.transpose(own, (1, 0, 2, 3)).reshape(depth, width)
     (other,) = swap([own])
 
@@ -438,10 +464,12 @@
     origin = (plane_at + planes - hop_steps) % planes * 2
     origin = jnp.concatenate([origin + core, origin + 1 - core])
     block = jnp.maximum(which(send, onward), 0)
+    back = jnp.maximum(which(take, onward), 0)
     place = which(take, origin)
     leaving = value_blocks(core_of, block, normed, own, other)
     landed = along_z(leaving)
-    (swapped,) = swap([jnp.stack(landed)])
+    leave = [lax.dynamic_index_in_dim(a, 1 - core, 0, keepdims=False) for a in landed]
+    (swapped,) = swap([jnp.stack(leave)])
     packed_v = pack(core_of, place, landed, swapped, rows)
 
     column = 2 * jnp.arange(planes, dtype=jnp.int32)
@@ -451,24 +479,32 @@
     turned = turn_columns(column + core, normed, got, tile)
     (partner,) = swap([send_to])
     sends = jnp.concatenate([send_to, partner], axis=0)
+    homes = jnp.stack([which(send, origin), which(partner[0], origin)])
 
     half_groups = KV_HEADS // 2
     key_at = wide // HEAD_DIM
     done = attention(
-        take, arrived_one, arrived_one, packed_v, out_grad, doc_ids,
-        0, half_groups, key_at, (),
+        take, back, arrived_one, arrived_one, packed_v, out_grad, doc_ids,
+        0, half_groups, key_at, (), planes,
     )
+    done, returning_one = done[:3], done[3:]
+    landed_one = along_z(returning_one)
+    landed_one += swap(landed_one)
     query_grad, key_grad, value_grad, returning = attention(
-        take, arrived_two, arrived_one, packed_v, out_grad, doc_ids,
-        half_groups, half_groups, key_at, done,
+        take, back, arrived_two, arrived_one, packed_v, out_grad, doc_ids,
+        half_groups, half_groups, key_at, done, 1,
     )
-    landed = lax.all_to_all(returning, "dp", 0, 0, tiled=True)
-    (swapped,) = swap([landed])
+    landed_two = lax.all_to_all(returning, "dp", 0, 0, tiled=True)
+    chip_one = weight_part(homes, core_of, turned, landed_one, fsdp_count, planes)
+    chips_one = lax.all_to_all(chip_one, "fsdp", 0, 0, tiled=True)
+    landed_two = [landed_two] + swap([landed_two])
+    chip_two = weight_part(sends, core_of, turned, landed_two, fsdp_count, planes)
     input_grad = input_gradient(core_of, value_grad, own, other)
-
-    chip = weight_part(sends, turned, landed, swapped, fsdp_count, planes)
-    chips = lax.all_to_all(chip, "fsdp", 0, 0, tiled=True)
-    plane = jnp.sum(chips.astype(jnp.float32), axis=0).astype(jnp.bfloat16)
+    chips_two = lax.all_to_all(chip_two, "fsdp", 0, 0, tiled=True)
+
+    plane = jnp.concatenate(
+        [jnp.sum(a.astype(jnp.float32), axis=0) for a in (chips_one, chips_two)], axis=-1
+    ).astype(jnp.bfloat16)
     groups = [list(range(c, dp_count, 2)) for c in range(2)]
     parts = lax.all_to_all(plane, "dp", 0, 0, axis_index_groups=groups, tiled=True)
     weight_grad = jnp.sum(parts.astype(jnp.float32), axis=0) * grad_scale

time: 254 us -> 259 us (1.020)
  blocking collectives: 34.7 us -> 0 us
  starting transfers between devices: 53.9 us -> 78.1 us
  waiting for transfers between devices: 78 us -> 91.3 us
  Pallas kernels: 65.3 us -> 68.7 us
    all_to_all x1 -> x0, blocking collectives: 34.7 us -> none  [local(): chips = lax.all_to_all(chip, 'fsdp', 0, 0, tiled=True)]
    ppermute x7 -> x14, starting transfers between devices: 18.1 us -> 33.1 us  [along_z(): lax.ppermute(a, 'dp', ring((dp_count, planes), d, 2))]
    all_to_all x1 -> x3, waiting for transfers between devices: 13.6 us -> 27.5 us  [the longest x1 16.1 us: local(): chips_two = lax.all_to_all(chip_two, 'fsdp', 0, 0, tiled=True)]
    all_to_all x1 -> x3, starting transfers between devices: 4.7 us -> 15.2 us  [the longest x1 7.02 us: local(): chips_one = lax.all_to_all(chip_one, 'fsdp', 0, 0, tiled=True)]
    ppermute x4 -> x3, waiting for transfers between devices: 2.22 us -> 5.68 us  [along_x(): return lax.ppermute(array, 'fsdp', ring((fsdp_count, side), step, side))]
    pallas_call x1 -> x2, Pallas kernels: 5.57 us -> 8.83 us  [weight_part(): pl.pallas_call(weight_kernel, grid_spec=pltpu.PrefetchScalarGridSpec(num_...]
    ppermute x4, waiting for transfers between devices: 13 us -> 10.1 us  [along_y(): return lax.ppermute(array, 'fsdp', ring((fsdp_count, side), step, 1))]
    ppermute x4 -> x3, starting transfers between devices: 6.7 us -> 5.13 us  [along_x(): return lax.ppermute(array, 'fsdp', ring((fsdp_count, side), step, side))]
  transfers between devices with their start and end apart: 24 -> 40, of which waited for: 13 -> 18; matrix products, arithmetic and copies ran while one was open for 5% -> 5% of each run, Pallas kernels for 20% -> 24%
where the time goes in v5:
time: 259 us; the launch traced here: 256 us
  waiting for transfers between devices  91.3 us (35%)
  starting transfers between devices  78.1 us (30%)
  Pallas kernels  68.7 us (27%)
  local copies, waits for them, and re-layouts  11.5 us (4%)
  other arithmetic  5.65 us (2%)
    ppermute x14, starting transfers between devices, along_z(): lax.ppermute(a, 'dp', ring((dp_count, planes), d, 2))  33.1 us
    ppermute x14, waiting for transfers between devices, along_z(): lax.ppermute(a, 'dp', ring((dp_count, planes), d, 2))  31.5 us
    pallas_call x2, Pallas kernels, attention(): pl.pallas_call(functools.partial(attention_kernel, len(done)), grid_spec=...  17.3 us
    all_to_all x1, waiting for transfers between devices, local(): chips_two = lax.all_to_all(chip_two, 'fsdp', 0, 0, tiled=True)  16.1 us
    all_to_all x1, waiting for transfers between devices, local(): arrived_one = lax.all_to_all(slots, 'dp', 0, 0, tiled=True)  13.4 us
    pallas_call x2, Pallas kernels, outgoing_slots(): pl.pallas_call(outgoing_kernel, grid_spec=pltpu.PrefetchScalarGridSpec(nu...  11.5 us
    all_to_all x1, waiting for transfers between devices, local(): chips_one = lax.all_to_all(chip_one, 'fsdp', 0, 0, tiled=True)  11.5 us
    ppermute x4, waiting for transfers between devices, along_y(): return lax.ppermute(array, 'fsdp', ring((fsdp_count, side), step, 1))  10.1 us
  transfers between devices with their start and end apart: 40, of which 18 were waited for; matrix products, arithmetic and copies ran while one was open for 5% of the time, Pallas kernels for 24%

profile of v5, /device:TPU:0, one launch (start us, length us, event | category | flops | bytes accessed | tf_op | source)
XLA Modules:
  0.0 256.5 jit_solution(762568385571693560)
XLA Ops:
  0.6 5.8 %outgoing_slots.3 = bf16[16,48,1536]{2,1,0:T(8,128)(2,1)} custom-call(s32[8]{0:T(128)} %bitcast.39, bf16[384,2048]{1,0:T(8,128)(2,1)} %refs_0_.3, bf16[384,512]{1,0:T(8,128)(2,1)} %refs_1_.1), custom_call_target="tpu_custom_call" | custom-call | tf_op jit(solution)/shard_map/outgoing_slots/pallas_call | solution.py:31
  6.5 7.0 %all-to-all-start.1 = ((bf16[16,48,1536]{2,1,0:T(8,128)(2,1)}), bf16[16,48,1536]{2,1,0:T(8,128)(2,1)S(1)}, u32[]{:S(2)}, u32[]{:S(2)}) async-start(bf16[16,48,1536]{2,1,0:T(8,128)(2,1)} %outgoing_slots.3), calls=%async_computation.1 | async-start | bytes 4718592 | tf_op jit(solution)/shard_map/all_to_all | solution.py:451
  13.6 1.6 collective-permute-start
  15.2 1.7 collective-permute-start.1
  16.9 1.8 collective-permute-start.2
  18.8 1.9 collective-permute-done
  20.7 2.1 collective-permute-done.1
  22.8 1.7 collective-permute-done.2
  24.5 1.7 collective-permute-start.3
  26.1 1.7 collective-permute-start.4
  27.8 1.6 broadcast_in_dim.64
  30.2 9.0 %collective-permute-done.3 = bf16[4,256,256]{2,1,0:T(8,128)(2,1)S(1)} collective-permute-done((bf16[4,256,256]{2,1,0:T(8,128)(2,1)S(1)}, bf16[4,256,256]{2,1,0:T(8,128)(2,1)S(1)}, u32[]{:S(2)}, u32[]{:S(2)}) %collective-permute-start.3) | collective-permute-done | bytes 524320 | tf_op jit(solution)/shard_map/ppermute | solution.py:443
  39.6 1.0 slice.9
  40.5 3.0 %collective-permute-start.6 = (bf16[2,256,256]{2,1,0:T(8,128)(2,1)S(1)}, bf16[2,256,256]{2,1,0:T(8,128)(2,1)S(1)}, u32[]{:S(2)}, u32[]{:S(2)}) collective-permute-start(bf16[2,256,256]{2,1,0:T(8,128)(2,1)S(1)} %slice.9), channel_id=1, source_target_pairs={{0,3},{1,0},{2,1},{3,2},{4,7},{5,4},{6,5},{7,6},{8,11},{9,8},{10,9... | collective-permute-start | bytes 786440 | tf_op jit(solution)/shard_map/ppermute | solution.py:443
  44.4 1.9 bitcast_dynamic-update-slice_fusion
  46.3 1.1 collective-permute-done.5
  49.3 5.7 %outgoing_slots.2 = bf16[16,48,1024]{2,1,0:T(8,128)(2,1)} custom-call(s32[8]{0:T(128)} %bitcast.40, bf16[384,2048]{1,0:T(8,128)(2,1)} %refs_0_.3), custom_call_target="tpu_custom_call" | custom-call | tf_op jit(solution)/shard_map/outgoing_slots/pallas_call | solution.py:31
  55.0 13.4 %all-to-all-done.1.q_ref.k_ref = bf16[16,48,1536]{2,1,0:T(8,128)(2,1)S(1)} async-done(((bf16[16,48,1536]{2,1,0:T(8,128)(2,1)}), bf16[16,48,1536]{2,1,0:T(8,128)(2,1)S(1)}, u32[]{:S(2)}, u32[]{:S(2)}) %all-to-all-start.1) | async-done | bytes 2359328 | tf_op jit(solution)/shard_map/all_to_all | solution.py:451
  68.4 4.6 %all-to-all-start = ((bf16[16,48,1024]{2,1,0:T(8,128)(2,1)}), bf16[16,48,1024]{2,1,0:T(8,128)(2,1)}, u32[]{:S(2)}, u32[]{:S(2)}) async-start(bf16[16,48,1024]{2,1,0:T(8,128)(2,1)} %outgoing_slots.2), calls=%async_computation | async-start | bytes 3145728 | tf_op jit(solution)/shard_map/all_to_all | solution.py:453
  73.9 6.6 %value_blocks.1 = (bf16[2,48,512]{2,1,0:T(8,128)(2,1)}, bf16[2,48,512]{2,1,0:T(8,128)(2,1)}, bf16[2,48,512]{2,1,0:T(8,128)(2,1)}, bf16[2,48,512]{2,1,0:T(8,128)(...) custom-call(s32[1]{0:T(128)} %bitcast.2.core, ...), custom_call_target="tpu_custom_call" | custom-call | flops 1610612736 | bytes 7340032 | tf_op jit(solution)/shard_map/value_blocks/pallas_call | solution.py:80
  80.5 5.9 %collective-permute-start.8 = (bf16[2,48,512]{2,1,0:T(8,128)(2,1)}, bf16[2,48,512]{2,1,0:T(8,128)(2,1)S(1)}, u32[]{:S(2)}, u32[]{:S(2)}) collective-permute-start(bf16[2,48,512]{2,1,0:T(8,128)(2,1)} %get-tuple-element.27), channel_id=1, source_target_pairs={{0,128},{16,144},{32,160},{48,176},{64,192},{80,208},{96,224},{112... | collective-permute-start | bytes 294920 | tf_op jit(solution)/shard_map/ppermute | solution.py:432
  87.0 6.3 %pick_columns.1 = bf16[384,2048]{1,0:T(8,128)(2,1)} custom-call(s32[8]{0:T(128)} %add_subtract_fusion.column, bf16[384,4096]{1,0:T(8,128)(2,1)} %own_ref.1), custom_call_target="tpu_custom_call" | custom-call | tf_op jit(solution)/shard_map/pick_columns/pallas_call | solution.py:139
  93.3 0.8 copy.31.doc_col
  94.7 4.5 %collective-permute-start.10 = (bf16[2,48,512]{2,1,0:T(8,128)(2,1)S(1)}, bf16[2,48,512]{2,1,0:T(8,128)(2,1)S(1)}, u32[]{:S(2)}, u32[]{:S(2)}) collective-permute-start(bf16[2,48,512]{2,1,0:T(8,128)(2,1)S(1)} %copy-done.38), channel_id=1, source_target_pairs={{0,160},{16,176},{32,192},{48,208},{64,224},{80,240},{96,0},{112,1... | collective-permute-start | bytes 294920 | tf_op jit(solution)/shard_map/ppermute | solution.py:432
  99.7 22.5 %collective-permute-done.8.refs_0_ = bf16[2,48,512]{2,1,0:T(8,128)(2,1)S(1)} collective-permute-done((bf16[2,48,512]{2,1,0:T(8,128)(2,1)}, bf16[2,48,512]{2,1,0:T(8,128)(2,1)S(1)}, u32[]{:S(2)}, u32[]{:S(2)}) %collective-permute-start.8) | collective-permute-done | bytes 98336 | tf_op jit(solution)/shard_map/ppermute | solution.py:432
  122.6 3.3 %collective-permute-start.14 = (bf16[2,48,512]{2,1,0:T(8,128)(2,1)S(1)}, bf16[2,48,512]{2,1,0:T(8,128)(2,1)S(1)}, u32[]{:S(2)}, u32[]{:S(2)}) collective-permute-start(bf16[2,48,512]{2,1,0:T(8,128)(2,1)S(1)} %copy-done.34), channel_id=1, source_target_pairs={{0,224},{16,240},{32,0},{48,16},{64,32},{80,48},{96,64},{112,80},{... | collective-permute-start | bytes 294920 | tf_op jit(solution)/shard_map/ppermute | solution.py:432
  125.9 2.7 %collective-permute-done.12.refs_4_ = bf16[2,48,512]{2,1,0:T(8,128)(2,1)S(1)} collective-permute-done((bf16[2,48,512]{2,1,0:T(8,128)(2,1)S(1)}, bf16[2,48,512]{2,1,0:T(8,128)(2,1)S(1)}, u32[]{:S(2)}, u32[]{:S(2)}) %collective-permute-start.12) | collective-permute-done | bytes 98336 | tf_op jit(solution)/shard_map/ppermute | solution.py:432
  132.0 2.9 %pack_values.1.v_ref = bf16[384,512]{1,0:T(8,128)(2,1)} custom-call(s32[1]{0:T(128)} %bitcast.2.core, s32[16]{0:T(128)} %broadcast_add_fusion.1.place, bf16[2,48,512]{2,1,0:T(8,128)(2,1)} %copy-done.5, bf16[2,48,512]{2,1,0:T(8,128)(2,1)} %copy-done.6, bf16[2,48,512]{2,1,0:T(8,128)(2,1)} %copy-done.7, bf16[2,48,512]{2,1,0:T(8,128)(2,1)} %copy-done.8, ...), custom_call_target="tpu_custom_call" | custom-call | tf_op jit(solution)/shard_map/pack_values/pallas_call | solution.py:118
  134.8 8.6 %attention_backward.2 = (bf16[384,2048]{1,0:T(8,128)(2,1)}, bf16[384,512]{1,0:T(8,128)(2,1)}, bf16[384,512]{1,0:T(8,128)(2,1)}, bf16[2,48,256]{2,1,0:T(8,128)(2,...) custom-call(s32[8]{0:T(128)} %bitcast.42, ...), custom_call_target="tpu_custom_call" | custom-call | flops 1811939328 | bytes 3932160 | tf_op jit(solution)/shard_map/attention_backward/pallas_call | solution.py:287
  143.5 8.8 %attention_backward.3 = (bf16[384,2048]{1,0:T(8,128)(2,1)}, bf16[384,512]{1,0:T(8,128)(2,1)}, bf16[384,512]{1,0:T(8,128)(2,1)}, bf16[16,48,256]{2,1,0:T(8,128)(2,1)}) custom-call(s32[8]{0:T(128)} %bitcast.43, s32[16]{0:T(128)} %add_maximum_fusion.1.back_block, ...), custom_call_target="tpu_custom_call", output_to_operand_aliasing={{0}: (8, {}), {1}: (9, {}), {2}: (10, {})} | custom-call | flops 1811939328 | bytes 3932160 | tf_op jit(solution)/shard_map/attention_backward/pallas_call | solution.py:287
  152.3 4.5 %all-to-all-start.3 = ((bf16[16,48,256]{2,1,0:T(8,128)(2,1)}), bf16[16,48,256]{2,1,0:T(8,128)(2,1)S(1)}, u32[]{:S(2)}, u32[]{:S(2)}) async-start(bf16[16,48,256]{2,1,0:T(8,128)(2,1)} %get-tuple-element.49), calls=%async_computation.3 | async-start | bytes 786432 | tf_op jit(solution)/shard_map/all_to_all | solution.py:497
  156.8 5.9 %collective-permute-start.18 = (bf16[2,48,256]{2,1,0:T(8,128)(2,1)S(1)}, bf16[2,48,256]{2,1,0:T(8,128)(2,1)S(1)}, u32[]{:S(2)}, u32[]{:S(2)}) collective-permute-start(bf16[2,48,256]{2,1,0:T(8,128)(2,1)S(1)} %copy-done.46), channel_id=1, source_target_pairs={{0,128},{16,144},{32,160},{48,176},{64,192},{80,208},{96,224},{112... | collective-permute-start | bytes 147464 | tf_op jit(solution)/shard_map/ppermute | solution.py:432
  163.3 4.5 %collective-permute-start.20 = (bf16[2,48,256]{2,1,0:T(8,128)(2,1)S(1)}, bf16[2,48,256]{2,1,0:T(8,128)(2,1)S(1)}, u32[]{:S(2)}, u32[]{:S(2)}) collective-permute-start(bf16[2,48,256]{2,1,0:T(8,128)(2,1)S(1)} %copy-done.44), channel_id=1, source_target_pairs={{0,160},{16,176},{32,192},{48,208},{64,224},{80,240},{96,0},{112,1... | collective-permute-start | bytes 147464 | tf_op jit(solution)/shard_map/ppermute | solution.py:432
  168.3 3.6 %collective-permute-start.22 = (bf16[2,48,256]{2,1,0:T(8,128)(2,1)S(1)}, bf16[2,48,256]{2,1,0:T(8,128)(2,1)S(1)}, u32[]{:S(2)}, u32[]{:S(2)}) collective-permute-start(bf16[2,48,256]{2,1,0:T(8,128)(2,1)S(1)} %copy-done.42), channel_id=1, source_target_pairs={{0,192},{16,208},{32,224},{48,240},{64,0},{80,16},{96,32},{112,48}... | collective-permute-start | bytes 147464 | tf_op jit(solution)/shard_map/ppermute | solution.py:432
  172.5 4.1 %collective-permute-done.18.refs_0_ = bf16[2,48,256]{2,1,0:T(8,128)(2,1)S(1)} collective-permute-done((bf16[2,48,256]{2,1,0:T(8,128)(2,1)S(1)}, bf16[2,48,256]{2,1,0:T(8,128)(2,1)S(1)}, u32[]{:S(2)}, u32[]{:S(2)}) %collective-permute-start.18) | collective-permute-done | bytes 49184 | tf_op jit(solution)/shard_map/ppermute | solution.py:432
  176.6 3.3 %collective-permute-start.24 = (bf16[2,48,256]{2,1,0:T(8,128)(2,1)S(1)}, bf16[2,48,256]{2,1,0:T(8,128)(2,1)S(1)}, u32[]{:S(2)}, u32[]{:S(2)}) collective-permute-start(bf16[2,48,256]{2,1,0:T(8,128)(2,1)S(1)} %copy-done.40), channel_id=1, source_target_pairs={{0,224},{16,240},{32,0},{48,16},{64,32},{80,48},{96,64},{112,80},{... | collective-permute-start | bytes 147464 | tf_op jit(solution)/shard_map/ppermute | solution.py:432
  180.6 1.3 collective-permute-done.23.refs_5_
  183.6 7.4 %turn_columns.1.turned_ref = bf16[2048,768]{1,0:T(8,128)(2,1)} custom-call(s32[8]{0:T(128)} %fusion.4.column, bf16[384,4096]{1,0:T(8,128)(2,1)} %own_ref.1, bf16[384,2048]{1,0:T(8,128)(2,1)} %collective-permute-done.17.got_ref), custom_call_target="tpu_custom_call" | custom-call | tf_op jit(solution)/shard_map/turn_columns/pallas_call | solution.py:161
  192.4 4.5 %weight_part.2 = bf16[16,8,16,256]{3,2,1,0:T(8,128)(2,1)} custom-call(s32[2,16]{1,0:T(2,128)} %pad_add_fusion.table, s32[1]{0:T(128)} %bitcast.2.core, bf16[2048,768]{1,0:T(8,128)(2,1)} %turn_columns.1.turned_ref, bf16[2,48,256]{2,1,0:T(8,128)(2,1)} %copy-done.14, bf16[2,48,256]{2,1,0:T(8,128)(2,1)} %copy-done.15, bf16[2,48,256]{2,1,0:T(8,128)(2,1)} %copy-done.16, ...), custom_call_target="tpu_custom_call" | custom-call | tf_op jit(solution)/shard_map/weight_part/pallas_call | solution.py:368
  196.9 7.0 %all-to-all-start.2 = ((bf16[16,8,16,256]{3,2,1,0:T(8,128)(2,1)}), bf16[16,8,16,256]{3,2,1,0:T(8,128)(2,1)S(1)}, u32[]{:S(2)}, u32[]{:S(2)}) async-start(bf16[16,8,16,256]{3,2,1,0:T(8,128)(2,1)} %weight_part.2), calls=%async_computation.2 | async-start | bytes 2097152 | tf_op jit(solution)/shard_map/all_to_all | solution.py:499
  204.7 1.0 collective-permute-done.33.refs_1_
  206.5 4.3 %weight_part.3 = bf16[16,8,16,256]{3,2,1,0:T(8,128)(2,1)} custom-call(s32[2,8]{1,0:T(2,128)} %pad_add_fusion.1.table, s32[1]{0:T(128)} %bitcast.2.core, bf16[2048,768]{1,0:T(8,128)(2,1)} %turn_columns.1.turned_ref, bf16[16,48,256]{2,1,0:T(8,128)(2,1)} %copy-done.1, bf16[16,48,256]{2,1,0:T(8,128)(2,1)} %copy-done.2), custom_call_target="tpu_custom_call" | custom-call | tf_op jit(solution)/shard_map/weight_part/pallas_call | solution.py:368
  210.8 11.5 %all-to-all-done.2 = bf16[16,8,16,256]{3,2,1,0:T(8,128)(2,1)S(1)} async-done(((bf16[16,8,16,256]{3,2,1,0:T(8,128)(2,1)}), bf16[16,8,16,256]{3,2,1,0:T(8,128)(2,1)S(1)}, u32[]{:S(2)}, u32[]{:S(2)}) %all-to-all-start.2) | async-done | bytes 1048608 | tf_op jit(solution)/shard_map/all_to_all | solution.py:499
  222.3 3.7 %all-to-all-start.4 = ((bf16[16,8,16,256]{3,2,1,0:T(8,128)(2,1)}), bf16[16,8,16,256]{3,2,1,0:T(8,128)(2,1)S(1)}, u32[]{:S(2)}, u32[]{:S(2)}) async-start(bf16[16,8,16,256]{3,2,1,0:T(8,128)(2,1)} %weight_part.3), calls=%async_computation.4 | async-start | bytes 2097152 | tf_op jit(solution)/shard_map/all_to_all | solution.py:503
  226.1 16.1 %all-to-all-done.4 = bf16[16,8,16,256]{3,2,1,0:T(8,128)(2,1)S(1)} async-done(((bf16[16,8,16,256]{3,2,1,0:T(8,128)(2,1)}), bf16[16,8,16,256]{3,2,1,0:T(8,128)(2,1)S(1)}, u32[]{:S(2)}, u32[]{:S(2)}) %all-to-all-start.4) | async-done | bytes 1048608 | tf_op jit(solution)/shard_map/all_to_all | solution.py:503
  243.0 3.8 %all-to-all-start.5 = ((bf16[8,16,512]{2,1,0:T(8,128)(2,1)}), bf16[8,16,512]{2,1,0:T(8,128)(2,1)S(1)}, u32[]{:S(2)}, u32[]{:S(2)}) async-start(bf16[8,16,512]{2,1,0:T(8,128)(2,1)} %pad_maximum_fusion), calls=%async_computation.5 | async-start | bytes 262144 | tf_op jit(solution)/shard_map/all_to_all | solution.py:509
  246.8 7.8 %input_gradient.1 = bf16[384,4096]{1,0:T(8,128)(2,1)} custom-call(s32[1]{0:T(128)} %bitcast.2.core, bf16[384,512]{1,0:T(8,128)(2,1)} %get-tuple-element.40.grad_ref, bf16[4096,256]{1,0:T(8,128)(2,1)} %bitcast.17.own_ref, bf16[4096,256]{1,0:T(8,128)(2,1)} %collective-permute-done.7.other_ref), custom_call_target="tpu_custom_call" | custom-call | flops 1610612736 | bytes 7340032 | tf_op jit(solution)/shard_map/input_gradient/pallas_call | solution.py:189
  254.5 1.3 all-to-all-done.5
  (182 shorter events, 18.8 us)
Async XLA Ops:
  6.5 62.0 %all-to-all-start.1 = ((bf16[16,48,1536]{2,1,0:T(8,128)(2,1)}), bf16[16,48,1536]{2,1,0:T(8,128)(2,1)S(1)}, u32[]{:S(2)}, u32[]{:S(2)}) async-start(bf16[16,48,1536]{2,1,0:T(8,128)(2,1)} %outgoing_slots.3), calls=%async_computation.1 | async-start | bytes 4718592 | tf_op jit(solution)/shard_map/all_to_all | solution.py:451
  13.6 7.0 %collective-permute-start = (bf16[256,256]{1,0:T(8,128)(2,1)S(1)}, bf16[256,256]{1,0:T(8,128)(2,1)S(1)}, u32[]{:S(2)}, u32[]{:S(2)}) collective-permute-start(bf16[256,256]{1,0:T(8,128)(2,1)S(1)} %get-tuple-element.56), channel_id=1, source_target_pairs={{0,4},{1,5},{2,6},{3,7},{4,8},{5,9},{6,10},{7,11},{8,12},{9,13},{1... | collective-permute-start | bytes 393224 | tf_op jit(solution)/shard_map/ppermute | solution.py:440
  15.2 7.6 %collective-permute-start.1 = (bf16[256,256]{1,0:T(8,128)(2,1)S(1)}, bf16[256,256]{1,0:T(8,128)(2,1)S(1)}, u32[]{:S(2)}, u32[]{:S(2)}) collective-permute-start(bf16[256,256]{1,0:T(8,128)(2,1)S(1)} %get-tuple-element.56), channel_id=1, source_target_pairs={{0,12},{1,13},{2,14},{3,15},{4,0},{5,1},{6,2},{7,3},{8,4},{9,5},{1... | collective-permute-start | bytes 393224 | tf_op jit(solution)/shard_map/ppermute | solution.py:440
  16.9 7.5 %collective-permute-start.2 = (bf16[256,256]{1,0:T(8,128)(2,1)S(1)}, bf16[256,256]{1,0:T(8,128)(2,1)S(1)}, u32[]{:S(2)}, u32[]{:S(2)}) collective-permute-start(bf16[256,256]{1,0:T(8,128)(2,1)S(1)} %get-tuple-element.56), channel_id=1, source_target_pairs={{0,8},{1,9},{2,10},{3,11},{4,12},{5,13},{6,14},{7,15},{8,0},{9,1},... | collective-permute-start | bytes 393224 | tf_op jit(solution)/shard_map/ppermute | solution.py:440
  24.5 14.7 %collective-permute-start.3 = (bf16[4,256,256]{2,1,0:T(8,128)(2,1)S(1)}, bf16[4,256,256]{2,1,0:T(8,128)(2,1)S(1)}, u32[]{:S(2)}, u32[]{:S(2)}) collective-permute-start(bf16[4,256,256]{2,1,0:T(8,128)(2,1)S(1)} %bitcast_dynamic-update-slice_fusion.5), channel_id=1, source_target_pairs={{0,1},{1,2},{2,3},{3,0},{4,5},{5,6},{6,7},{7,4},{8,9},{9,10},{10,1... | collective-permute-start | bytes 1572872 | tf_op jit(solution)/shard_map/ppermute | solution.py:443
  26.1 13.4 %collective-permute-start.4 = (bf16[4,256,256]{2,1,0:T(8,128)(2,1)S(1)}, bf16[4,256,256]{2,1,0:T(8,128)(2,1)}, u32[]{:S(2)}, u32[]{:S(2)}) collective-permute-start(bf16[4,256,256]{2,1,0:T(8,128)(2,1)S(1)} %bitcast_dynamic-update-slice_fusion.5), channel_id=1, source_target_pairs={{0,3},{1,0},{2,1},{3,2},{4,7},{5,4},{6,5},{7,6},{8,11},{9,8},{10,9... | collective-permute-start | bytes 1572872 | tf_op jit(solution)/shard_map/ppermute | solution.py:443
  39.2 8.2 %collective-permute-start.5 = (bf16[2,256,256]{2,1,0:T(8,128)(2,1)S(1)}, bf16[2,256,256]{2,1,0:T(8,128)(2,1)S(1)}, u32[]{:S(2)}, u32[]{:S(2)}) collective-permute-start(bf16[2,256,256]{2,1,0:T(8,128)(2,1)S(1)} %slice.8), channel_id=1, source_target_pairs={{0,1},{1,2},{2,3},{3,0},{4,5},{5,6},{6,7},{7,4},{8,9},{9,10},{10,1... | collective-permute-start | bytes 786440 | tf_op jit(solution)/shard_map/ppermute | solution.py:443
  40.5 7.6 %collective-permute-start.6 = (bf16[2,256,256]{2,1,0:T(8,128)(2,1)S(1)}, bf16[2,256,256]{2,1,0:T(8,128)(2,1)S(1)}, u32[]{:S(2)}, u32[]{:S(2)}) collective-permute-start(bf16[2,256,256]{2,1,0:T(8,128)(2,1)S(1)} %slice.9), channel_id=1, source_target_pairs={{0,3},{1,0},{2,1},{3,2},{4,7},{5,4},{6,5},{7,6},{8,11},{9,8},{10,9... | collective-permute-start | bytes 786440 | tf_op jit(solution)/shard_map/ppermute | solution.py:443
  48.8 25.1 %collective-permute-start.7 = (bf16[4096,256]{1,0:T(8,128)(2,1)}, bf16[4096,256]{1,0:T(8,128)(2,1)}, u32[]{:S(2)}, u32[]{:S(2)}) collective-permute-start(bf16[4096,256]{1,0:T(8,128)(2,1)} %bitcast.17.own_ref), channel_id=1, source_target_pairs={{0,16},{16,0},{32,48},{48,32},{64,80},{80,64},{96,112},{112,96},{1... | collective-permute-start | bytes 6291464 | tf_op jit(solution)/shard_map/ppermute | solution.py:437
  48.8 24.5 %collective-permute-start.16 = (s32[1,8]{1,0:T(1,128)S(1)}, s32[1,8]{1,0:T(1,128)S(1)}, u32[]{:S(2)}, u32[]{:S(2)}) collective-permute-start(s32[1,8]{1,0:T(1,128)S(1)} %copy-done.30), channel_id=1, source_target_pairs={{0,16},{16,0},{32,48},{48,32},{64,80},{80,64},{96,112},{112,96},{1... | collective-permute-start | bytes 104 | tf_op jit(solution)/shard_map/ppermute | solution.py:437
  68.4 75.0 %all-to-all-start = ((bf16[16,48,1024]{2,1,0:T(8,128)(2,1)}), bf16[16,48,1024]{2,1,0:T(8,128)(2,1)}, u32[]{:S(2)}, u32[]{:S(2)}) async-start(bf16[16,48,1024]{2,1,0:T(8,128)(2,1)} %outgoing_slots.2), calls=%async_computation | async-start | bytes 3145728 | tf_op jit(solution)/shard_map/all_to_all | solution.py:453
  80.5 41.7 %collective-permute-start.8 = (bf16[2,48,512]{2,1,0:T(8,128)(2,1)}, bf16[2,48,512]{2,1,0:T(8,128)(2,1)S(1)}, u32[]{:S(2)}, u32[]{:S(2)}) collective-permute-start(bf16[2,48,512]{2,1,0:T(8,128)(2,1)} %get-tuple-element.27), channel_id=1, source_target_pairs={{0,128},{16,144},{32,160},{48,176},{64,192},{80,208},{96,224},{112... | collective-permute-start | bytes 294920 | tf_op jit(solution)/shard_map/ppermute | solution.py:432
  86.9 35.3 %copy-start.36 = (bf16[2,48,512]{2,1,0:T(8,128)(2,1)S(1)}, bf16[2,48,512]{2,1,0:T(8,128)(2,1)}, u32[]{:S(2)}) copy-start(bf16[2,48,512]{2,1,0:T(8,128)(2,1)} %get-tuple-element.31) | copy-start | bytes 294916
  86.9 35.6 %copy-start.35 = (bf16[2,48,512]{2,1,0:T(8,128)(2,1)S(1)}, bf16[2,48,512]{2,1,0:T(8,128)(2,1)}, u32[]{:S(2)}) copy-start(bf16[2,48,512]{2,1,0:T(8,128)(2,1)} %get-tuple-element.32) | copy-start | bytes 294916
  86.9 35.6 %copy-start.34 = (bf16[2,48,512]{2,1,0:T(8,128)(2,1)S(1)}, bf16[2,48,512]{2,1,0:T(8,128)(2,1)}, u32[]{:S(2)}) copy-start(bf16[2,48,512]{2,1,0:T(8,128)(2,1)} %get-tuple-element.33) | copy-start | bytes 294916
  86.9 42.4 %copy-start.4 = (bf16[2,48,512]{2,1,0:T(8,128)(2,1)S(1)}, bf16[2,48,512]{2,1,0:T(8,128)(2,1)}, u32[]{:S(2)}) copy-start(bf16[2,48,512]{2,1,0:T(8,128)(2,1)} %get-tuple-element.34.refs_7_) | copy-start | bytes 294916
  93.2 75.1 %collective-permute-start.17 = (bf16[384,2048]{1,0:T(8,128)(2,1)}, bf16[384,2048]{1,0:T(8,128)(2,1)}, u32[]{:S(2)}, u32[]{:S(2)}) collective-permute-start(bf16[384,2048]{1,0:T(8,128)(2,1)} %pick_columns.1), channel_id=1, source_target_pairs={{0,16},{16,0},{32,48},{48,32},{64,80},{80,64},{96,112},{112,96},{1... | collective-permute-start | bytes 4718600 | tf_op jit(solution)/shard_map/ppermute | solution.py:437
  94.1 28.4 %collective-permute-start.9 = (bf16[2,48,512]{2,1,0:T(8,128)(2,1)S(1)}, bf16[2,48,512]{2,1,0:T(8,128)(2,1)S(1)}, u32[]{:S(2)}, u32[]{:S(2)}) collective-permute-start(bf16[2,48,512]{2,1,0:T(8,128)(2,1)S(1)} %copy-done.39), channel_id=1, source_target_pairs={{0,96},{16,112},{32,128},{48,144},{64,160},{80,176},{96,192},{112,... | collective-permute-start | bytes 294920 | tf_op jit(solution)/shard_map/ppermute | solution.py:432
  94.7 27.9 %collective-permute-start.10 = (bf16[2,48,512]{2,1,0:T(8,128)(2,1)S(1)}, bf16[2,48,512]{2,1,0:T(8,128)(2,1)S(1)}, u32[]{:S(2)}, u32[]{:S(2)}) collective-permute-start(bf16[2,48,512]{2,1,0:T(8,128)(2,1)S(1)} %copy-done.38), channel_id=1, source_target_pairs={{0,160},{16,176},{32,192},{48,208},{64,224},{80,240},{96,0},{112,1... | collective-permute-start | bytes 294920 | tf_op jit(solution)/shard_map/ppermute | solution.py:432
  99.1 26.8 %collective-permute-start.11 = (bf16[2,48,512]{2,1,0:T(8,128)(2,1)S(1)}, bf16[2,48,512]{2,1,0:T(8,128)(2,1)S(1)}, u32[]{:S(2)}, u32[]{:S(2)}) collective-permute-start(bf16[2,48,512]{2,1,0:T(8,128)(2,1)S(1)} %copy-done.37), channel_id=1, source_target_pairs={{0,64},{16,80},{32,96},{48,112},{64,128},{80,144},{96,160},{112,17... | collective-permute-start | bytes 294920 | tf_op jit(solution)/shard_map/ppermute | solution.py:432
  122.2 6.4 %collective-permute-start.12 = (bf16[2,48,512]{2,1,0:T(8,128)(2,1)S(1)}, bf16[2,48,512]{2,1,0:T(8,128)(2,1)S(1)}, u32[]{:S(2)}, u32[]{:S(2)}) collective-permute-start(bf16[2,48,512]{2,1,0:T(8,128)(2,1)S(1)} %copy-done.36), channel_id=1, source_target_pairs={{0,192},{16,208},{32,224},{48,240},{64,0},{80,16},{96,32},{112,48}... | collective-permute-start | bytes 294920 | tf_op jit(solution)/shard_map/ppermute | solution.py:432
  122.5 6.1 %collective-permute-start.13 = (bf16[2,48,512]{2,1,0:T(8,128)(2,1)S(1)}, bf16[2,48,512]{2,1,0:T(8,128)(2,1)S(1)}, u32[]{:S(2)}, u32[]{:S(2)}) collective-permute-start(bf16[2,48,512]{2,1,0:T(8,128)(2,1)S(1)} %copy-done.35), channel_id=1, source_target_pairs={{0,32},{16,48},{32,64},{48,80},{64,96},{80,112},{96,128},{112,144}... | collective-permute-start | bytes 294920 | tf_op jit(solution)/shard_map/ppermute | solution.py:432
  122.6 6.7 %collective-permute-start.14 = (bf16[2,48,512]{2,1,0:T(8,128)(2,1)S(1)}, bf16[2,48,512]{2,1,0:T(8,128)(2,1)S(1)}, u32[]{:S(2)}, u32[]{:S(2)}) collective-permute-start(bf16[2,48,512]{2,1,0:T(8,128)(2,1)S(1)} %copy-done.34), channel_id=1, source_target_pairs={{0,224},{16,240},{32,0},{48,16},{64,32},{80,48},{96,64},{112,80},{... | collective-permute-start | bytes 294920 | tf_op jit(solution)/shard_map/ppermute | solution.py:432
  129.4 1.8 collective-permute-start.15
  143.5 24.8 %copy-start.42 = (bf16[2,48,256]{2,1,0:T(8,128)(2,1)S(1)}, bf16[2,48,256]{2,1,0:T(8,128)(2,1)}, u32[]{:S(2)}) copy-start(bf16[2,48,256]{2,1,0:T(8,128)(2,1)} %get-tuple-element.45) | copy-start | bytes 147460
  143.5 33.0 %copy-start.41 = (bf16[2,48,256]{2,1,0:T(8,128)(2,1)S(1)}, bf16[2,48,256]{2,1,0:T(8,128)(2,1)}, u32[]{:S(2)}) copy-start(bf16[2,48,256]{2,1,0:T(8,128)(2,1)} %get-tuple-element.46) | copy-start | bytes 147460
  143.5 33.1 %copy-start.40 = (bf16[2,48,256]{2,1,0:T(8,128)(2,1)S(1)}, bf16[2,48,256]{2,1,0:T(8,128)(2,1)}, u32[]{:S(2)}) copy-start(bf16[2,48,256]{2,1,0:T(8,128)(2,1)} %get-tuple-element.47) | copy-start | bytes 147460
  143.5 36.3 %copy-start.13 = (bf16[2,48,256]{2,1,0:T(8,128)(2,1)S(1)}, bf16[2,48,256]{2,1,0:T(8,128)(2,1)}, u32[]{:S(2)}) copy-start(bf16[2,48,256]{2,1,0:T(8,128)(2,1)} %get-tuple-element.48.refs_7_) | copy-start | bytes 147460
  152.3 44.6 %all-to-all-start.3 = ((bf16[16,48,256]{2,1,0:T(8,128)(2,1)}), bf16[16,48,256]{2,1,0:T(8,128)(2,1)S(1)}, u32[]{:S(2)}, u32[]{:S(2)}) async-start(bf16[16,48,256]{2,1,0:T(8,128)(2,1)} %get-tuple-element.49), calls=%async_computation.3 | async-start | bytes 786432 | tf_op jit(solution)/shard_map/all_to_all | solution.py:497
  156.8 19.7 %collective-permute-start.18 = (bf16[2,48,256]{2,1,0:T(8,128)(2,1)S(1)}, bf16[2,48,256]{2,1,0:T(8,128)(2,1)S(1)}, u32[]{:S(2)}, u32[]{:S(2)}) collective-permute-start(bf16[2,48,256]{2,1,0:T(8,128)(2,1)S(1)} %copy-done.46), channel_id=1, source_target_pairs={{0,128},{16,144},{32,160},{48,176},{64,192},{80,208},{96,224},{112... | collective-permute-start | bytes 147464 | tf_op jit(solution)/shard_map/ppermute | solution.py:432
  162.7 13.8 %collective-permute-start.19 = (bf16[2,48,256]{2,1,0:T(8,128)(2,1)S(1)}, bf16[2,48,256]{2,1,0:T(8,128)(2,1)S(1)}, u32[]{:S(2)}, u32[]{:S(2)}) collective-permute-start(bf16[2,48,256]{2,1,0:T(8,128)(2,1)S(1)} %copy-done.45), channel_id=1, source_target_pairs={{0,96},{16,112},{32,128},{48,144},{64,160},{80,176},{96,192},{112,... | collective-permute-start | bytes 147464 | tf_op jit(solution)/shard_map/ppermute | solution.py:432
  163.3 16.6 %collective-permute-start.20 = (bf16[2,48,256]{2,1,0:T(8,128)(2,1)S(1)}, bf16[2,48,256]{2,1,0:T(8,128)(2,1)S(1)}, u32[]{:S(2)}, u32[]{:S(2)}) collective-permute-start(bf16[2,48,256]{2,1,0:T(8,128)(2,1)S(1)} %copy-done.44), channel_id=1, source_target_pairs={{0,160},{16,176},{32,192},{48,208},{64,224},{80,240},{96,0},{112,1... | collective-permute-start | bytes 147464 | tf_op jit(solution)/shard_map/ppermute | solution.py:432
  167.7 12.2 %collective-permute-start.21 = (bf16[2,48,256]{2,1,0:T(8,128)(2,1)S(1)}, bf16[2,48,256]{2,1,0:T(8,128)(2,1)S(1)}, u32[]{:S(2)}, u32[]{:S(2)}) collective-permute-start(bf16[2,48,256]{2,1,0:T(8,128)(2,1)S(1)} %copy-done.43), channel_id=1, source_target_pairs={{0,64},{16,80},{32,96},{48,112},{64,128},{80,144},{96,160},{112,17... | collective-permute-start | bytes 147464 | tf_op jit(solution)/shard_map/ppermute | solution.py:432
  168.3 12.1 %collective-permute-start.22 = (bf16[2,48,256]{2,1,0:T(8,128)(2,1)S(1)}, bf16[2,48,256]{2,1,0:T(8,128)(2,1)S(1)}, u32[]{:S(2)}, u32[]{:S(2)}) collective-permute-start(bf16[2,48,256]{2,1,0:T(8,128)(2,1)S(1)} %copy-done.42), channel_id=1, source_target_pairs={{0,192},{16,208},{32,224},{48,240},{64,0},{80,16},{96,32},{112,48}... | collective-permute-start | bytes 147464 | tf_op jit(solution)/shard_map/ppermute | solution.py:432
  176.5 5.3 %collective-permute-start.23 = (bf16[2,48,256]{2,1,0:T(8,128)(2,1)S(1)}, bf16[2,48,256]{2,1,0:T(8,128)(2,1)S(1)}, u32[]{:S(2)}, u32[]{:S(2)}) collective-permute-start(bf16[2,48,256]{2,1,0:T(8,128)(2,1)S(1)} %copy-done.41), channel_id=1, source_target_pairs={{0,32},{16,48},{32,64},{48,80},{64,96},{80,112},{96,128},{112,144}... | collective-permute-start | bytes 147464 | tf_op jit(solution)/shard_map/ppermute | solution.py:432
  176.6 5.3 %collective-permute-start.24 = (bf16[2,48,256]{2,1,0:T(8,128)(2,1)S(1)}, bf16[2,48,256]{2,1,0:T(8,128)(2,1)S(1)}, u32[]{:S(2)}, u32[]{:S(2)}) collective-permute-start(bf16[2,48,256]{2,1,0:T(8,128)(2,1)S(1)} %copy-done.40), channel_id=1, source_target_pairs={{0,224},{16,240},{32,0},{48,16},{64,32},{80,48},{96,64},{112,80},{... | collective-permute-start | bytes 147464 | tf_op jit(solution)/shard_map/ppermute | solution.py:432
  179.9 2.5 collective-permute-start.32
  180.0 2.5 collective-permute-start.25
  180.5 2.4 collective-permute-start.26
  181.8 9.2 %collective-permute-start.27 = (bf16[2,48,256]{2,1,0:T(8,128)(2,1)S(1)}, bf16[2,48,256]{2,1,0:T(8,128)(2,1)S(1)}, u32[]{:S(2)}, u32[]{:S(2)}) collective-permute-start(bf16[2,48,256]{2,1,0:T(8,128)(2,1)S(1)} %collective-permute-done.20.refs_2_), channel_id=1, source_target_pairs={{0,16},{16,0},{32,48},{48,32},{64,80},{80,64},{96,112},{112,96},{1... | collective-permute-start | bytes 147464 | tf_op jit(solution)/shard_map/ppermute | solution.py:437
  181.9 9.2 %collective-permute-start.28 = (bf16[2,48,256]{2,1,0:T(8,128)(2,1)S(1)}, bf16[2,48,256]{2,1,0:T(8,128)(2,1)S(1)}, u32[]{:S(2)}, u32[]{:S(2)}) collective-permute-start(bf16[2,48,256]{2,1,0:T(8,128)(2,1)S(1)} %collective-permute-done.21.refs_3_), channel_id=1, source_target_pairs={{0,16},{16,0},{32,48},{48,32},{64,80},{80,64},{96,112},{112,96},{1... | collective-permute-start | bytes 147464 | tf_op jit(solution)/shard_map/ppermute | solution.py:437
  182.4 8.7 %collective-permute-start.29 = (bf16[2,48,256]{2,1,0:T(8,128)(2,1)S(1)}, bf16[2,48,256]{2,1,0:T(8,128)(2,1)S(1)}, u32[]{:S(2)}, u32[]{:S(2)}) collective-permute-start(bf16[2,48,256]{2,1,0:T(8,128)(2,1)S(1)} %collective-permute-done.22.refs_4_), channel_id=1, source_target_pairs={{0,16},{16,0},{32,48},{48,32},{64,80},{80,64},{96,112},{112,96},{1... | collective-permute-start | bytes 147464 | tf_op jit(solution)/shard_map/ppermute | solution.py:437
  182.5 8.6 %collective-permute-start.30 = (bf16[2,48,256]{2,1,0:T(8,128)(2,1)S(1)}, bf16[2,48,256]{2,1,0:T(8,128)(2,1)S(1)}, u32[]{:S(2)}, u32[]{:S(2)}) collective-permute-start(bf16[2,48,256]{2,1,0:T(8,128)(2,1)S(1)} %collective-permute-done.23.refs_5_), channel_id=1, source_target_pairs={{0,16},{16,0},{32,48},{48,32},{64,80},{80,64},{96,112},{112,96},{1... | collective-permute-start | bytes 147464 | tf_op jit(solution)/shard_map/ppermute | solution.py:437
  182.9 8.3 %collective-permute-start.31 = (bf16[2,48,256]{2,1,0:T(8,128)(2,1)S(1)}, bf16[2,48,256]{2,1,0:T(8,128)(2,1)S(1)}, u32[]{:S(2)}, u32[]{:S(2)}) collective-permute-start(bf16[2,48,256]{2,1,0:T(8,128)(2,1)S(1)} %collective-permute-done.24.refs_6_), channel_id=1, source_target_pairs={{0,16},{16,0},{32,48},{48,32},{64,80},{80,64},{96,112},{112,96},{1... | collective-permute-start | bytes 147464 | tf_op jit(solution)/shard_map/ppermute | solution.py:437
  196.9 25.4 %all-to-all-start.2 = ((bf16[16,8,16,256]{3,2,1,0:T(8,128)(2,1)}), bf16[16,8,16,256]{3,2,1,0:T(8,128)(2,1)S(1)}, u32[]{:S(2)}, u32[]{:S(2)}) async-start(bf16[16,8,16,256]{3,2,1,0:T(8,128)(2,1)} %weight_part.2), calls=%async_computation.2 | async-start | bytes 2097152 | tf_op jit(solution)/shard_map/all_to_all | solution.py:499
  203.9 1.8 collective-permute-start.33
  222.3 19.9 %all-to-all-start.4 = ((bf16[16,8,16,256]{3,2,1,0:T(8,128)(2,1)}), bf16[16,8,16,256]{3,2,1,0:T(8,128)(2,1)S(1)}, u32[]{:S(2)}, u32[]{:S(2)}) async-start(bf16[16,8,16,256]{3,2,1,0:T(8,128)(2,1)} %weight_part.3), calls=%async_computation.4 | async-start | bytes 2097152 | tf_op jit(solution)/shard_map/all_to_all | solution.py:503
  243.0 12.8 %all-to-all-start.5 = ((bf16[8,16,512]{2,1,0:T(8,128)(2,1)}), bf16[8,16,512]{2,1,0:T(8,128)(2,1)S(1)}, u32[]{:S(2)}, u32[]{:S(2)}) async-start(bf16[8,16,512]{2,1,0:T(8,128)(2,1)} %pad_maximum_fusion), calls=%async_computation.5 | async-start | bytes 262144 | tf_op jit(solution)/shard_map/all_to_all | solution.py:509
  (40 other events, 368.7 us)

commit v6 on v4

--- a/solution.py
+++ b/solution.py
@@ -1,3 +1,5 @@
+import functools
+
 import jax
 import jax.numpy as jnp
 from jax import lax
@@ -12,30 +14,51 @@
 GROUP = HEADS // KV_HEADS
 BLOCK_ROWS = 48
 QUERY_TILE = 128
-
-
-def outgoing_kernel(send, *refs):
-    *sources, out = refs
-    at = 0
-    for ref in sources:
-        out[0, :, at : at + ref.shape[1]] = ref[...]
-        at += ref.shape[1]
+EARLY = 3
+
+
+def outgoing_kernel(columns, send, *refs):
+    count = len(columns)
+    sources, out, held = refs[:count], refs[count], refs[count + 1 : -2]
+    came, gone = refs[-2:]
+    blocks = held[0].shape[0]
+
+    def fetch(b, i):
+        width, first = columns[i]
+        rows = pl.ds(b * BLOCK_ROWS, BLOCK_ROWS)
+        part = sources[i].at[rows, pl.ds(first * width, width)]
+        return pltpu.make_async_copy(part, held[i].at[b], came.at[b, i])
+
+    def store(b, i):
+        at = sum(width for width, _ in columns[:i])
+        part = out.at[send[b], :, pl.ds(at, columns[i][0])]
+        return pltpu.make_async_copy(held[i].at[b], part, gone.at[b, i])
+
+    steps = [(b, i) for b in range(blocks) for i in range(count)]
+    for b, i in steps:
+        fetch(b, i).start()
+    for b, i in steps:
+        fetch(b, i).wait()
+        store(b, i).start()
+    for b, i in steps:
+        store(b, i).wait()
 
 
 def outgoing_slots(send, sources, peers):
     blocks = send.shape[0]
-    width = sum(columns for _, columns, _ in sources)
+    columns = tuple((width, first) for _, width, first in sources)
+    width = sum(part for part, _ in columns)
     dtype = sources[0][0].dtype
-    return pl.pallas_call(
-        outgoing_kernel,
+    anywhere = pl.BlockSpec(memory_space=pl.ANY)
+    return pl.pallas_call(
+        functools.partial(outgoing_kernel, columns),
         grid_spec=pltpu.PrefetchScalarGridSpec(
             num_scalar_prefetch=1,
-            grid=(blocks,),
-            in_specs=[
-                pl.BlockSpec((BLOCK_ROWS, columns), lambda b, send, at=at: (b, at))
-                for _, columns, at in sources
-            ],
-            out_specs=pl.BlockSpec((1, BLOCK_ROWS, width), lambda b, send: (send[b], 0, 0)),
+            grid=(1,),
+            in_specs=[anywhere] * len(columns),
+            out_specs=anywhere,
+            scratch_shapes=[pltpu.VMEM((blocks, BLOCK_ROWS, part), dtype) for part, _ in columns]
+            + [pltpu.SemaphoreType.DMA((blocks, len(columns)))] * 2,
         ),
         out_shape=jax.ShapeDtypeStruct((peers, BLOCK_ROWS, width), dtype),
         name="outgoing_slots",
@@ -99,9 +122,9 @@
 
 
 def pack_kernel(core, place, *refs):
-    *own, swapped, out = refs
-    sources = [ref.at[core[0]] for ref in own]
-    sources += [swapped.at[o, core[0]] for o in range(swapped.shape[0])]
+    out = refs[-1]
+    *own, swapped = refs[:-1]
+    sources = [ref.at[core[0]] for ref in own] + [swapped.at[o] for o in range(swapped.shape[0])]
     for o, ref in enumerate(sources):
 
         @pl.when(place[o] >= 0)
@@ -111,7 +134,7 @@
 
 
 def pack(core, place, own, swapped, rows):
-    width = swapped.shape[3]
+    width = swapped.shape[2]
     shape = (2, BLOCK_ROWS, width)
     return pl.pallas_call(
         pack_kernel,
@@ -119,27 +142,49 @@
             num_scalar_prefetch=2,
             grid=(1,),
             in_specs=[pl.BlockSpec(shape, lambda k, *_: (0, 0, 0))] * len(own)
-            + [pl.BlockSpec((len(own),) + shape, lambda k, *_: (0, 0, 0, 0))],
+            + [pl.BlockSpec(swapped.shape, lambda k, *_: (0, 0, 0))],
             out_specs=pl.BlockSpec((rows, width), lambda k, *_: (0, 0)),
         ),
         out_shape=jax.ShapeDtypeStruct((rows, width), swapped.dtype),
+        name="pack_values",
     )(core, place, *own, swapped)
 
 
-def pick_kernel(column, in_ref, out_ref):
-    out_ref[...] = in_ref[...]
+def pick_kernel(tile, column, source, out, held, came, gone):
+    steps = held.shape[0]
+
+    def fetch(z):
+        first = pl.multiple_of(column[z] * tile, tile)
+        return pltpu.make_async_copy(source.at[:, pl.ds(first, tile)], held.at[z], came.at[z])
+
+    def store(z):
+        return pltpu.make_async_copy(held.at[z], out.at[:, pl.ds(z * tile, tile)], gone.at[z])
+
+    for z in range(steps):
+        fetch(z).start()
+    for z in range(steps):
+        fetch(z).wait()
+        store(z).start()
+    for z in range(steps):
+        store(z).wait()
 
 
 def pick_columns(column, array, tile):
     rows = array.shape[0]
     steps = column.shape[0]
-    return pl.pallas_call(
-        pick_kernel,
+    anywhere = pl.BlockSpec(memory_space=pl.ANY)
+    return pl.pallas_call(
+        functools.partial(pick_kernel, tile),
         grid_spec=pltpu.PrefetchScalarGridSpec(
             num_scalar_prefetch=1,
-            grid=(steps,),
-            in_specs=[pl.BlockSpec((rows, tile), lambda z, column: (0, column[z]))],
-            out_specs=pl.BlockSpec((rows, tile), lambda z, column: (0, z)),
+            grid=(1,),
+            in_specs=[anywhere],
+            out_specs=anywhere,
+            scratch_shapes=[
+                pltpu.VMEM((steps, rows, tile), array.dtype),
+                pltpu.SemaphoreType.DMA((steps,)),
+                pltpu.SemaphoreType.DMA((steps,)),
+            ],
         ),
         out_shape=jax.ShapeDtypeStruct((rows, tile * steps), array.dtype),
         name="pick_columns",
@@ -372,13 +417,17 @@
     return sorted(range(count), key=lambda d: -min(d, count - d))
 
 
-def gather_ring(array, at, size, shift):
+def gather_ring(array, at, size, shift, relay):
     cut = array.shape[0] // 2
     before, after = shift(array, 1), shift(array, -1)
-    top, low = shift(before[:cut], 1), shift(after[cut:], -1)
+    if relay:
+        far = [(0, shift(before[:cut], 1)), (cut, shift(after[cut:], -1))]
+    else:
+        far = [(0, shift(array, 2))]
+    pieces = [(0, 0, array), (1, 0, before), (3, 0, after)] + [(2, row, part) for row, part in far]
     out = jnp.zeros((size,) + array.shape, array.dtype)
     none = (0,) * (array.ndim - 1)
-    for step, row, piece in ((0, 0, array), (1, 0, before), (2, 0, top), (2, cut, low), (3, 0, after)):
+    for step, row, piece in pieces:
         out = lax.dynamic_update_slice(out, piece[None], ((at + size - step) % size, row) + none)
     return out
 
@@ -419,18 +468,19 @@
     def which(table, devices):
         return jnp.sum(jnp.where(table[None, :] == devices[:, None], number + 1, 0), axis=1) - 1
 
-    wide = queries.shape[1] // 2
+    late = KV_HEADS - EARLY
+    wide = GROUP * HEAD_DIM
     keys = key_rows.shape[1]
-    slots = outgoing_slots(send, [(queries, wide, 0), (key_rows, keys, 0)], dp_count)
+    slots = outgoing_slots(send, [(queries, EARLY * wide, 0), (key_rows, keys, 0)], dp_count)
     arrived_one = lax.all_to_all(slots, "dp", 0, 0, tiled=True)
-    slots = outgoing_slots(send, [(queries, wide, 1)], dp_count)
+    slots = outgoing_slots(send, [(queries, wide, EARLY + g) for g in range(late)], dp_count)
     arrived_two = lax.all_to_all(slots, "dp", 0, 0, tiled=True)
 
     width = value_weight.shape[1] // 2
     half = lax.dynamic_slice_in_dim(value_weight, core * width, width, axis=1)
     x, y = fsdp // side, fsdp % side
-    line = gather_ring(half, x, side, along_x)
-    own = gather_ring(line, y, side, along_y)
+    line = gather_ring(half, x, side, along_x, False)
+    own = gather_ring(line, y, side, along_y, True)
     own = jnp.transpose(own, (1, 0, 2, 3)).reshape(depth, width)
     (other,) = swap([own])
 
@@ -441,7 +491,8 @@
     place = which(take, origin)
     leaving = value_blocks(core_of, block, normed, own, other)
     landed = along_z(leaving)
-    (swapped,) = swap([jnp.stack(landed)])
+    leave = [lax.dynamic_index_in_dim(a, 1 - core, 0, keepdims=False) for a in landed]
+    (swapped,) = swap([jnp.stack(leave)])
     packed_v = pack(core_of, place, landed, swapped, rows)
 
     column = 2 * jnp.arange(planes, dtype=jnp.int32)
@@ -452,15 +503,14 @@
     (partner,) = swap([send_to])
     sends = jnp.concatenate([send_to, partner], axis=0)
 
-    half_groups = KV_HEADS // 2
-    key_at = wide // HEAD_DIM
+    key_at = EARLY * GROUP
     done = attention(
         take, arrived_one, arrived_one, packed_v, out_grad, doc_ids,
-        0, half_groups, key_at, (),
+        0, EARLY, key_at, (),
     )
     query_grad, key_grad, value_grad, returning = attention(
         take, arrived_two, arrived_one, packed_v, out_grad, doc_ids,
-        half_groups, half_groups, key_at, done,
+        EARLY, late, key_at, done,
     )
     landed = lax.all_to_all(returning, "dp", 0, 0, tiled=True)
     (swapped,) = swap([landed])

time: 254 us -> 237 us (0.933)
  Pallas kernels: 65.3 us -> 55.9 us
  local copies, waits for them, and re-layouts: 13.5 us -> 7.32 us
  waiting for transfers between devices: 78 us -> 74.6 us
    pallas_call x3, Pallas kernels: 17.6 us -> 8.68 us  [the longest x2 5.58 us: outgoing_slots(): pl.pallas_call(functools.partial(outgoing_kernel, columns), grid_spec=plt...]
    ppermute x7, waiting for transfers between devices: 30.4 us -> 21.9 us  [along_z(): lax.ppermute(a, 'dp', ring((dp_count, planes), d, 2))]
    all_to_all x1, waiting for transfers between devices: 15.3 us -> 10.2 us  [local(): arrived_one = lax.all_to_all(slots, 'dp', 0, 0, tiled=True)]
    dynamic_update_slice x10 -> x9, local copies, waits for them, and re-layouts: 6 us -> 1.27 us  [gather_ring(): lax.dynamic_update_slice(out, piece[None], ((at + size - step) % size, ro...]
    ppermute x4 -> x3, waiting for transfers between devices: 2.22 us -> 5.63 us  [along_x(): return lax.ppermute(array, 'fsdp', ring((fsdp_count, side), step, side))]
    all_to_all x1, starting transfers between devices: 4.6 us -> 7.6 us  [local(): arrived_two = lax.all_to_all(slots, 'dp', 0, 0, tiled=True)]
    all_to_all x1, waiting for transfers between devices: 13.6 us -> 16.5 us  [local(): landed = lax.all_to_all(returning, 'dp', 0, 0, tiled=True)]
    ppermute x5, waiting for transfers between devices: 2.26 us -> 4.86 us  [swap(): return [lax.ppermute(a, 'dp', cores) for a in arrays]]
  transfers between devices with their start and end apart: 24 -> 23, of which waited for: 13 -> 16; matrix products, arithmetic and copies ran while one was open for 5% -> 3% of each run, Pallas kernels for 20% -> 18%
where the time goes in v6:
time: 237 us; the launch traced here: 235 us
  waiting for transfers between devices  74.6 us (31%)
  Pallas kernels  55.9 us (24%)
  starting transfers between devices  55.4 us (23%)
  blocking collectives  35.9 us (15%)
  local copies, waits for them, and re-layouts  7.32 us (3%)
  other arithmetic  4.74 us (2%)
    all_to_all x1, blocking collectives, local(): chips = lax.all_to_all(chip, 'fsdp', 0, 0, tiled=True)  35.9 us
    ppermute x7, waiting for transfers between devices, along_z(): lax.ppermute(a, 'dp', ring((dp_count, planes), d, 2))  21.9 us
    ppermute x7, starting transfers between devices, along_z(): lax.ppermute(a, 'dp', ring((dp_count, planes), d, 2))  17.7 us
    pallas_call x2, Pallas kernels, attention(): pl.pallas_call(attention_kernel, grid_spec=pltpu.PrefetchScalarGridSpec(n...  17 us
    all_to_all x1, waiting for transfers between devices, local(): landed = lax.all_to_all(returning, 'dp', 0, 0, tiled=True)  16.5 us
    ppermute x4, waiting for transfers between devices, along_y(): return lax.ppermute(array, 'fsdp', ring((fsdp_count, side), step, 1))  14.3 us
    all_to_all x1, waiting for transfers between devices, local(): arrived_one = lax.all_to_all(slots, 'dp', 0, 0, tiled=True)  10.2 us
    pallas_call x1, Pallas kernels, input_gradient(): pl.pallas_call(input_grad_kernel, grid_spec=pltpu.PrefetchScalarGridSpec(...  7.78 us
  transfers between devices with their start and end apart: 23, of which 16 were waited for; matrix products, arithmetic and copies ran while one was open for 3% of the time, Pallas kernels for 18%

profile of v6, /device:TPU:0, one launch (start us, length us, event | category | flops | bytes accessed | tf_op | source)
XLA Modules:
  0.0 235.0 jit_solution(9356465143640490009)
XLA Ops:
  0.6 3.1 %outgoing_slots.3 = bf16[16,48,2048]{2,1,0:T(8,128)(2,1)} custom-call(s32[8]{0:T(128)} %bitcast.36, bf16[384,2048]{1,0:T(8,128)(2,1)} %refs_0_.3, bf16[384,512]{1,0:T(8,128)(2,1)} %refs_1_.1), custom_call_target="tpu_custom_call" | custom-call | tf_op jit(solution)/shard_map/outgoing_slots/pallas_call | solution.py:53
  3.7 7.1 %all-to-all-start.1 = ((bf16[16,48,2048]{2,1,0:T(8,128)(2,1)}), bf16[16,48,2048]{2,1,0:T(8,128)(2,1)}, u32[]{:S(2)}, u32[]{:S(2)}) async-start(bf16[16,48,2048]{2,1,0:T(8,128)(2,1)} %outgoing_slots.3), calls=%async_computation.1 | async-start | bytes 6291456 | tf_op jit(solution)/shard_map/all_to_all | solution.py:475
  10.9 1.6 collective-permute-start
  12.5 1.7 collective-permute-start.1
  14.2 1.8 collective-permute-start.2
  16.1 1.9 collective-permute-done
  17.9 2.1 collective-permute-done.1
  20.0 1.7 collective-permute-done.2
  21.7 1.7 collective-permute-start.3
  23.4 1.7 collective-permute-start.4
  25.3 11.1 %collective-permute-done.3 = bf16[4,256,256]{2,1,0:T(8,128)(2,1)S(1)} collective-permute-done((bf16[4,256,256]{2,1,0:T(8,128)(2,1)S(1)}, bf16[4,256,256]{2,1,0:T(8,128)(2,1)S(1)}, u32[]{:S(2)}, u32[]{:S(2)}) %collective-permute-start.3) | collective-permute-done | bytes 524320 | tf_op jit(solution)/shard_map/ppermute | solution.py:466
  36.9 1.0 slice.9
  37.8 3.0 %collective-permute-start.6 = (bf16[2,256,256]{2,1,0:T(8,128)(2,1)S(1)}, bf16[2,256,256]{2,1,0:T(8,128)(2,1)S(1)}, u32[]{:S(2)}, u32[]{:S(2)}) collective-permute-start(bf16[2,256,256]{2,1,0:T(8,128)(2,1)S(1)} %slice.9), channel_id=1, source_target_pairs={{0,3},{1,0},{2,1},{3,2},{4,7},{5,4},{6,5},{7,6},{8,11},{9,8},{10,9... | collective-permute-start | bytes 786440 | tf_op jit(solution)/shard_map/ppermute | solution.py:466
  40.9 1.1 bitcast_dynamic-update-slice_fusion
  42.0 2.9 %collective-permute-done.5 = bf16[2,256,256]{2,1,0:T(8,128)(2,1)S(1)} collective-permute-done((bf16[2,256,256]{2,1,0:T(8,128)(2,1)S(1)}, bf16[2,256,256]{2,1,0:T(8,128)(2,1)S(1)}, u32[]{:S(2)}, u32[]{:S(2)}) %collective-permute-start.5) | collective-permute-done | bytes 262176 | tf_op jit(solution)/shard_map/ppermute | solution.py:466
  45.7 0.7 add_maximum_fusion.block
  46.4 3.2 %collective-permute-done.7.other_ref = bf16[4096,256]{1,0:T(8,128)(2,1)} collective-permute-done((bf16[4096,256]{1,0:T(8,128)(2,1)S(1)}, bf16[4096,256]{1,0:T(8,128)(2,1)}, u32[]{:S(2)}, u32[]{:S(2)}) %collective-permute-start.7) | collective-permute-done | bytes 2097184 | tf_op jit(solution)/shard_map/ppermute | solution.py:460
  49.6 6.6 %value_blocks.1 = (bf16[2,48,512]{2,1,0:T(8,128)(2,1)}, bf16[2,48,512]{2,1,0:T(8,128)(2,1)}, bf16[2,48,512]{2,1,0:T(8,128)(2,1)}, bf16[2,48,512]{2,1,0:T(8,128)(...) custom-call(s32[1]{0:T(128)} %bitcast.2.core, ...), custom_call_target="tpu_custom_call" | custom-call | flops 1610612736 | bytes 7340032 | tf_op jit(solution)/shard_map/value_blocks/pallas_call | solution.py:101
  56.2 5.3 %collective-permute-start.8 = (bf16[2,48,512]{2,1,0:T(8,128)(2,1)}, bf16[2,48,512]{2,1,0:T(8,128)(2,1)S(1)}, u32[]{:S(2)}, u32[]{:S(2)}) collective-permute-start(bf16[2,48,512]{2,1,0:T(8,128)(2,1)} %get-tuple-element.20), channel_id=1, source_target_pairs={{0,128},{16,144},{32,160},{48,176},{64,192},{80,208},{96,224},{112... | collective-permute-start | bytes 294920 | tf_op jit(solution)/shard_map/ppermute | solution.py:455
  61.5 2.5 %outgoing_slots.2 = bf16[16,48,512]{2,1,0:T(8,128)(2,1)} custom-call(s32[8]{0:T(128)} %bitcast.37, bf16[384,2048]{1,0:T(8,128)(2,1)} %refs_0_.3), custom_call_target="tpu_custom_call" | custom-call | tf_op jit(solution)/shard_map/outgoing_slots/pallas_call | solution.py:53
  64.7 4.5 %collective-permute-start.10 = (bf16[2,48,512]{2,1,0:T(8,128)(2,1)S(1)}, bf16[2,48,512]{2,1,0:T(8,128)(2,1)S(1)}, u32[]{:S(2)}, u32[]{:S(2)}) collective-permute-start(bf16[2,48,512]{2,1,0:T(8,128)(2,1)S(1)} %copy-done.24), channel_id=1, source_target_pairs={{0,160},{16,176},{32,192},{48,208},{64,224},{80,240},{96,0},{112,1... | collective-permute-start | bytes 294920 | tf_op jit(solution)/shard_map/ppermute | solution.py:455
  69.6 3.8 %collective-permute-start.12 = (bf16[2,48,512]{2,1,0:T(8,128)(2,1)S(1)}, bf16[2,48,512]{2,1,0:T(8,128)(2,1)S(1)}, u32[]{:S(2)}, u32[]{:S(2)}) collective-permute-start(bf16[2,48,512]{2,1,0:T(8,128)(2,1)S(1)} %copy-done.22), channel_id=1, source_target_pairs={{0,192},{16,208},{32,224},{48,240},{64,0},{80,16},{96,32},{112,48}... | collective-permute-start | bytes 294920 | tf_op jit(solution)/shard_map/ppermute | solution.py:455
  73.3 10.2 %all-to-all-done.1.q_ref.k_ref = bf16[16,48,2048]{2,1,0:T(8,128)(2,1)} async-done(((bf16[16,48,2048]{2,1,0:T(8,128)(2,1)}), bf16[16,48,2048]{2,1,0:T(8,128)(2,1)}, u32[]{:S(2)}, u32[]{:S(2)}) %all-to-all-start.1) | async-done | bytes 3145760 | tf_op jit(solution)/shard_map/all_to_all | solution.py:475
  83.5 7.6 %all-to-all-start = ((bf16[16,48,512]{2,1,0:T(8,128)(2,1)}), bf16[16,48,512]{2,1,0:T(8,128)(2,1)S(1)}, u32[]{:S(2)}, u32[]{:S(2)}) async-start(bf16[16,48,512]{2,1,0:T(8,128)(2,1)} %outgoing_slots.2), calls=%async_computation | async-start | bytes 1572864 | tf_op jit(solution)/shard_map/all_to_all | solution.py:477
  91.2 2.6 %collective-permute-done.8.refs_0_ = bf16[2,48,512]{2,1,0:T(8,128)(2,1)S(1)} collective-permute-done((bf16[2,48,512]{2,1,0:T(8,128)(2,1)}, bf16[2,48,512]{2,1,0:T(8,128)(2,1)S(1)}, u32[]{:S(2)}, u32[]{:S(2)}) %collective-permute-start.8) | collective-permute-done | bytes 98336 | tf_op jit(solution)/shard_map/ppermute | solution.py:455
  94.0 3.1 %collective-permute-start.14 = (bf16[2,48,512]{2,1,0:T(8,128)(2,1)S(1)}, bf16[2,48,512]{2,1,0:T(8,128)(2,1)S(1)}, u32[]{:S(2)}, u32[]{:S(2)}) collective-permute-start(bf16[2,48,512]{2,1,0:T(8,128)(2,1)S(1)} %copy-done.20), channel_id=1, source_target_pairs={{0,224},{16,240},{32,0},{48,16},{64,32},{80,48},{96,64},{112,80},{... | collective-permute-start | bytes 294920 | tf_op jit(solution)/shard_map/ppermute | solution.py:455
  97.1 1.4 collective-permute-done.11.refs_3_
  98.6 17.7 %collective-permute-done.13.refs_5_ = bf16[2,48,512]{2,1,0:T(8,128)(2,1)S(1)} collective-permute-done((bf16[2,48,512]{2,1,0:T(8,128)(2,1)S(1)}, bf16[2,48,512]{2,1,0:T(8,128)(2,1)S(1)}, u32[]{:S(2)}, u32[]{:S(2)}) %collective-permute-start.13) | collective-permute-done | bytes 98336 | tf_op jit(solution)/shard_map/ppermute | solution.py:455
  116.4 0.8 copy.32.doc_col
  118.2 0.7 copy-done.5
  118.9 2.9 %pack_values.1.v_ref = bf16[384,512]{1,0:T(8,128)(2,1)} custom-call(s32[1]{0:T(128)} %bitcast.2.core, s32[16]{0:T(128)} %broadcast_add_fusion.place, bf16[2,48,512]{2,1,0:T(8,128)(2,1)} %copy-done.7, bf16[2,48,512]{2,1,0:T(8,128)(2,1)} %copy-done.8, bf16[2,48,512]{2,1,0:T(8,128)(2,1)} %copy-done.9, bf16[2,48,512]{2,1,0:T(8,128)(2,1)} %copy-done.10, ...), custom_call_target="tpu_custom_call" | custom-call | tf_op jit(solution)/shard_map/pack_values/pallas_call | solution.py:139
  121.8 11.4 %attention_backward.2 = (bf16[384,2048]{1,0:T(8,128)(2,1)}, bf16[384,512]{1,0:T(8,128)(2,1)}, bf16[384,512]{1,0:T(8,128)(2,1)}, bf16[16,48,512]{2,1,0:T(8,128)(2,1)}) custom-call(s32[8]{0:T(128)} %bitcast.40, bf16[16,48,2048]{2,1,0:T(8,128)(2,1)} %all-to-all-done.1.q_ref.k_ref, bf16[16,48,2048]{2,1,0:T(8,128)(2,1)} %all-to-all-done.1.q_ref.k_ref, ...), custom_call_target="tpu_custom_call" | custom-call | flops 2717908992 | bytes 5898240 | tf_op jit(solution)/shard_map/attention_backward/pallas_call | solution.py:321
  133.2 0.9 copy-done.1
  134.1 5.6 %attention_backward.3 = (bf16[384,2048]{1,0:T(8,128)(2,1)}, bf16[384,512]{1,0:T(8,128)(2,1)}, bf16[384,512]{1,0:T(8,128)(2,1)}, bf16[16,48,512]{2,1,0:T(8,128)(2,1)}) custom-call(s32[8]{0:T(128)} %bitcast.41, bf16[16,48,512]{2,1,0:T(8,128)(2,1)} %copy-done.1, ...), custom_call_target="tpu_custom_call", output_to_operand_aliasing={{0}: (7, {}), {1}: (8, {}), {2}: (9, {}), {3}: (10, {})} | custom-call | flops 905969664 | bytes 1966080 | tf_op jit(solution)/shard_map/attention_backward/pallas_call | solution.py:321
  139.7 4.6 %all-to-all-start.2 = ((bf16[16,48,512]{2,1,0:T(8,128)(2,1)}), bf16[16,48,512]{2,1,0:T(8,128)(2,1)S(1)}, u32[]{:S(2)}, u32[]{:S(2)}) async-start(bf16[16,48,512]{2,1,0:T(8,128)(2,1)} %get-tuple-element.35), calls=%async_computation.2 | async-start | bytes 1572864 | tf_op jit(solution)/shard_map/all_to_all | solution.py:515
  144.8 3.1 %pick_columns.1 = bf16[384,2048]{1,0:T(8,128)(2,1)} custom-call(s32[8]{0:T(128)} %add_subtract_fusion.column, bf16[384,4096]{1,0:T(8,128)(2,1)} %own_ref.1), custom_call_target="tpu_custom_call" | custom-call | tf_op jit(solution)/shard_map/pick_columns/pallas_call | solution.py:176
  148.4 16.5 %all-to-all-done.2.landed_ref = bf16[16,48,512]{2,1,0:T(8,128)(2,1)S(1)} async-done(((bf16[16,48,512]{2,1,0:T(8,128)(2,1)}), bf16[16,48,512]{2,1,0:T(8,128)(2,1)S(1)}, u32[]{:S(2)}, u32[]{:S(2)}) %all-to-all-start.2) | async-done | bytes 786464 | tf_op jit(solution)/shard_map/all_to_all | solution.py:515
  164.9 2.5 %collective-permute-start.18 = (bf16[16,48,512]{2,1,0:T(8,128)(2,1)S(1)}, bf16[16,48,512]{2,1,0:T(8,128)(2,1)S(1)}, u32[]{:S(2)}, u32[]{:S(2)}) collective-permute-start(bf16[16,48,512]{2,1,0:T(8,128)(2,1)S(1)} %all-to-all-done.2.landed_ref), channel_id=1, source_target_pairs={{0,16},{16,0},{32,48},{48,32},{64,80},{80,64},{96,112},{112,96},{1... | collective-permute-start | bytes 2359304 | tf_op jit(solution)/shard_map/ppermute | solution.py:460
  168.0 1.3 collective-permute-done.16
  169.9 1.2 copy-done.3
  171.1 7.4 %turn_columns.1.turned_ref = bf16[2048,768]{1,0:T(8,128)(2,1)} custom-call(s32[8]{0:T(128)} %fusion.4.column, bf16[384,4096]{1,0:T(8,128)(2,1)} %own_ref.1, bf16[384,2048]{1,0:T(8,128)(2,1)} %copy-done.3), custom_call_target="tpu_custom_call" | custom-call | tf_op jit(solution)/shard_map/turn_columns/pallas_call | solution.py:203
  178.5 0.9 copy-done.4
  179.5 5.6 %weight_part.1 = bf16[16,8,16,512]{3,2,1,0:T(8,128)(2,1)} custom-call(s32[2,8]{1,0:T(2,128)} %pad_add_fusion.send, bf16[2048,768]{1,0:T(8,128)(2,1)} %turn_columns.1.turned_ref, bf16[16,48,512]{2,1,0:T(8,128)(2,1)} %copy-done.2, bf16[16,48,512]{2,1,0:T(8,128)(2,1)} %copy-done.4), custom_call_target="tpu_custom_call" | custom-call | tf_op jit(solution)/shard_map/weight_part/pallas_call | solution.py:390
  185.0 35.9 %all_to_all.25 = bf16[16,8,16,512]{3,2,1,0:T(8,128)(2,1)S(1)} all-to-all(bf16[16,8,16,512]{3,2,1,0:T(8,128)(2,1)} %weight_part.1), channel_id=1, replica_groups=mesh['dp'=16,'fsdp'=16] {'fsdp'}, dimensions={0} | all-to-all | bytes 4194304 | tf_op jit(solution)/shard_map/all_to_all | solution.py:520
  221.0 1.1 reduce_sum.41
  222.0 3.4 %all-to-all-start.4 = ((bf16[8,16,512]{2,1,0:T(8,128)(2,1)}), bf16[8,16,512]{2,1,0:T(8,128)(2,1)S(1)}, u32[]{:S(2)}, u32[]{:S(2)}) async-start(bf16[8,16,512]{2,1,0:T(8,128)(2,1)} %reduce_sum.41), calls=%async_computation.4 | async-start | bytes 262144 | tf_op jit(solution)/shard_map/all_to_all | solution.py:523
  225.4 7.8 %input_gradient.1 = bf16[384,4096]{1,0:T(8,128)(2,1)} custom-call(s32[1]{0:T(128)} %bitcast.2.core, bf16[384,512]{1,0:T(8,128)(2,1)} %get-tuple-element.34.grad_ref, bf16[4096,256]{1,0:T(8,128)(2,1)} %bitcast.35, bf16[4096,256]{1,0:T(8,128)(2,1)} %collective-permute-done.7.other_ref), custom_call_target="tpu_custom_call" | custom-call | flops 1610612736 | bytes 7340032 | tf_op jit(solution)/shard_map/input_gradient/pallas_call | solution.py:231
  233.2 1.2 all-to-all-done.4
  (101 shorter events, 6.7 us)
Async XLA Ops:
  3.7 7.2 %copy-start.14 = (bf16[256,512]{1,0:T(8,128)(2,1)S(1)}, bf16[256,512]{1,0:T(8,128)(2,1)}, u32[]{:S(2)}) copy-start(bf16[256,512]{1,0:T(8,128)(2,1)} %param.13) | copy-start | bytes 786436
  3.7 79.8 %all-to-all-start.1 = ((bf16[16,48,2048]{2,1,0:T(8,128)(2,1)}), bf16[16,48,2048]{2,1,0:T(8,128)(2,1)}, u32[]{:S(2)}, u32[]{:S(2)}) async-start(bf16[16,48,2048]{2,1,0:T(8,128)(2,1)} %outgoing_slots.3), calls=%async_computation.1 | async-start | bytes 6291456 | tf_op jit(solution)/shard_map/all_to_all | solution.py:475
  10.9 7.0 %collective-permute-start = (bf16[256,256]{1,0:T(8,128)(2,1)S(1)}, bf16[256,256]{1,0:T(8,128)(2,1)S(1)}, u32[]{:S(2)}, u32[]{:S(2)}) collective-permute-start(bf16[256,256]{1,0:T(8,128)(2,1)S(1)} %get-tuple-element.39), channel_id=1, source_target_pairs={{0,4},{1,5},{2,6},{3,7},{4,8},{5,9},{6,10},{7,11},{8,12},{9,13},{1... | collective-permute-start | bytes 393224 | tf_op jit(solution)/shard_map/ppermute | solution.py:463
  12.5 7.5 %collective-permute-start.1 = (bf16[256,256]{1,0:T(8,128)(2,1)S(1)}, bf16[256,256]{1,0:T(8,128)(2,1)S(1)}, u32[]{:S(2)}, u32[]{:S(2)}) collective-permute-start(bf16[256,256]{1,0:T(8,128)(2,1)S(1)} %get-tuple-element.39), channel_id=1, source_target_pairs={{0,12},{1,13},{2,14},{3,15},{4,0},{5,1},{6,2},{7,3},{8,4},{9,5},{1... | collective-permute-start | bytes 393224 | tf_op jit(solution)/shard_map/ppermute | solution.py:463
  14.2 7.5 %collective-permute-start.2 = (bf16[256,256]{1,0:T(8,128)(2,1)S(1)}, bf16[256,256]{1,0:T(8,128)(2,1)S(1)}, u32[]{:S(2)}, u32[]{:S(2)}) collective-permute-start(bf16[256,256]{1,0:T(8,128)(2,1)S(1)} %get-tuple-element.39), channel_id=1, source_target_pairs={{0,8},{1,9},{2,10},{3,11},{4,12},{5,13},{6,14},{7,15},{8,0},{9,1},... | collective-permute-start | bytes 393224 | tf_op jit(solution)/shard_map/ppermute | solution.py:463
  21.7 14.7 %collective-permute-start.3 = (bf16[4,256,256]{2,1,0:T(8,128)(2,1)S(1)}, bf16[4,256,256]{2,1,0:T(8,128)(2,1)S(1)}, u32[]{:S(2)}, u32[]{:S(2)}) collective-permute-start(bf16[4,256,256]{2,1,0:T(8,128)(2,1)S(1)} %bitcast_dynamic-update-slice_fusion.5), channel_id=1, source_target_pairs={{0,1},{1,2},{2,3},{3,0},{4,5},{5,6},{6,7},{7,4},{8,9},{9,10},{10,1... | collective-permute-start | bytes 1572872 | tf_op jit(solution)/shard_map/ppermute | solution.py:466
  23.4 13.5 %collective-permute-start.4 = (bf16[4,256,256]{2,1,0:T(8,128)(2,1)S(1)}, bf16[4,256,256]{2,1,0:T(8,128)(2,1)}, u32[]{:S(2)}, u32[]{:S(2)}) collective-permute-start(bf16[4,256,256]{2,1,0:T(8,128)(2,1)S(1)} %bitcast_dynamic-update-slice_fusion.5), channel_id=1, source_target_pairs={{0,3},{1,0},{2,1},{3,2},{4,7},{5,4},{6,5},{7,6},{8,11},{9,8},{10,9... | collective-permute-start | bytes 1572872 | tf_op jit(solution)/shard_map/ppermute | solution.py:466
  25.3 20.0 %copy-start.26 = (s32[8]{0:T(128)S(1)}, s32[8]{0:T(128)}, u32[]{:S(2)}) copy-start(s32[8]{0:T(128)} %constant.156.clone) | copy-start | bytes 100
  25.3 20.2 %copy-start.19 = (s32[8]{0:T(128)S(1)}, s32[8]{0:T(128)}, u32[]{:S(2)}) copy-start(s32[8]{0:T(128)} %constant.164) | copy-start | bytes 100
  25.3 20.3 %copy-start.15 = (s32[1,8]{1,0:T(1,128)S(1)}, s32[1,8]{1,0:T(1,128)}, u32[]{:S(2)}) copy-start(s32[1,8]{1,0:T(1,128)} %param.15) | copy-start | bytes 100
  25.3 20.3 %copy-start.18 = (s32[1,8]{1,0:T(1,128)S(1)}, s32[1,8]{1,0:T(1,128)}, u32[]{:S(2)}) copy-start(s32[1,8]{1,0:T(1,128)} %param.16) | copy-start | bytes 100
  36.5 8.4 %collective-permute-start.5 = (bf16[2,256,256]{2,1,0:T(8,128)(2,1)S(1)}, bf16[2,256,256]{2,1,0:T(8,128)(2,1)S(1)}, u32[]{:S(2)}, u32[]{:S(2)}) collective-permute-start(bf16[2,256,256]{2,1,0:T(8,128)(2,1)S(1)} %slice.8), channel_id=1, source_target_pairs={{0,1},{1,2},{2,3},{3,0},{4,5},{5,6},{6,7},{7,4},{8,9},{9,10},{10,1... | collective-permute-start | bytes 786440 | tf_op jit(solution)/shard_map/ppermute | solution.py:466
  37.8 7.3 %collective-permute-start.6 = (bf16[2,256,256]{2,1,0:T(8,128)(2,1)S(1)}, bf16[2,256,256]{2,1,0:T(8,128)(2,1)S(1)}, u32[]{:S(2)}, u32[]{:S(2)}) collective-permute-start(bf16[2,256,256]{2,1,0:T(8,128)(2,1)S(1)} %slice.9), channel_id=1, source_target_pairs={{0,3},{1,0},{2,1},{3,2},{4,7},{5,4},{6,5},{7,6},{8,11},{9,8},{10,9... | collective-permute-start | bytes 786440 | tf_op jit(solution)/shard_map/ppermute | solution.py:466
  45.2 4.4 %copy-start = (bf16[4,4,256,256]{3,2,0,1:T(8,128)(2,1)}, bf16[4,4,256,256]{3,2,0,1:T(8,128)(2,1)S(1)}, u32[]{:S(2)}) copy-start(bf16[4,4,256,256]{3,2,0,1:T(8,128)(2,1)S(1)} %bitcast_dynamic-update-slice_fusion.4) | copy-start | bytes 6291460
  45.2 4.4 %collective-permute-start.7 = (bf16[4096,256]{1,0:T(8,128)(2,1)S(1)}, bf16[4096,256]{1,0:T(8,128)(2,1)}, u32[]{:S(2)}, u32[]{:S(2)}) collective-permute-start(bf16[4096,256]{1,0:T(8,128)(2,1)S(1)} %bitcast.33), channel_id=1, source_target_pairs={{0,16},{16,0},{32,48},{48,32},{64,80},{80,64},{96,112},{112,96},{1... | collective-permute-start | bytes 6291464 | tf_op jit(solution)/shard_map/ppermute | solution.py:460
  56.2 7.9 %copy-start.25 = (bf16[2,48,512]{2,1,0:T(8,128)(2,1)S(1)}, bf16[2,48,512]{2,1,0:T(8,128)(2,1)}, u32[]{:S(2)}) copy-start(bf16[2,48,512]{2,1,0:T(8,128)(2,1)} %get-tuple-element.21) | copy-start | bytes 294916
  56.2 8.5 %copy-start.24 = (bf16[2,48,512]{2,1,0:T(8,128)(2,1)S(1)}, bf16[2,48,512]{2,1,0:T(8,128)(2,1)}, u32[]{:S(2)}) copy-start(bf16[2,48,512]{2,1,0:T(8,128)(2,1)} %get-tuple-element.22) | copy-start | bytes 294916
  56.2 13.0 %copy-start.23 = (bf16[2,48,512]{2,1,0:T(8,128)(2,1)S(1)}, bf16[2,48,512]{2,1,0:T(8,128)(2,1)}, u32[]{:S(2)}) copy-start(bf16[2,48,512]{2,1,0:T(8,128)(2,1)} %get-tuple-element.23) | copy-start | bytes 294916
  56.2 13.4 %copy-start.22 = (bf16[2,48,512]{2,1,0:T(8,128)(2,1)S(1)}, bf16[2,48,512]{2,1,0:T(8,128)(2,1)}, u32[]{:S(2)}) copy-start(bf16[2,48,512]{2,1,0:T(8,128)(2,1)} %get-tuple-element.24) | copy-start | bytes 294916
  56.2 37.5 %copy-start.21 = (bf16[2,48,512]{2,1,0:T(8,128)(2,1)S(1)}, bf16[2,48,512]{2,1,0:T(8,128)(2,1)}, u32[]{:S(2)}) copy-start(bf16[2,48,512]{2,1,0:T(8,128)(2,1)} %get-tuple-element.25) | copy-start | bytes 294916
  56.2 37.8 %copy-start.20 = (bf16[2,48,512]{2,1,0:T(8,128)(2,1)S(1)}, bf16[2,48,512]{2,1,0:T(8,128)(2,1)}, u32[]{:S(2)}) copy-start(bf16[2,48,512]{2,1,0:T(8,128)(2,1)} %get-tuple-element.26) | copy-start | bytes 294916
  56.2 37.5 %collective-permute-start.8 = (bf16[2,48,512]{2,1,0:T(8,128)(2,1)}, bf16[2,48,512]{2,1,0:T(8,128)(2,1)S(1)}, u32[]{:S(2)}, u32[]{:S(2)}) collective-permute-start(bf16[2,48,512]{2,1,0:T(8,128)(2,1)} %get-tuple-element.20), channel_id=1, source_target_pairs={{0,128},{16,144},{32,160},{48,176},{64,192},{80,208},{96,224},{112... | collective-permute-start | bytes 294920 | tf_op jit(solution)/shard_map/ppermute | solution.py:455
  61.5 54.8 %copy-start.6 = (bf16[2,48,512]{2,1,0:T(8,128)(2,1)S(1)}, bf16[2,48,512]{2,1,0:T(8,128)(2,1)}, u32[]{:S(2)}) copy-start(bf16[2,48,512]{2,1,0:T(8,128)(2,1)} %get-tuple-element.27.refs_7_) | copy-start | bytes 294916
  61.5 54.9 %copy-start.17 = (s32[1,384]{1,0:T(1,128)S(1)}, s32[1,384]{1,0:T(1,128)}, u32[]{:S(2)}) copy-start(s32[1,384]{1,0:T(1,128)} %doc_row.3) | copy-start | bytes 4612
  64.1 29.9 %collective-permute-start.9 = (bf16[2,48,512]{2,1,0:T(8,128)(2,1)S(1)}, bf16[2,48,512]{2,1,0:T(8,128)(2,1)S(1)}, u32[]{:S(2)}, u32[]{:S(2)}) collective-permute-start(bf16[2,48,512]{2,1,0:T(8,128)(2,1)S(1)} %copy-done.25), channel_id=1, source_target_pairs={{0,96},{16,112},{32,128},{48,144},{64,160},{80,176},{96,192},{112,... | collective-permute-start | bytes 294920 | tf_op jit(solution)/shard_map/ppermute | solution.py:455
  64.7 32.4 %collective-permute-start.10 = (bf16[2,48,512]{2,1,0:T(8,128)(2,1)S(1)}, bf16[2,48,512]{2,1,0:T(8,128)(2,1)S(1)}, u32[]{:S(2)}, u32[]{:S(2)}) collective-permute-start(bf16[2,48,512]{2,1,0:T(8,128)(2,1)S(1)} %copy-done.24), channel_id=1, source_target_pairs={{0,160},{16,176},{32,192},{48,208},{64,224},{80,240},{96,0},{112,1... | collective-permute-start | bytes 294920 | tf_op jit(solution)/shard_map/ppermute | solution.py:455
  69.2 29.3 %collective-permute-start.11 = (bf16[2,48,512]{2,1,0:T(8,128)(2,1)S(1)}, bf16[2,48,512]{2,1,0:T(8,128)(2,1)S(1)}, u32[]{:S(2)}, u32[]{:S(2)}) collective-permute-start(bf16[2,48,512]{2,1,0:T(8,128)(2,1)S(1)} %copy-done.23), channel_id=1, source_target_pairs={{0,64},{16,80},{32,96},{48,112},{64,128},{80,144},{96,160},{112,17... | collective-permute-start | bytes 294920 | tf_op jit(solution)/shard_map/ppermute | solution.py:455
  69.6 29.0 %collective-permute-start.12 = (bf16[2,48,512]{2,1,0:T(8,128)(2,1)S(1)}, bf16[2,48,512]{2,1,0:T(8,128)(2,1)S(1)}, u32[]{:S(2)}, u32[]{:S(2)}) collective-permute-start(bf16[2,48,512]{2,1,0:T(8,128)(2,1)S(1)} %copy-done.22), channel_id=1, source_target_pairs={{0,192},{16,208},{32,224},{48,240},{64,0},{80,16},{96,32},{112,48}... | collective-permute-start | bytes 294920 | tf_op jit(solution)/shard_map/ppermute | solution.py:455
  83.5 49.7 %all-to-all-start = ((bf16[16,48,512]{2,1,0:T(8,128)(2,1)}), bf16[16,48,512]{2,1,0:T(8,128)(2,1)S(1)}, u32[]{:S(2)}, u32[]{:S(2)}) async-start(bf16[16,48,512]{2,1,0:T(8,128)(2,1)} %outgoing_slots.2), calls=%async_computation | async-start | bytes 1572864 | tf_op jit(solution)/shard_map/all_to_all | solution.py:477
  93.8 24.4 %copy-start.7 = (bf16[2,48,512]{2,1,0:T(8,128)(2,1)}, bf16[2,48,512]{2,1,0:T(8,128)(2,1)S(1)}, u32[]{:S(2)}) copy-start(bf16[2,48,512]{2,1,0:T(8,128)(2,1)S(1)} %collective-permute-done.8.refs_0_) | copy-start | bytes 294916
  93.8 22.5 %collective-permute-start.13 = (bf16[2,48,512]{2,1,0:T(8,128)(2,1)S(1)}, bf16[2,48,512]{2,1,0:T(8,128)(2,1)S(1)}, u32[]{:S(2)}, u32[]{:S(2)}) collective-permute-start(bf16[2,48,512]{2,1,0:T(8,128)(2,1)S(1)} %copy-done.21), channel_id=1, source_target_pairs={{0,32},{16,48},{32,64},{48,80},{64,96},{80,112},{96,128},{112,144}... | collective-permute-start | bytes 294920 | tf_op jit(solution)/shard_map/ppermute | solution.py:455
  94.0 24.1 %copy-start.8 = (bf16[2,48,512]{2,1,0:T(8,128)(2,1)}, bf16[2,48,512]{2,1,0:T(8,128)(2,1)S(1)}, u32[]{:S(2)}) copy-start(bf16[2,48,512]{2,1,0:T(8,128)(2,1)S(1)} %collective-permute-done.9.refs_1_) | copy-start | bytes 294916
  94.0 22.3 %collective-permute-start.14 = (bf16[2,48,512]{2,1,0:T(8,128)(2,1)S(1)}, bf16[2,48,512]{2,1,0:T(8,128)(2,1)S(1)}, u32[]{:S(2)}, u32[]{:S(2)}) collective-permute-start(bf16[2,48,512]{2,1,0:T(8,128)(2,1)S(1)} %copy-done.20), channel_id=1, source_target_pairs={{0,224},{16,240},{32,0},{48,16},{64,32},{80,48},{96,64},{112,80},{... | collective-permute-start | bytes 294920 | tf_op jit(solution)/shard_map/ppermute | solution.py:455
  97.1 21.0 %copy-start.9 = (bf16[2,48,512]{2,1,0:T(8,128)(2,1)}, bf16[2,48,512]{2,1,0:T(8,128)(2,1)S(1)}, u32[]{:S(2)}) copy-start(bf16[2,48,512]{2,1,0:T(8,128)(2,1)S(1)} %collective-permute-done.10.refs_2_) | copy-start | bytes 294916
  98.5 19.6 %copy-start.10 = (bf16[2,48,512]{2,1,0:T(8,128)(2,1)}, bf16[2,48,512]{2,1,0:T(8,128)(2,1)S(1)}, u32[]{:S(2)}) copy-start(bf16[2,48,512]{2,1,0:T(8,128)(2,1)S(1)} %collective-permute-done.11.refs_3_) | copy-start | bytes 294916
  98.6 19.6 %copy-start.11 = (bf16[2,48,512]{2,1,0:T(8,128)(2,1)}, bf16[2,48,512]{2,1,0:T(8,128)(2,1)S(1)}, u32[]{:S(2)}) copy-start(bf16[2,48,512]{2,1,0:T(8,128)(2,1)S(1)} %collective-permute-done.12.refs_4_) | copy-start | bytes 294916
  116.3 1.9 copy-start.12
  116.3 1.9 copy-start.13
  116.3 1.8 collective-permute-start.15
  139.7 25.2 %all-to-all-start.2 = ((bf16[16,48,512]{2,1,0:T(8,128)(2,1)}), bf16[16,48,512]{2,1,0:T(8,128)(2,1)S(1)}, u32[]{:S(2)}, u32[]{:S(2)}) async-start(bf16[16,48,512]{2,1,0:T(8,128)(2,1)} %get-tuple-element.35), calls=%async_computation.2 | async-start | bytes 1572864 | tf_op jit(solution)/shard_map/all_to_all | solution.py:515
  144.8 22.6 %copy-start.16 = (s32[1,8]{1,0:T(1,128)S(1)}, s32[1,8]{1,0:T(1,128)}, u32[]{:S(2)}) copy-start(s32[1,8]{1,0:T(1,128)} %param.15) | copy-start | bytes 100
  147.9 22.0 %collective-permute-start.17 = (bf16[384,2048]{1,0:T(8,128)(2,1)}, bf16[384,2048]{1,0:T(8,128)(2,1)S(1)}, u32[]{:S(2)}, u32[]{:S(2)}) collective-permute-start(bf16[384,2048]{1,0:T(8,128)(2,1)} %pick_columns.1), channel_id=1, source_target_pairs={{0,16},{16,0},{32,48},{48,32},{64,80},{80,64},{96,112},{112,96},{1... | collective-permute-start | bytes 4718600 | tf_op jit(solution)/shard_map/ppermute | solution.py:460
  164.9 13.6 %copy-start.2 = (bf16[16,48,512]{2,1,0:T(8,128)(2,1)}, bf16[16,48,512]{2,1,0:T(8,128)(2,1)S(1)}, u32[]{:S(2)}) copy-start(bf16[16,48,512]{2,1,0:T(8,128)(2,1)S(1)} %all-to-all-done.2.landed_ref) | copy-start | bytes 2359300
  164.9 13.6 %collective-permute-start.18 = (bf16[16,48,512]{2,1,0:T(8,128)(2,1)S(1)}, bf16[16,48,512]{2,1,0:T(8,128)(2,1)S(1)}, u32[]{:S(2)}, u32[]{:S(2)}) collective-permute-start(bf16[16,48,512]{2,1,0:T(8,128)(2,1)S(1)} %all-to-all-done.2.landed_ref), channel_id=1, source_target_pairs={{0,16},{16,0},{32,48},{48,32},{64,80},{80,64},{96,112},{112,96},{1... | collective-permute-start | bytes 2359304 | tf_op jit(solution)/shard_map/ppermute | solution.py:460
  167.4 1.9 collective-permute-start.16
  169.9 1.2 copy-start.3
  178.5 0.9 copy-start.4
  222.0 12.4 %all-to-all-start.4 = ((bf16[8,16,512]{2,1,0:T(8,128)(2,1)}), bf16[8,16,512]{2,1,0:T(8,128)(2,1)S(1)}, u32[]{:S(2)}, u32[]{:S(2)}) async-start(bf16[8,16,512]{2,1,0:T(8,128)(2,1)} %reduce_sum.41), calls=%async_computation.4 | async-start | bytes 262144 | tf_op jit(solution)/shard_map/all_to_all | solution.py:523
  (2 other events, 1.6 us)

commit v7 on v6

--- a/solution.py
+++ b/solution.py
@@ -123,31 +123,28 @@
 
 def pack_kernel(core, place, *refs):
     out = refs[-1]
-    *own, swapped = refs[:-1]
-    sources = [ref.at[core[0]] for ref in own] + [swapped.at[o] for o in range(swapped.shape[0])]
-    for o, ref in enumerate(sources):
+    for o, ref in enumerate(refs[:-1]):
 
         @pl.when(place[o] >= 0)
         def _():
             first = pl.multiple_of(place[o] * BLOCK_ROWS, 16)
-            out[pl.ds(first, BLOCK_ROWS), :] = ref[...]
-
-
-def pack(core, place, own, swapped, rows):
-    width = swapped.shape[2]
+            out[pl.ds(first, BLOCK_ROWS), :] = ref[core[0]]
+
+
+def pack(core, place, blocks, rows):
+    width = blocks[0].shape[2]
     shape = (2, BLOCK_ROWS, width)
     return pl.pallas_call(
         pack_kernel,
         grid_spec=pltpu.PrefetchScalarGridSpec(
             num_scalar_prefetch=2,
             grid=(1,),
-            in_specs=[pl.BlockSpec(shape, lambda k, *_: (0, 0, 0))] * len(own)
-            + [pl.BlockSpec(swapped.shape, lambda k, *_: (0, 0, 0))],
+            in_specs=[pl.BlockSpec(shape, lambda k, *_: (0, 0, 0))] * len(blocks),
             out_specs=pl.BlockSpec((rows, width), lambda k, *_: (0, 0)),
         ),
-        out_shape=jax.ShapeDtypeStruct((rows, width), swapped.dtype),
+        out_shape=jax.ShapeDtypeStruct((rows, width), blocks[0].dtype),
         name="pack_values",
-    )(core, place, *own, swapped)
+    )(core, place, *blocks)
 
 
 def pick_kernel(tile, column, source, out, held, came, gone):
@@ -312,7 +309,7 @@
         returning[take[p]] = value_total[place, :].astype(returning.dtype)
 
 
-def attention(take, arrived_q, arrived_k, packed_v, out_grad, doc_ids, first, count, key_at, done):
+def attention(take, arrived_q, arrived_k, packed_v, out_grad, docs, first, count, key_at, done):
     peers = arrived_q.shape[0]
     rows = out_grad.shape[0]
     wide = GROUP * HEAD_DIM
@@ -359,7 +356,7 @@
             transcendentals=rows * rows * GROUP * count,
         ),
         name="attention_backward",
-    )(take, arrived_q, arrived_k, packed_v, out_grad, doc_ids, doc_ids.reshape(rows, 1), *done)
+    )(take, arrived_q, arrived_k, packed_v, out_grad, *docs, *done)
 
 
 def weight_kernel(send, turned_ref, landed_ref, swapped_ref, out_ref, home):
@@ -489,11 +486,11 @@
     origin = jnp.concatenate([origin + core, origin + 1 - core])
     block = jnp.maximum(which(send, onward), 0)
     place = which(take, origin)
+    doc_column = doc_ids.reshape(rows, 1)
     leaving = value_blocks(core_of, block, normed, own, other)
     landed = along_z(leaving)
-    leave = [lax.dynamic_index_in_dim(a, 1 - core, 0, keepdims=False) for a in landed]
-    (swapped,) = swap([jnp.stack(leave)])
-    packed_v = pack(core_of, place, landed, swapped, rows)
+    landed += swap(landed)
+    packed_v = pack(core_of, place, landed, rows)
 
     column = 2 * jnp.arange(planes, dtype=jnp.int32)
     tile = depth // dp_count
@@ -505,11 +502,11 @@
 
     key_at = EARLY * GROUP
     done = attention(
-        take, arrived_one, arrived_one, packed_v, out_grad, doc_ids,
+        take, arrived_one, arrived_one, packed_v, out_grad, (doc_ids, doc_column),
         0, EARLY, key_at, (),
     )
     query_grad, key_grad, value_grad, returning = attention(
-        take, arrived_two, arrived_one, packed_v, out_grad, doc_ids,
+        take, arrived_two, arrived_one, packed_v, out_grad, (doc_ids, doc_column),
         EARLY, late, key_at, done,
     )
     landed = lax.all_to_all(returning, "dp", 0, 0, tiled=True)

time: 237 us -> 248 us (1.046)
  waiting for transfers between devices: 74.6 us -> 86.4 us
    all_to_all x1, waiting for transfers between devices: 10.2 us -> 34.7 us  [local(): arrived_one = lax.all_to_all(slots, 'dp', 0, 0, tiled=True)]
    ppermute x7, waiting for transfers between devices: 21.9 us -> 12.5 us  [along_z(): lax.ppermute(a, 'dp', ring((dp_count, planes), d, 2))]
    ppermute x5 -> x12, waiting for transfers between devices: 4.86 us -> 1.42 us  [swap(): return [lax.ppermute(a, 'dp', cores) for a in arrays]]
    all_to_all x1, starting transfers between devices: 7.6 us -> 4.58 us  [local(): arrived_two = lax.all_to_all(slots, 'dp', 0, 0, tiled=True)]
  transfers between devices with their start and end apart: 23 -> 30, of which waited for: 16 -> 14; matrix products, arithmetic and copies ran while one was open for 3% -> 3% of each run, Pallas kernels for 18% -> 17%
where the time goes in v7:
time: 248 us; the launch traced here: 246 us
  waiting for transfers between devices  86.4 us (35%)
  Pallas kernels  56 us (23%)
  starting transfers between devices  54 us (22%)
  blocking collectives  35.9 us (14%)
  local copies, waits for them, and re-layouts  7.69 us (3%)
  other arithmetic  4.62 us (2%)
    all_to_all x1, blocking collectives, local(): chips = lax.all_to_all(chip, 'fsdp', 0, 0, tiled=True)  35.9 us
    all_to_all x1, waiting for transfers between devices, local(): arrived_one = lax.all_to_all(slots, 'dp', 0, 0, tiled=True)  34.7 us
    ppermute x7, starting transfers between devices, along_z(): lax.ppermute(a, 'dp', ring((dp_count, planes), d, 2))  17.9 us
    pallas_call x2, Pallas kernels, attention(): pl.pallas_call(attention_kernel, grid_spec=pltpu.PrefetchScalarGridSpec(n...  17 us
    all_to_all x1, waiting for transfers between devices, local(): landed = lax.all_to_all(returning, 'dp', 0, 0, tiled=True)  16.6 us
    ppermute x4, waiting for transfers between devices, along_y(): return lax.ppermute(array, 'fsdp', ring((fsdp_count, side), step, 1))  14.3 us
    ppermute x7, waiting for transfers between devices, along_z(): lax.ppermute(a, 'dp', ring((dp_count, planes), d, 2))  12.5 us
    pallas_call x1, Pallas kernels, input_gradient(): pl.pallas_call(input_grad_kernel, grid_spec=pltpu.PrefetchScalarGridSpec(...  7.77 us
  transfers between devices with their start and end apart: 30, of which 14 were waited for; matrix products, arithmetic and copies ran while one was open for 3% of the time, Pallas kernels for 17%

profile of v7, /device:TPU:0, one launch (start us, length us, event | category | flops | bytes accessed | tf_op | source)
XLA Modules:
  0.0 245.8 jit_solution(16017282678151615999)
XLA Ops:
  0.6 3.1 %outgoing_slots.3 = bf16[16,48,2048]{2,1,0:T(8,128)(2,1)} custom-call(s32[8]{0:T(128)} %bitcast.36, bf16[384,2048]{1,0:T(8,128)(2,1)} %refs_0_.3, bf16[384,512]{1,0:T(8,128)(2,1)} %refs_1_.1), custom_call_target="tpu_custom_call" | custom-call | tf_op jit(solution)/shard_map/outgoing_slots/pallas_call | solution.py:53
  3.7 7.1 %all-to-all-start.1 = ((bf16[16,48,2048]{2,1,0:T(8,128)(2,1)}), bf16[16,48,2048]{2,1,0:T(8,128)(2,1)}, u32[]{:S(2)}, u32[]{:S(2)}) async-start(bf16[16,48,2048]{2,1,0:T(8,128)(2,1)} %outgoing_slots.3), calls=%async_computation.1 | async-start | bytes 6291456 | tf_op jit(solution)/shard_map/all_to_all | solution.py:472
  10.9 1.6 collective-permute-start
  12.5 1.7 collective-permute-start.1
  14.2 1.8 collective-permute-start.2
  16.1 1.9 collective-permute-done
  17.9 2.1 collective-permute-done.1
  20.0 1.7 collective-permute-done.2
  21.7 1.7 collective-permute-start.3
  23.4 1.7 collective-permute-start.4
  25.3 11.2 %collective-permute-done.3 = bf16[4,256,256]{2,1,0:T(8,128)(2,1)S(1)} collective-permute-done((bf16[4,256,256]{2,1,0:T(8,128)(2,1)S(1)}, bf16[4,256,256]{2,1,0:T(8,128)(2,1)S(1)}, u32[]{:S(2)}, u32[]{:S(2)}) %collective-permute-start.3) | collective-permute-done | bytes 524320 | tf_op jit(solution)/shard_map/ppermute | solution.py:463
  36.9 1.0 slice.9
  37.8 3.0 %collective-permute-start.6 = (bf16[2,256,256]{2,1,0:T(8,128)(2,1)S(1)}, bf16[2,256,256]{2,1,0:T(8,128)(2,1)S(1)}, u32[]{:S(2)}, u32[]{:S(2)}) collective-permute-start(bf16[2,256,256]{2,1,0:T(8,128)(2,1)S(1)} %slice.9), channel_id=1, source_target_pairs={{0,3},{1,0},{2,1},{3,2},{4,7},{5,4},{6,5},{7,6},{8,11},{9,8},{10,9... | collective-permute-start | bytes 786440 | tf_op jit(solution)/shard_map/ppermute | solution.py:463
  40.9 1.1 bitcast_dynamic-update-slice_fusion
  42.0 2.8 %collective-permute-done.5 = bf16[2,256,256]{2,1,0:T(8,128)(2,1)S(1)} collective-permute-done((bf16[2,256,256]{2,1,0:T(8,128)(2,1)S(1)}, bf16[2,256,256]{2,1,0:T(8,128)(2,1)S(1)}, u32[]{:S(2)}, u32[]{:S(2)}) %collective-permute-start.5) | collective-permute-done | bytes 262176 | tf_op jit(solution)/shard_map/ppermute | solution.py:463
  45.3 2.4 outgoing_slots.2
  48.0 34.7 %all-to-all-done.1.q_ref.k_ref = bf16[16,48,2048]{2,1,0:T(8,128)(2,1)} async-done(((bf16[16,48,2048]{2,1,0:T(8,128)(2,1)}), bf16[16,48,2048]{2,1,0:T(8,128)(2,1)}, u32[]{:S(2)}, u32[]{:S(2)}) %all-to-all-start.1) | async-done | bytes 3145760 | tf_op jit(solution)/shard_map/all_to_all | solution.py:472
  82.6 4.6 %all-to-all-start = ((bf16[16,48,512]{2,1,0:T(8,128)(2,1)}), bf16[16,48,512]{2,1,0:T(8,128)(2,1)S(1)}, u32[]{:S(2)}, u32[]{:S(2)}) async-start(bf16[16,48,512]{2,1,0:T(8,128)(2,1)} %outgoing_slots.2), calls=%async_computation | async-start | bytes 1572864 | tf_op jit(solution)/shard_map/all_to_all | solution.py:474
  87.9 6.7 %value_blocks.1 = (bf16[2,48,512]{2,1,0:T(8,128)(2,1)}, bf16[2,48,512]{2,1,0:T(8,128)(2,1)}, bf16[2,48,512]{2,1,0:T(8,128)(2,1)}, bf16[2,48,512]{2,1,0:T(8,128)(...) custom-call(s32[1]{0:T(128)} %bitcast.2.core, ...), custom_call_target="tpu_custom_call" | custom-call | flops 1610612736 | bytes 7340032 | tf_op jit(solution)/shard_map/value_blocks/pallas_call | solution.py:101
  94.7 5.9 %collective-permute-start.8 = (bf16[2,48,512]{2,1,0:T(8,128)(2,1)}, bf16[2,48,512]{2,1,0:T(8,128)(2,1)S(1)}, u32[]{:S(2)}, u32[]{:S(2)}) collective-permute-start(bf16[2,48,512]{2,1,0:T(8,128)(2,1)} %get-tuple-element.20), channel_id=1, source_target_pairs={{0,128},{16,144},{32,160},{48,176},{64,192},{80,208},{96,224},{112... | collective-permute-start | bytes 294920 | tf_op jit(solution)/shard_map/ppermute | solution.py:452
  101.1 4.5 %collective-permute-start.10 = (bf16[2,48,512]{2,1,0:T(8,128)(2,1)}, bf16[2,48,512]{2,1,0:T(8,128)(2,1)S(1)}, u32[]{:S(2)}, u32[]{:S(2)}) collective-permute-start(bf16[2,48,512]{2,1,0:T(8,128)(2,1)} %get-tuple-element.22), channel_id=1, source_target_pairs={{0,160},{16,176},{32,192},{48,208},{64,224},{80,240},{96,0},{112,1... | collective-permute-start | bytes 294920 | tf_op jit(solution)/shard_map/ppermute | solution.py:452
  106.1 3.6 %collective-permute-start.12 = (bf16[2,48,512]{2,1,0:T(8,128)(2,1)}, bf16[2,48,512]{2,1,0:T(8,128)(2,1)S(1)}, u32[]{:S(2)}, u32[]{:S(2)}) collective-permute-start(bf16[2,48,512]{2,1,0:T(8,128)(2,1)} %get-tuple-element.24), channel_id=1, source_target_pairs={{0,192},{16,208},{32,224},{48,240},{64,0},{80,16},{96,32},{112,48}... | collective-permute-start | bytes 294920 | tf_op jit(solution)/shard_map/ppermute | solution.py:452
  109.7 9.9 %collective-permute-done.8.refs_0_ = bf16[2,48,512]{2,1,0:T(8,128)(2,1)S(1)} collective-permute-done((bf16[2,48,512]{2,1,0:T(8,128)(2,1)}, bf16[2,48,512]{2,1,0:T(8,128)(2,1)S(1)}, u32[]{:S(2)}, u32[]{:S(2)}) %collective-permute-start.8) | collective-permute-done | bytes 98336 | tf_op jit(solution)/shard_map/ppermute | solution.py:452
  120.0 2.9 %collective-permute-start.14 = (bf16[2,48,512]{2,1,0:T(8,128)(2,1)}, bf16[2,48,512]{2,1,0:T(8,128)(2,1)S(1)}, u32[]{:S(2)}, u32[]{:S(2)}) collective-permute-start(bf16[2,48,512]{2,1,0:T(8,128)(2,1)} %get-tuple-element.26), channel_id=1, source_target_pairs={{0,224},{16,240},{32,0},{48,16},{64,32},{80,48},{96,64},{112,80},{... | collective-permute-start | bytes 294920 | tf_op jit(solution)/shard_map/ppermute | solution.py:452
  122.9 1.4 collective-permute-done.11.refs_3_
  124.8 0.9 collective-permute-done.13.refs_5_
  127.3 0.8 copy.32.doc_col
  128.9 0.6 copy-done.19
  129.6 3.0 %pack_values.1.v_ref = bf16[384,512]{1,0:T(8,128)(2,1)} custom-call(s32[1]{0:T(128)} %bitcast.2.core, s32[16]{0:T(128)} %broadcast_add_fusion.place, bf16[2,48,512]{2,1,0:T(8,128)(2,1)} %copy-done.5, bf16[2,48,512]{2,1,0:T(8,128)(2,1)} %copy-done.6, bf16[2,48,512]{2,1,0:T(8,128)(2,1)} %copy-done.7, bf16[2,48,512]{2,1,0:T(8,128)(2,1)} %copy-done.8, ...), custom_call_target="tpu_custom_call" | custom-call | tf_op jit(solution)/shard_map/pack_values/pallas_call | solution.py:137
  132.6 11.4 %attention_backward.2 = (bf16[384,2048]{1,0:T(8,128)(2,1)}, bf16[384,512]{1,0:T(8,128)(2,1)}, bf16[384,512]{1,0:T(8,128)(2,1)}, bf16[16,48,512]{2,1,0:T(8,128)(2,1)}) custom-call(s32[8]{0:T(128)} %bitcast.40, bf16[16,48,2048]{2,1,0:T(8,128)(2,1)} %all-to-all-done.1.q_ref.k_ref, bf16[16,48,2048]{2,1,0:T(8,128)(2,1)} %all-to-all-done.1.q_ref.k_ref, ...), custom_call_target="tpu_custom_call" | custom-call | flops 2717908992 | bytes 5898240 | tf_op jit(solution)/shard_map/attention_backward/pallas_call | solution.py:318
  144.0 0.9 copy-done.1
  144.8 5.6 %attention_backward.3 = (bf16[384,2048]{1,0:T(8,128)(2,1)}, bf16[384,512]{1,0:T(8,128)(2,1)}, bf16[384,512]{1,0:T(8,128)(2,1)}, bf16[16,48,512]{2,1,0:T(8,128)(2,1)}) custom-call(s32[8]{0:T(128)} %bitcast.41, bf16[16,48,512]{2,1,0:T(8,128)(2,1)} %copy-done.1, ...), custom_call_target="tpu_custom_call", output_to_operand_aliasing={{0}: (7, {}), {1}: (8, {}), {2}: (9, {}), {3}: (10, {})} | custom-call | flops 905969664 | bytes 1966080 | tf_op jit(solution)/shard_map/attention_backward/pallas_call | solution.py:318
  150.5 4.5 %all-to-all-start.2 = ((bf16[16,48,512]{2,1,0:T(8,128)(2,1)}), bf16[16,48,512]{2,1,0:T(8,128)(2,1)S(1)}, u32[]{:S(2)}, u32[]{:S(2)}) async-start(bf16[16,48,512]{2,1,0:T(8,128)(2,1)} %get-tuple-element.35), calls=%async_computation.2 | async-start | bytes 1572864 | tf_op jit(solution)/shard_map/all_to_all | solution.py:512
  155.5 3.0 %pick_columns.1 = bf16[384,2048]{1,0:T(8,128)(2,1)} custom-call(s32[8]{0:T(128)} %add_subtract_fusion.column, bf16[384,4096]{1,0:T(8,128)(2,1)} %own_ref.1), custom_call_target="tpu_custom_call" | custom-call | tf_op jit(solution)/shard_map/pick_columns/pallas_call | solution.py:173
  159.0 16.6 %all-to-all-done.2.landed_ref = bf16[16,48,512]{2,1,0:T(8,128)(2,1)S(1)} async-done(((bf16[16,48,512]{2,1,0:T(8,128)(2,1)}), bf16[16,48,512]{2,1,0:T(8,128)(2,1)S(1)}, u32[]{:S(2)}, u32[]{:S(2)}) %all-to-all-start.2) | async-done | bytes 786464 | tf_op jit(solution)/shard_map/all_to_all | solution.py:512
  175.6 2.5 %collective-permute-start.25 = (bf16[16,48,512]{2,1,0:T(8,128)(2,1)S(1)}, bf16[16,48,512]{2,1,0:T(8,128)(2,1)S(1)}, u32[]{:S(2)}, u32[]{:S(2)}) collective-permute-start(bf16[16,48,512]{2,1,0:T(8,128)(2,1)S(1)} %all-to-all-done.2.landed_ref), channel_id=1, source_target_pairs={{0,16},{16,0},{32,48},{48,32},{64,80},{80,64},{96,112},{112,96},{1... | collective-permute-start | bytes 2359304 | tf_op jit(solution)/shard_map/ppermute | solution.py:457
  178.7 1.4 collective-permute-done.23
  180.0 0.6 pad_add_fusion.send
  180.6 1.2 copy-done.3
  181.8 7.4 %turn_columns.1.turned_ref = bf16[2048,768]{1,0:T(8,128)(2,1)} custom-call(s32[8]{0:T(128)} %fusion.4.column, bf16[384,4096]{1,0:T(8,128)(2,1)} %own_ref.1, bf16[384,2048]{1,0:T(8,128)(2,1)} %copy-done.3), custom_call_target="tpu_custom_call" | custom-call | tf_op jit(solution)/shard_map/turn_columns/pallas_call | solution.py:200
  189.2 0.9 copy-done.4
  190.2 5.6 %weight_part.1 = bf16[16,8,16,512]{3,2,1,0:T(8,128)(2,1)} custom-call(s32[2,8]{1,0:T(2,128)} %pad_add_fusion.send, bf16[2048,768]{1,0:T(8,128)(2,1)} %turn_columns.1.turned_ref, bf16[16,48,512]{2,1,0:T(8,128)(2,1)} %copy-done.2, bf16[16,48,512]{2,1,0:T(8,128)(2,1)} %copy-done.4), custom_call_target="tpu_custom_call" | custom-call | tf_op jit(solution)/shard_map/weight_part/pallas_call | solution.py:387
  195.8 35.9 %all_to_all.25 = bf16[16,8,16,512]{3,2,1,0:T(8,128)(2,1)S(1)} all-to-all(bf16[16,8,16,512]{3,2,1,0:T(8,128)(2,1)} %weight_part.1), channel_id=1, replica_groups=mesh['dp'=16,'fsdp'=16] {'fsdp'}, dimensions={0} | all-to-all | bytes 4194304 | tf_op jit(solution)/shard_map/all_to_all | solution.py:517
  231.7 1.1 reduce_sum.41
  232.8 3.4 %all-to-all-start.4 = ((bf16[8,16,512]{2,1,0:T(8,128)(2,1)}), bf16[8,16,512]{2,1,0:T(8,128)(2,1)S(1)}, u32[]{:S(2)}, u32[]{:S(2)}) async-start(bf16[8,16,512]{2,1,0:T(8,128)(2,1)} %reduce_sum.41), calls=%async_computation.4 | async-start | bytes 262144 | tf_op jit(solution)/shard_map/all_to_all | solution.py:520
  236.2 7.8 %input_gradient.1 = bf16[384,4096]{1,0:T(8,128)(2,1)} custom-call(s32[1]{0:T(128)} %bitcast.2.core, bf16[384,512]{1,0:T(8,128)(2,1)} %get-tuple-element.34.grad_ref, bf16[4096,256]{1,0:T(8,128)(2,1)} %bitcast.35, bf16[4096,256]{1,0:T(8,128)(2,1)} %collective-permute-done.7.other_ref), custom_call_target="tpu_custom_call" | custom-call | flops 1610612736 | bytes 7340032 | tf_op jit(solution)/shard_map/input_gradient/pallas_call | solution.py:228
  243.9 1.2 all-to-all-done.4
  245.2 0.6 broadcast_multiply_fusion
  (105 shorter events, 7.9 us)
Async XLA Ops:
  3.7 7.2 %copy-start.20 = (bf16[256,512]{1,0:T(8,128)(2,1)S(1)}, bf16[256,512]{1,0:T(8,128)(2,1)}, u32[]{:S(2)}) copy-start(bf16[256,512]{1,0:T(8,128)(2,1)} %param.13) | copy-start | bytes 786436
  3.7 78.9 %all-to-all-start.1 = ((bf16[16,48,2048]{2,1,0:T(8,128)(2,1)}), bf16[16,48,2048]{2,1,0:T(8,128)(2,1)}, u32[]{:S(2)}, u32[]{:S(2)}) async-start(bf16[16,48,2048]{2,1,0:T(8,128)(2,1)} %outgoing_slots.3), calls=%async_computation.1 | async-start | bytes 6291456 | tf_op jit(solution)/shard_map/all_to_all | solution.py:472
  10.9 7.0 %collective-permute-start = (bf16[256,256]{1,0:T(8,128)(2,1)S(1)}, bf16[256,256]{1,0:T(8,128)(2,1)S(1)}, u32[]{:S(2)}, u32[]{:S(2)}) collective-permute-start(bf16[256,256]{1,0:T(8,128)(2,1)S(1)} %get-tuple-element.39), channel_id=1, source_target_pairs={{0,4},{1,5},{2,6},{3,7},{4,8},{5,9},{6,10},{7,11},{8,12},{9,13},{1... | collective-permute-start | bytes 393224 | tf_op jit(solution)/shard_map/ppermute | solution.py:460
  12.5 7.5 %collective-permute-start.1 = (bf16[256,256]{1,0:T(8,128)(2,1)S(1)}, bf16[256,256]{1,0:T(8,128)(2,1)S(1)}, u32[]{:S(2)}, u32[]{:S(2)}) collective-permute-start(bf16[256,256]{1,0:T(8,128)(2,1)S(1)} %get-tuple-element.39), channel_id=1, source_target_pairs={{0,12},{1,13},{2,14},{3,15},{4,0},{5,1},{6,2},{7,3},{8,4},{9,5},{1... | collective-permute-start | bytes 393224 | tf_op jit(solution)/shard_map/ppermute | solution.py:460
  14.2 7.5 %collective-permute-start.2 = (bf16[256,256]{1,0:T(8,128)(2,1)S(1)}, bf16[256,256]{1,0:T(8,128)(2,1)S(1)}, u32[]{:S(2)}, u32[]{:S(2)}) collective-permute-start(bf16[256,256]{1,0:T(8,128)(2,1)S(1)} %get-tuple-element.39), channel_id=1, source_target_pairs={{0,8},{1,9},{2,10},{3,11},{4,12},{5,13},{6,14},{7,15},{8,0},{9,1},... | collective-permute-start | bytes 393224 | tf_op jit(solution)/shard_map/ppermute | solution.py:460
  21.7 14.7 %collective-permute-start.3 = (bf16[4,256,256]{2,1,0:T(8,128)(2,1)S(1)}, bf16[4,256,256]{2,1,0:T(8,128)(2,1)S(1)}, u32[]{:S(2)}, u32[]{:S(2)}) collective-permute-start(bf16[4,256,256]{2,1,0:T(8,128)(2,1)S(1)} %bitcast_dynamic-update-slice_fusion.5), channel_id=1, source_target_pairs={{0,1},{1,2},{2,3},{3,0},{4,5},{5,6},{6,7},{7,4},{8,9},{9,10},{10,1... | collective-permute-start | bytes 1572872 | tf_op jit(solution)/shard_map/ppermute | solution.py:463
  23.4 13.5 %collective-permute-start.4 = (bf16[4,256,256]{2,1,0:T(8,128)(2,1)S(1)}, bf16[4,256,256]{2,1,0:T(8,128)(2,1)}, u32[]{:S(2)}, u32[]{:S(2)}) collective-permute-start(bf16[4,256,256]{2,1,0:T(8,128)(2,1)S(1)} %bitcast_dynamic-update-slice_fusion.5), channel_id=1, source_target_pairs={{0,3},{1,0},{2,1},{3,2},{4,7},{5,4},{6,5},{7,6},{8,11},{9,8},{10,9... | collective-permute-start | bytes 1572872 | tf_op jit(solution)/shard_map/ppermute | solution.py:463
  36.5 8.4 %collective-permute-start.5 = (bf16[2,256,256]{2,1,0:T(8,128)(2,1)S(1)}, bf16[2,256,256]{2,1,0:T(8,128)(2,1)S(1)}, u32[]{:S(2)}, u32[]{:S(2)}) collective-permute-start(bf16[2,256,256]{2,1,0:T(8,128)(2,1)S(1)} %slice.8), channel_id=1, source_target_pairs={{0,1},{1,2},{2,3},{3,0},{4,5},{5,6},{6,7},{7,4},{8,9},{9,10},{10,1... | collective-permute-start | bytes 786440 | tf_op jit(solution)/shard_map/ppermute | solution.py:463
  37.8 7.3 %collective-permute-start.6 = (bf16[2,256,256]{2,1,0:T(8,128)(2,1)S(1)}, bf16[2,256,256]{2,1,0:T(8,128)(2,1)S(1)}, u32[]{:S(2)}, u32[]{:S(2)}) collective-permute-start(bf16[2,256,256]{2,1,0:T(8,128)(2,1)S(1)} %slice.9), channel_id=1, source_target_pairs={{0,3},{1,0},{2,1},{3,2},{4,7},{5,4},{6,5},{7,6},{8,11},{9,8},{10,9... | collective-permute-start | bytes 786440 | tf_op jit(solution)/shard_map/ppermute | solution.py:463
  40.9 6.9 %copy-start.25 = (s32[8]{0:T(128)S(1)}, s32[8]{0:T(128)}, u32[]{:S(2)}) copy-start(s32[8]{0:T(128)} %constant.137.clone) | copy-start | bytes 100
  40.9 7.0 %copy-start.24 = (s32[8]{0:T(128)S(1)}, s32[8]{0:T(128)}, u32[]{:S(2)}) copy-start(s32[8]{0:T(128)} %constant.145) | copy-start | bytes 100
  45.2 42.7 %copy-start = (bf16[4,4,256,256]{3,2,0,1:T(8,128)(2,1)}, bf16[4,4,256,256]{3,2,0,1:T(8,128)(2,1)S(1)}, u32[]{:S(2)}) copy-start(bf16[4,4,256,256]{3,2,0,1:T(8,128)(2,1)S(1)} %bitcast_dynamic-update-slice_fusion.4) | copy-start | bytes 6291460
  45.2 42.1 %copy-start.21 = (s32[1,8]{1,0:T(1,128)S(1)}, s32[1,8]{1,0:T(1,128)}, u32[]{:S(2)}) copy-start(s32[1,8]{1,0:T(1,128)} %param.15) | copy-start | bytes 100
  45.2 42.1 %copy-start.23 = (s32[1,8]{1,0:T(1,128)S(1)}, s32[1,8]{1,0:T(1,128)}, u32[]{:S(2)}) copy-start(s32[1,8]{1,0:T(1,128)} %param.16) | copy-start | bytes 100
  45.2 42.7 %collective-permute-start.7 = (bf16[4096,256]{1,0:T(8,128)(2,1)S(1)}, bf16[4096,256]{1,0:T(8,128)(2,1)}, u32[]{:S(2)}, u32[]{:S(2)}) collective-permute-start(bf16[4096,256]{1,0:T(8,128)(2,1)S(1)} %bitcast.33), channel_id=1, source_target_pairs={{0,16},{16,0},{32,48},{48,32},{64,80},{80,64},{96,112},{112,96},{1... | collective-permute-start | bytes 6291464 | tf_op jit(solution)/shard_map/ppermute | solution.py:457
  82.6 61.3 %all-to-all-start = ((bf16[16,48,512]{2,1,0:T(8,128)(2,1)}), bf16[16,48,512]{2,1,0:T(8,128)(2,1)S(1)}, u32[]{:S(2)}, u32[]{:S(2)}) async-start(bf16[16,48,512]{2,1,0:T(8,128)(2,1)} %outgoing_slots.2), calls=%async_computation | async-start | bytes 1572864 | tf_op jit(solution)/shard_map/all_to_all | solution.py:474
  87.9 39.4 %copy-start.22 = (s32[1,384]{1,0:T(1,128)S(1)}, s32[1,384]{1,0:T(1,128)}, u32[]{:S(2)}) copy-start(s32[1,384]{1,0:T(1,128)} %doc_row.3) | copy-start | bytes 4612
  94.7 25.0 %collective-permute-start.8 = (bf16[2,48,512]{2,1,0:T(8,128)(2,1)}, bf16[2,48,512]{2,1,0:T(8,128)(2,1)S(1)}, u32[]{:S(2)}, u32[]{:S(2)}) collective-permute-start(bf16[2,48,512]{2,1,0:T(8,128)(2,1)} %get-tuple-element.20), channel_id=1, source_target_pairs={{0,128},{16,144},{32,160},{48,176},{64,192},{80,208},{96,224},{112... | collective-permute-start | bytes 294920 | tf_op jit(solution)/shard_map/ppermute | solution.py:452
  100.5 19.4 %collective-permute-start.9 = (bf16[2,48,512]{2,1,0:T(8,128)(2,1)}, bf16[2,48,512]{2,1,0:T(8,128)(2,1)S(1)}, u32[]{:S(2)}, u32[]{:S(2)}) collective-permute-start(bf16[2,48,512]{2,1,0:T(8,128)(2,1)} %get-tuple-element.21), channel_id=1, source_target_pairs={{0,96},{16,112},{32,128},{48,144},{64,160},{80,176},{96,192},{112,... | collective-permute-start | bytes 294920 | tf_op jit(solution)/shard_map/ppermute | solution.py:452
  101.1 21.8 %collective-permute-start.10 = (bf16[2,48,512]{2,1,0:T(8,128)(2,1)}, bf16[2,48,512]{2,1,0:T(8,128)(2,1)S(1)}, u32[]{:S(2)}, u32[]{:S(2)}) collective-permute-start(bf16[2,48,512]{2,1,0:T(8,128)(2,1)} %get-tuple-element.22), channel_id=1, source_target_pairs={{0,160},{16,176},{32,192},{48,208},{64,224},{80,240},{96,0},{112,1... | collective-permute-start | bytes 294920 | tf_op jit(solution)/shard_map/ppermute | solution.py:452
  105.6 18.7 %collective-permute-start.11 = (bf16[2,48,512]{2,1,0:T(8,128)(2,1)}, bf16[2,48,512]{2,1,0:T(8,128)(2,1)S(1)}, u32[]{:S(2)}, u32[]{:S(2)}) collective-permute-start(bf16[2,48,512]{2,1,0:T(8,128)(2,1)} %get-tuple-element.23), channel_id=1, source_target_pairs={{0,64},{16,80},{32,96},{48,112},{64,128},{80,144},{96,160},{112,17... | collective-permute-start | bytes 294920 | tf_op jit(solution)/shard_map/ppermute | solution.py:452
  106.1 18.2 %collective-permute-start.12 = (bf16[2,48,512]{2,1,0:T(8,128)(2,1)}, bf16[2,48,512]{2,1,0:T(8,128)(2,1)S(1)}, u32[]{:S(2)}, u32[]{:S(2)}) collective-permute-start(bf16[2,48,512]{2,1,0:T(8,128)(2,1)} %get-tuple-element.24), channel_id=1, source_target_pairs={{0,192},{16,208},{32,224},{48,240},{64,0},{80,16},{96,32},{112,48}... | collective-permute-start | bytes 294920 | tf_op jit(solution)/shard_map/ppermute | solution.py:452
  119.6 8.6 %copy-start.5 = (bf16[2,48,512]{2,1,0:T(8,128)(2,1)}, bf16[2,48,512]{2,1,0:T(8,128)(2,1)S(1)}, u32[]{:S(2)}) copy-start(bf16[2,48,512]{2,1,0:T(8,128)(2,1)S(1)} %collective-permute-done.8.refs_0_) | copy-start | bytes 294916
  119.6 6.0 %collective-permute-start.13 = (bf16[2,48,512]{2,1,0:T(8,128)(2,1)}, bf16[2,48,512]{2,1,0:T(8,128)(2,1)S(1)}, u32[]{:S(2)}, u32[]{:S(2)}) collective-permute-start(bf16[2,48,512]{2,1,0:T(8,128)(2,1)} %get-tuple-element.25), channel_id=1, source_target_pairs={{0,32},{16,48},{32,64},{48,80},{64,96},{80,112},{96,128},{112,144}... | collective-permute-start | bytes 294920 | tf_op jit(solution)/shard_map/ppermute | solution.py:452
  120.0 8.3 %copy-start.6 = (bf16[2,48,512]{2,1,0:T(8,128)(2,1)}, bf16[2,48,512]{2,1,0:T(8,128)(2,1)S(1)}, u32[]{:S(2)}) copy-start(bf16[2,48,512]{2,1,0:T(8,128)(2,1)S(1)} %collective-permute-done.9.refs_1_) | copy-start | bytes 294916
  120.0 5.7 %collective-permute-start.14 = (bf16[2,48,512]{2,1,0:T(8,128)(2,1)}, bf16[2,48,512]{2,1,0:T(8,128)(2,1)S(1)}, u32[]{:S(2)}, u32[]{:S(2)}) collective-permute-start(bf16[2,48,512]{2,1,0:T(8,128)(2,1)} %get-tuple-element.26), channel_id=1, source_target_pairs={{0,224},{16,240},{32,0},{48,16},{64,32},{80,48},{96,64},{112,80},{... | collective-permute-start | bytes 294920 | tf_op jit(solution)/shard_map/ppermute | solution.py:452
  122.9 5.4 %copy-start.7 = (bf16[2,48,512]{2,1,0:T(8,128)(2,1)}, bf16[2,48,512]{2,1,0:T(8,128)(2,1)S(1)}, u32[]{:S(2)}) copy-start(bf16[2,48,512]{2,1,0:T(8,128)(2,1)S(1)} %collective-permute-done.10.refs_2_) | copy-start | bytes 294916
  122.9 3.3 %collective-permute-start.22 = (bf16[2,48,512]{2,1,0:T(8,128)(2,1)}, bf16[2,48,512]{2,1,0:T(8,128)(2,1)S(1)}, u32[]{:S(2)}, u32[]{:S(2)}) collective-permute-start(bf16[2,48,512]{2,1,0:T(8,128)(2,1)} %get-tuple-element.27.refs_7_), channel_id=1, source_target_pairs={{0,16},{16,0},{32,48},{48,32},{64,80},{80,64},{96,112},{112,96},{1... | collective-permute-start | bytes 294920 | tf_op jit(solution)/shard_map/ppermute | solution.py:457
  124.3 4.0 %copy-start.8 = (bf16[2,48,512]{2,1,0:T(8,128)(2,1)}, bf16[2,48,512]{2,1,0:T(8,128)(2,1)S(1)}, u32[]{:S(2)}) copy-start(bf16[2,48,512]{2,1,0:T(8,128)(2,1)S(1)} %collective-permute-done.11.refs_3_) | copy-start | bytes 294916
  124.3 2.0 collective-permute-start.15
  124.3 4.0 %copy-start.9 = (bf16[2,48,512]{2,1,0:T(8,128)(2,1)}, bf16[2,48,512]{2,1,0:T(8,128)(2,1)S(1)}, u32[]{:S(2)}) copy-start(bf16[2,48,512]{2,1,0:T(8,128)(2,1)S(1)} %collective-permute-done.12.refs_4_) | copy-start | bytes 294916
  124.3 2.4 collective-permute-start.16
  125.7 2.6 %copy-start.10 = (bf16[2,48,512]{2,1,0:T(8,128)(2,1)}, bf16[2,48,512]{2,1,0:T(8,128)(2,1)S(1)}, u32[]{:S(2)}) copy-start(bf16[2,48,512]{2,1,0:T(8,128)(2,1)S(1)} %collective-permute-done.13.refs_5_) | copy-start | bytes 294916
  125.7 2.5 %collective-permute-start.17 = (bf16[2,48,512]{2,1,0:T(8,128)(2,1)S(1)}, bf16[2,48,512]{2,1,0:T(8,128)(2,1)S(1)}, u32[]{:S(2)}, u32[]{:S(2)}) collective-permute-start(bf16[2,48,512]{2,1,0:T(8,128)(2,1)S(1)} %collective-permute-done.10.refs_2_), channel_id=1, source_target_pairs={{0,16},{16,0},{32,48},{48,32},{64,80},{80,64},{96,112},{112,96},{1... | collective-permute-start | bytes 294920 | tf_op jit(solution)/shard_map/ppermute | solution.py:457
  125.7 2.6 %copy-start.11 = (bf16[2,48,512]{2,1,0:T(8,128)(2,1)}, bf16[2,48,512]{2,1,0:T(8,128)(2,1)S(1)}, u32[]{:S(2)}) copy-start(bf16[2,48,512]{2,1,0:T(8,128)(2,1)S(1)} %collective-permute-done.14.refs_6_) | copy-start | bytes 294916
  125.7 2.5 %collective-permute-start.18 = (bf16[2,48,512]{2,1,0:T(8,128)(2,1)S(1)}, bf16[2,48,512]{2,1,0:T(8,128)(2,1)S(1)}, u32[]{:S(2)}, u32[]{:S(2)}) collective-permute-start(bf16[2,48,512]{2,1,0:T(8,128)(2,1)S(1)} %collective-permute-done.11.refs_3_), channel_id=1, source_target_pairs={{0,16},{16,0},{32,48},{48,32},{64,80},{80,64},{96,112},{112,96},{1... | collective-permute-start | bytes 294920 | tf_op jit(solution)/shard_map/ppermute | solution.py:457
  126.2 2.1 copy-start.12
  126.2 2.0 collective-permute-start.19
  126.3 2.0 copy-start.13
  126.3 1.9 collective-permute-start.20
  126.7 1.6 copy-start.14
  126.7 1.5 collective-permute-start.21
  150.5 25.1 %all-to-all-start.2 = ((bf16[16,48,512]{2,1,0:T(8,128)(2,1)}), bf16[16,48,512]{2,1,0:T(8,128)(2,1)S(1)}, u32[]{:S(2)}, u32[]{:S(2)}) async-start(bf16[16,48,512]{2,1,0:T(8,128)(2,1)} %get-tuple-element.35), calls=%async_computation.2 | async-start | bytes 1572864 | tf_op jit(solution)/shard_map/all_to_all | solution.py:512
  158.5 22.1 %collective-permute-start.24 = (bf16[384,2048]{1,0:T(8,128)(2,1)}, bf16[384,2048]{1,0:T(8,128)(2,1)S(1)}, u32[]{:S(2)}, u32[]{:S(2)}) collective-permute-start(bf16[384,2048]{1,0:T(8,128)(2,1)} %pick_columns.1), channel_id=1, source_target_pairs={{0,16},{16,0},{32,48},{48,32},{64,80},{80,64},{96,112},{112,96},{1... | collective-permute-start | bytes 4718600 | tf_op jit(solution)/shard_map/ppermute | solution.py:457
  175.6 13.6 %copy-start.2 = (bf16[16,48,512]{2,1,0:T(8,128)(2,1)}, bf16[16,48,512]{2,1,0:T(8,128)(2,1)S(1)}, u32[]{:S(2)}) copy-start(bf16[16,48,512]{2,1,0:T(8,128)(2,1)S(1)} %all-to-all-done.2.landed_ref) | copy-start | bytes 2359300
  175.6 13.6 %collective-permute-start.25 = (bf16[16,48,512]{2,1,0:T(8,128)(2,1)S(1)}, bf16[16,48,512]{2,1,0:T(8,128)(2,1)S(1)}, u32[]{:S(2)}, u32[]{:S(2)}) collective-permute-start(bf16[16,48,512]{2,1,0:T(8,128)(2,1)S(1)} %all-to-all-done.2.landed_ref), channel_id=1, source_target_pairs={{0,16},{16,0},{32,48},{48,32},{64,80},{80,64},{96,112},{112,96},{1... | collective-permute-start | bytes 2359304 | tf_op jit(solution)/shard_map/ppermute | solution.py:457
  178.1 1.9 collective-permute-start.23
  232.8 12.4 %all-to-all-start.4 = ((bf16[8,16,512]{2,1,0:T(8,128)(2,1)}), bf16[8,16,512]{2,1,0:T(8,128)(2,1)S(1)}, u32[]{:S(2)}, u32[]{:S(2)}) async-start(bf16[8,16,512]{2,1,0:T(8,128)(2,1)} %reduce_sum.41), calls=%async_computation.4 | async-start | bytes 262144 | tf_op jit(solution)/shard_map/all_to_all | solution.py:520
  (8 other events, 6.3 us)
